TPU v7x, 32 devices: a whole 2x2x4 slice. The times are simulated.
32 devices in a mesh: dom: 2 (over y), frame: 4 (over z), query: 2 (over x), split: 2 (over core).
Axes of the slice: x: 2, y: 2, z: 4, core: 2. Of those that a mesh axis runs over, the one named last changes fastest.
Arguments:
- frames: bfloat16 [16, 1024, 256], P(('dom', 'frame')), parts along dimension 0, may hold values from -64 to 64
- query_frame: int32 [2048], P(('dom', 'query')), parts along dimension 0, may hold values from 0 to 7, as said below
- query_pixel: int32 [2, 2048], P(None, ('dom', 'query')), parts along dimension 1, may hold values from 0 to 31
- in_weight: bfloat16 [512, 512], replicated, may hold values from -0.25 to 0.25
- conv_weight: float32 [1, 3, 512], replicated, may hold values from -3 to 3
- up_weight: bfloat16 [1, 512, 2048], P(None, None, 'split'), may hold values from -0.25 to 0.25
- down_weight: bfloat16 [1, 2048, 512], P(None, 'split'), may hold values from -0.125 to 0.125
Outputs:
- tokens: bfloat16 [2048, 8, 512], P(('dom', 'query'), 'frame'), parts along dimension 0
There are 2 independent parts, one for each index of `dom`. A program takes and returns all parts, laid end to end along the dimension named above; an argument that names none is the same for every part. Nothing has to cross between parts.
Inputs may be any that keep to these rules, and one draw needn't show every extreme that they name: `query_frame`: within each aligned group of 512 query points (one index of query), at most 384 start frames lie among any aligned 2 frames (one index of frame), and in every group some such frames hold exactly 384.
All inputs are finite; a program needn't handle non-finite values.
Results may differ from a plain program's by a relative error of at most 0.006.
Values may be sent and summed in bfloat16 or wider, within the bound.
No kernel may reach another device: no remote copies, remote signals or barrier semaphores. Data moves between devices by JAX's collectives and lax.ppermute only.
A program may use at most 64 MiB of HBM per device.

v0:
```python
import math

import jax
import jax.numpy as jnp
from jax import lax
from jax.sharding import PartitionSpec as P

SIDE = 32


def with_halo(cells, sides, width):
    for axis, dim in sides:
        count = lax.axis_size(axis)
        ends = count - 1
        head = lax.slice_in_dim(cells, 0, width, axis=dim)
        tail = lax.slice_in_dim(cells, cells.shape[dim] - width, cells.shape[dim], axis=dim)
        cells = jnp.concatenate(
            [
                lax.ppermute(tail, axis, [(i, (i + 1) % count) for i in range(ends)]),
                cells,
                lax.ppermute(head, axis, [((i + 1) % count, i) for i in range(ends)]),
            ],
            axis=dim,
        )
    return cells


def rms_scale(values, epsilon):
    return values / jnp.sqrt(jnp.mean(values * values, axis=-1, keepdims=True) + epsilon)


def on_device(frames, query_frame, query_pixel, in_weight, conv_weight, up_weight, down_weight):
    frame_count, pixel_count, channels = frames.shape
    query_count = query_frame.shape[0]
    width = in_weight.shape[1]
    first_frame = lax.axis_index("frame") * frame_count
    flat_frames = frames.reshape(frame_count * pixel_count, channels)
    pixel_index = query_pixel[0] * SIDE + query_pixel[1]
    local_frame = query_frame - first_frame
    is_owned = (local_frame >= 0) & (local_frame < frame_count)
    column = jnp.where(is_owned, local_frame * pixel_count + pixel_index, -1)
    picker = (
        column[:, None] == jnp.arange(frame_count * pixel_count, dtype=jnp.int32)[None, :]
    ).astype(jnp.bfloat16)
    own_features = jnp.dot(picker, flat_frames, preferred_element_type=jnp.float32)
    devices = lax.axis_size("frame")
    capacity = max(2, 3 * query_count // devices)
    owner = query_frame // frame_count
    order = jnp.arange(query_count, dtype=jnp.int32)
    earlier = (owner[:, None] == owner[None, :]) & (order[None, :] < order[:, None])
    ranking = jnp.sum(earlier.astype(jnp.int32), axis=1)
    slot_pick = (
        (ranking[None, :] == jnp.arange(capacity, dtype=jnp.int32)[:, None]) & is_owned[None, :]
    ).astype(jnp.bfloat16)
    packed = jnp.dot(
        slot_pick, own_features.astype(jnp.bfloat16), preferred_element_type=jnp.float32
    ).astype(jnp.bfloat16)
    every_slot = lax.all_gather(packed, "frame", axis=0, tiled=True)
    source = owner * capacity + ranking
    unpick = (source[:, None] == jnp.arange(devices * capacity, dtype=jnp.int32)[None, :]).astype(
        jnp.bfloat16
    )
    query_features = jnp.dot(unpick, every_slot, preferred_element_type=jnp.float32).astype(
        jnp.bfloat16
    )
    scores = jnp.einsum(
        "qc,tpc->qtp", query_features, frames, preferred_element_type=jnp.float32
    ) * (1.0 / math.sqrt(channels))
    peak = jnp.max(scores, axis=-1, keepdims=True)
    expd = jnp.exp(scores - peak)
    weights = (expd / jnp.sum(expd, axis=-1, keepdims=True)).astype(jnp.bfloat16)
    pooled = jnp.einsum("qtp,tpc->qtc", weights, frames, preferred_element_type=jnp.float32)
    normed = rms_scale(pooled, 1e-06).astype(jnp.bfloat16)
    joined = jnp.concatenate(
        [normed, jnp.broadcast_to(query_features[:, None, :], normed.shape)], axis=-1
    )
    stream = jnp.einsum("qtc,cd->qtd", joined, in_weight, preferred_element_type=jnp.float32)
    rows_total = query_count * frame_count
    level = rms_scale(stream, 1e-05).astype(jnp.bfloat16)
    padded = with_halo(level, (("frame", 1),), 1).astype(jnp.float32)
    taps = conv_weight[0]
    mixed_time = taps[0] * padded[:, :-2] + taps[1] * padded[:, 1:-1] + taps[2] * padded[:, 2:]
    stream = stream + mixed_time
    gated = rms_scale(stream, 1e-05).astype(jnp.bfloat16).reshape(rows_total, width)
    hidden = jax.nn.gelu(jnp.dot(gated, up_weight[0], preferred_element_type=jnp.float32)).astype(
        jnp.bfloat16
    )
    partial_delta = jnp.dot(hidden, down_weight[0], preferred_element_type=jnp.float32)
    summed = lax.psum(partial_delta.astype(jnp.bfloat16), "split").astype(jnp.float32)
    stream = stream + summed.reshape(query_count, frame_count, width)
    return stream.astype(jnp.bfloat16)


def solution(mesh):
    return jax.shard_map(
        on_device,
        mesh=mesh,
        in_specs=(
            P(("dom", "frame"), None, None),
            P(("dom", "query")),
            P(None, ("dom", "query")),
            P(),
            P(),
            P(None, None, "split"),
            P(None, "split", None),
        ),
        out_specs=P(("dom", "query"), "frame", None),
        check_vma=False,
    )
```

profile of v0, /device:TPU:17, one launch (start us, length us, event | category | flops | bytes accessed | tf_op | source)
XLA Modules:
  0.0 101.3 jit_solution(10552802000820765589)
XLA Ops:
  6.5 0.8 slice_add_fusion
  7.3 0.7 compare_and_fusion
  8.0 0.7 add_select_fusion
  9.0 1.2 %convolution_convert_fusion.1 = bf16[384,256]{1,0:T(8,128)(2,1)S(1)} fusion(bf16[2048,256]{1,0:T(8,128)(2,1)S(1)} %bitcast.38, s32[512]{0:T(512)S(1)} %get-tuple-element.13, s32[512]{0:T(512)S(1)} %convert_reduce_fusion, pred[512]{0:T(512)(128)(4,1)S(1)} %compare_and_fusion), kind=kOutput, calls=%fused_computation.38 | convolution fusion | flops 639205376 | bytes 1249792 | tf_op jit(solution)/shard_map/dot_general | solution.py:55
  10.2 15.8 %all_gather.3 = bf16[1536,256]{1,0:T(8,128)(2,1)S(1)} all-gather(bf16[384,256]{1,0:T(8,128)(2,1)S(1)} %convolution_convert_fusion.1), channel_id=1, replica_groups=mesh['dom'=2,'frame'=4,'query'=2,'split'=2] {'frame'}, dimensions={0}, use_global_device_ids=true | all-gather | bytes 983040 | tf_op jit(solution)/shard_map/all_gather | solution.py:58
  25.9 0.7 fusion.23
  26.8 3.3 %fusion.57 = (f32[512,2]{0,1:T(2,128)S(1)}, f32[512,2,1024]{2,0,1:T(8,128)}) fusion(bf16[2,1024,256]{2,1,0:T(8,128)(2,1)S(1)} %copy-done, bf16[512,256]{1,0:T(8,128)(2,1)S(1)} %fusion.23), kind=kOutput, calls=%fused_computation.81 | convolution fusion | flops 540017664 | bytes 5509120 | tf_op jit(solution)/shard_map/sub | solution.py:70
  30.0 3.1 %multiply_reduce_fusion.3 = (f32[512,2]{0,1:T(2,128)S(1)}, f32[512,2,256]{0,2,1:T(8,128)S(1)}) fusion(bf16[2,1024,256]{2,1,0:T(8,128)(2,1)S(1)} %copy-done, f32[512,2,1024]{2,0,1:T(8,128)} %get-tuple-element.15, f32[512,2]{0,1:T(2,128)S(1)} %get-tuple-element.14), kind=kOutput, calls=%fused_computation.46 | convolution fusion | flops 539491328 | bytes 6299648 | tf_op jit(solution)/shard_map/qtp,tpc->qtc/dot_general | solution.py:72
  33.3 0.8 copy-done.2
  34.2 0.8 multiply_reduce_fusion.2
  35.3 4.1 %collective-permute-start = (bf16[512,1,512]{2,0,1:T(8,128)(2,1)S(1)}, bf16[512,1,512]{2,0,1:T(8,128)(2,1)S(1)}, u32[]{:S(2)}, u32[]{:S(2)}) collective-permute-start(bf16[512,1,512]{2,0,1:T(8,128)(2,1)S(1)} %get-tuple-element.7), channel_id=1, source_target_pairs={{0,4},{4,8},{8,12},{1,5},{5,9},{9,13},{2,6},{6,10},{10,14},{3,7},{... | collective-permute-start | bytes 1572872 | tf_op jit(solution)/shard_map/ppermute | solution.py:19
  39.4 2.1 %collective-permute-start.1 = (bf16[512,1,512]{2,0,1:T(8,128)(2,1)S(1)}, bf16[512,1,512]{2,0,1:T(8,128)(2,1)S(1)}, u32[]{:S(2)}, u32[]{:S(2)}) collective-permute-start(bf16[512,1,512]{2,0,1:T(8,128)(2,1)S(1)} %get-tuple-element.8), channel_id=1, source_target_pairs={{4,0},{8,4},{12,8},{5,1},{9,5},{13,9},{6,2},{10,6},{14,10},{7,3},{... | collective-permute-start | bytes 1572872 | tf_op jit(solution)/shard_map/ppermute | solution.py:21
  41.5 7.2 %collective-permute-done = bf16[512,1,512]{2,0,1:T(8,128)(2,1)S(1)} collective-permute-done((bf16[512,1,512]{2,0,1:T(8,128)(2,1)S(1)}, bf16[512,1,512]{2,0,1:T(8,128)(2,1)S(1)}, u32[]{:S(2)}, u32[]{:S(2)}) %collective-permute-start) | collective-permute-done | bytes 524320 | tf_op jit(solution)/shard_map/ppermute | solution.py:19
  48.7 3.8 %collective-permute-done.1 = bf16[512,1,512]{2,0,1:T(8,128)(2,1)S(1)} collective-permute-done((bf16[512,1,512]{2,0,1:T(8,128)(2,1)S(1)}, bf16[512,1,512]{2,0,1:T(8,128)(2,1)S(1)}, u32[]{:S(2)}, u32[]{:S(2)}) %collective-permute-start.1) | collective-permute-done | bytes 524320 | tf_op jit(solution)/shard_map/ppermute | solution.py:21
  52.5 0.3 maximum_convert_fusion
  52.9 0.7 multiply_reduce_fusion.1
  53.8 2.0 %copy.21 = bf16[512,2,512]{2,1,0:T(2,128)(2,1)} copy(bf16[512,2,512]{2,0,1:T(8,128)(2,1)S(1)} %divide_convert_fusion.1) | data formatting | bytes 2097152 | tf_op jit(solution)/shard_map/convert_element_type | solution.py:84
  55.8 2.3 %reshape.55 = bf16[1024,512]{1,0:T(8,128)(2,1)} reshape(bf16[512,2,512]{2,1,0:T(2,128)(2,1)} %copy.21) | data formatting | bytes 2097152 | tf_op jit(solution)/shard_map/reshape | solution.py:84
  58.1 5.3 %convolution_convert_fusion = bf16[1024,512]{1,0:T(8,128)(2,1)} fusion(bf16[1024,512]{1,0:T(8,128)(2,1)} %reshape.55, bf16[1,1024,512]{2,1,0:T(8,128)(2,1)} %param.13, bf16[1,512,1024]{2,1,0:T(8,128)(2,1)} %param.12), kind=kOutput, calls=%fused_computation.34 | convolution fusion | flops 2157445120 | bytes 4194304 | tf_op jit(solution)/shard_map/dot_general | solution.py:88
  63.4 2.3 %reshape.56 = bf16[512,2,512]{2,1,0:T(2,128)(2,1)} reshape(bf16[1024,512]{1,0:T(8,128)(2,1)} %convolution_convert_fusion) | data formatting | bytes 2097152 | tf_op jit(solution)/shard_map/reshape | solution.py:90
  65.6 2.4 %copy.22 = bf16[512,2,512]{2,0,1:T(8,128)(2,1)} copy(bf16[512,2,512]{2,1,0:T(2,128)(2,1)} %reshape.56) | data formatting | bytes 2097152 | tf_op jit(solution)/shard_map/reshape | solution.py:90
  68.0 22.8 %all-reduce.2.cloned.1.call-done = bf16[512,2,512]{2,0,1:T(8,128)(2,1)} async-done(((bf16[512,2,512]{2,0,1:T(8,128)(2,1)}), bf16[512,2,512]{2,0,1:T(8,128)(2,1)}) %all-reduce.2.cloned.1.call-update) | async-done | bytes 1048592 | tf_op jit(solution)/shard_map/psum | solution.py:89
  90.8 1.6 %add_convert_fusion = bf16[512,2,512]{2,0,1:T(8,128)(2,1)S(1)} fusion(f32[512,2,512]{2,0,1:T(8,128)S(1)} %get-tuple-element.6, bf16[512,2,512]{2,0,1:T(8,128)(2,1)} %all-reduce.2.cloned.1.call-done), kind=kLoop, calls=%fused_computation.25 | loop fusion | flops 1572864 | bytes 4194304 | tf_op jit(solution)/shard_map/convert_element_type | solution.py:91
  92.4 2.0 %copy.23 = bf16[512,2,512]{2,1,0:T(2,128)(2,1)} copy(bf16[512,2,512]{2,0,1:T(8,128)(2,1)S(1)} %add_convert_fusion) | data formatting | bytes 2097152 | tf_op jit(solution)/shard_map/convert_element_type | solution.py:91
  (19 shorter events, 1.1 us)
Async XLA Ops:
  6.5 2.4 %copy-start = (bf16[2,1024,256]{2,1,0:T(8,128)(2,1)S(1)}, bf16[2,1024,256]{2,1,0:T(8,128)(2,1)}, u32[]{:S(2)}) copy-start(bf16[2,1024,256]{2,1,0:T(8,128)(2,1)} %param.7) | copy-start | bytes 3145732
  6.5 84.3 %all-reduce.2.cloned.1.call-start = ((), (), s32[]{:S(2)}) async-start(), calls=%async_computation | async-start | bytes 2097152 | tf_op jit(solution)/shard_map/psum | solution.py:89
  33.1 1.0 %copy-start.2 = (bf16[512,512]{1,0:T(8,128)(2,1)S(1)}, bf16[512,512]{1,0:T(8,128)(2,1)}, u32[]{:S(2)}) copy-start(bf16[512,512]{1,0:T(8,128)(2,1)} %param.10) | copy-start | bytes 1572868
  35.0 6.5 %copy-start.1 = (f32[1,3,512]{2,0,1:T(1,128)S(1)}, f32[1,3,512]{2,0,1:T(1,128)}, u32[]{:S(2)}) copy-start(f32[1,3,512]{2,0,1:T(1,128)} %param.11) | copy-start | bytes 18436
  35.3 13.4 %collective-permute-start = (bf16[512,1,512]{2,0,1:T(8,128)(2,1)S(1)}, bf16[512,1,512]{2,0,1:T(8,128)(2,1)S(1)}, u32[]{:S(2)}, u32[]{:S(2)}) collective-permute-start(bf16[512,1,512]{2,0,1:T(8,128)(2,1)S(1)} %get-tuple-element.7), channel_id=1, source_target_pairs={{0,4},{4,8},{8,12},{1,5},{5,9},{9,13},{2,6},{6,10},{10,14},{3,7},{... | collective-permute-start | bytes 1572872 | tf_op jit(solution)/shard_map/ppermute | solution.py:19
  39.4 13.1 %collective-permute-start.1 = (bf16[512,1,512]{2,0,1:T(8,128)(2,1)S(1)}, bf16[512,1,512]{2,0,1:T(8,128)(2,1)S(1)}, u32[]{:S(2)}, u32[]{:S(2)}) collective-permute-start(bf16[512,1,512]{2,0,1:T(8,128)(2,1)S(1)} %get-tuple-element.8), channel_id=1, source_target_pairs={{4,0},{8,4},{12,8},{5,1},{9,5},{13,9},{6,2},{10,6},{14,10},{7,3},{... | collective-permute-start | bytes 1572872 | tf_op jit(solution)/shard_map/ppermute | solution.py:21
Sparse Core Ops, SparseCore 0:
  68.1 22.6 all-reduce.1
where the time goes:
time: 103 us; the launch traced here: 101 us
  waiting for transfers between devices  33.8 us (33%)
  blocking collectives  15.8 us (15%)
  matrix products  14.3 us (14%)
  between operations  13.5 us (13%)
  local copies, waits for them, and re-layouts  12.1 us (12%)
  starting transfers between devices  6.19 us (6%)
  other arithmetic  5.59 us (5%)
    psum x1, waiting for transfers between devices, on_device(): lax.psum(partial_delta.astype(jnp.bfloat16), 'split').astype(jnp.float32)  22.8 us
    all_gather x1, blocking collectives, on_device(): every_slot = lax.all_gather(packed, 'frame', axis=0, tiled=True)  15.8 us
    ppermute x1, waiting for transfers between devices, with_halo(): lax.ppermute(tail, axis, [(i, (i + 1) % count) for i in range(ends)])  7.17 us
    dot_general x1, matrix products, on_device(): jnp.dot(hidden, down_weight[0], preferred_element_type=jnp.float32)  5.26 us
    reshape x2, local copies, waits for them, and re-layouts, on_device(): stream = stream + summed.reshape(query_count, frame_count, width)  4.62 us
    ppermute x1, starting transfers between devices, with_halo(): lax.ppermute(tail, axis, [(i, (i + 1) % count) for i in range(ends)])  4.09 us
    ppermute x1, waiting for transfers between devices, with_halo(): lax.ppermute(head, axis, [((i + 1) % count, i) for i in range(ends)])  3.84 us
    sub x1, matrix products, on_device(): expd = jnp.exp(scores - peak)  3.28 us
  transfers between devices with their start and end apart: 3, of which 3 were waited for; matrix products, arithmetic and copies ran while one was open for 0% of the time, Pallas kernels for 0%

commit v1 on v0

v1 whole, which is shorter than its diff:
```python
import functools
import math

import jax
import jax.numpy as jnp
from jax import lax
from jax.experimental import pallas as pl
from jax.experimental.pallas import tpu as pltpu
from jax.sharding import PartitionSpec as P

LANES = 128
BF16 = jnp.bfloat16
F32 = jnp.float32
VMEM = pl.BlockSpec(memory_space=pltpu.VMEM)
ANY = pl.BlockSpec(memory_space=pl.ANY)


def dot(a, b):
    return jnp.dot(a, b, preferred_element_type=F32)


def dot_t(a, b):
    return lax.dot_general(a, b, (((1,), (1,)), ((), ())), preferred_element_type=F32)


def my_part(whole, part, parts):
    size = whole.shape[-1] // parts
    mine = whole[:, :size]
    for at in range(1, parts):
        mine = jnp.where(part == at, whole[:, at * size : (at + 1) * size], mine)
    return mine


def inverse_rms(values, epsilon):
    return lax.rsqrt(jnp.mean(values * values, axis=-1, keepdims=True) + epsilon)


def pick_body(parts, frame_ref, pixel_ref, frames_ref, out_ref):
    frame_count, pixel_count, _ = frames_ref.shape
    part = lax.axis_index("split")
    first = lax.axis_index("frame") * frame_count
    side = math.isqrt(pixel_count)
    pixel = pixel_ref[...]
    local = my_part(frame_ref[...], part, parts) - first
    row = my_part(pixel[0:1], part, parts)
    col = my_part(pixel[1:2], part, parts)
    owned = (local >= 0) & (local < frame_count)
    place = jnp.where(owned, local * pixel_count + row * side + col, -1)
    count = place.shape[1]
    place = jnp.transpose(jnp.broadcast_to(place, (8, count)))[:, :1]
    chunk = min(512, pixel_count)
    order = lax.broadcasted_iota(jnp.int32, (count, chunk), 1)
    total = None
    for t in range(frame_count):
        for at in range(0, pixel_count, chunk):
            start = t * pixel_count + at
            hot = jnp.where(order == place - start, 1.0, 0.0).astype(BF16)
            part_sum = dot(hot, frames_ref[t, at : at + chunk, :])
            total = part_sum if total is None else total + part_sum
    out_ref[...] = total.astype(BF16)


def add_body(a_ref, b_ref, out_ref):
    out_ref[...] = a_ref[...] + b_ref[...]


def attend(features, frame_ref, t, scale):
    rows = features.shape[0]
    step = 64
    out = []
    for at in range(0, rows, step):
        scores = dot_t(features[at : at + step], frame_ref[t])
        peak = jnp.max(scores, axis=-1, keepdims=True)
        expd = jnp.exp2((scores - peak) * scale)
        total = jnp.sum(expd, axis=-1, keepdims=True)
        pooled = dot(expd.astype(BF16), frame_ref[t])
        mean = jnp.mean(pooled * pooled, axis=-1, keepdims=True)
        out.append((pooled * lax.rsqrt(mean + 1e-6 * total * total)).astype(BF16))
    return jnp.concatenate(out, axis=0)


def attend_body(scale, a_ref, b_ref, frames_ref, normed_ref, features_ref, near_ref, far_ref):
    frame_count = frames_ref.shape[0]
    features = a_ref[...] + b_ref[...]
    features_ref[...] = features
    for t in range(frame_count):
        normed_ref[t] = attend(features, frames_ref, t, scale)
    even = lax.rem(lax.axis_index("frame"), 2) == 0
    first, last = normed_ref[0], normed_ref[frame_count - 1]
    near_ref[...] = jnp.where(even, last, first)
    far_ref[...] = jnp.where(even, first, last)


def mixer_body(
    devices,
    normed_ref,
    features_ref,
    near_ref,
    far_ref,
    in_ref,
    taps_ref,
    up_a_ref,
    up_b_ref,
    down_a_ref,
    down_b_ref,
    out_ref,
    scratch,
):
    frame_count, rows, channels = normed_ref.shape
    width = in_ref.shape[1]
    place = lax.axis_index("frame")
    even = lax.rem(place, 2) == 0
    near, far = near_ref[...], far_ref[...]
    before = jnp.where(even, far, near)
    after = jnp.where(even, near, far)
    base = dot(features_ref[...], in_ref[channels:, :])

    def stream_of(normed):
        return dot(normed, in_ref[:channels, :]) + base

    def level_of(stream):
        return (stream * inverse_rms(stream, 1e-5)).astype(BF16).astype(F32)

    streams = [stream_of(normed_ref[t]) for t in range(frame_count)]
    levels = [level_of(s) for s in streams]
    left = level_of(stream_of(before)) * (place > 0).astype(F32)
    right = level_of(stream_of(after)) * (place < devices - 1).astype(F32)
    levels = [left] + levels + [right]
    taps = taps_ref[0]
    gated = []
    for t in range(frame_count):
        mixed = (
            taps[0:1] * levels[t] + taps[1:2] * levels[t + 1] + taps[2:3] * levels[t + 2]
        )
        streams[t] = streams[t] + mixed
        gated.append((streams[t] * inverse_rms(streams[t], 1e-5)).astype(BF16))
    gated = jnp.concatenate(gated, axis=0)
    total = jnp.concatenate(streams, axis=0)
    for up_ref, down_ref in ((up_a_ref, down_a_ref), (up_b_ref, down_b_ref)):
        units = up_ref.shape[2]
        step = min(512, units)
        for at in range(0, units, step):
            hidden = jax.nn.gelu(dot(gated, up_ref[0, :, at : at + step])).astype(BF16)
            total = total + dot(hidden, down_ref[0, at : at + step, :])
    blocks = width // LANES
    stride = blocks * frame_count
    for t in range(frame_count):
        for b in range(blocks):
            scratch[pl.ds(b * frame_count + t, rows, stride=stride), :] = total[
                t * rows : (t + 1) * rows, b * LANES : (b + 1) * LANES
            ]
    out_ref[...] = scratch[...].astype(BF16)


def merge_body(own_ref, other_ref, out_ref, sems):
    rows = own_ref.shape[0]
    part = lax.axis_index("split")
    own = pltpu.make_async_copy(own_ref, out_ref.at[pl.ds(part * rows, rows)], sems.at[0])
    other = pltpu.make_async_copy(
        other_ref, out_ref.at[pl.ds((1 - part) * rows, rows)], sems.at[1]
    )
    own.start()
    other.start()
    own.wait()
    other.wait()


def on_device(frames, query_frame, query_pixel, in_weight, conv_weight, up_weight, down_weight):
    frame_count, pixel_count, channels = frames.shape
    query_count = query_frame.shape[0]
    width = in_weight.shape[1]
    parts = lax.axis_size("split")
    devices = lax.axis_size("frame")
    assert parts == 2 and devices & (devices - 1) == 0
    rows = query_count // parts
    swap = [(0, 1), (1, 0)]
    up_other = lax.ppermute(up_weight, "split", swap)
    down_other = lax.ppermute(down_weight, "split", swap)
    shape = jax.ShapeDtypeStruct
    mine = pl.pallas_call(
        functools.partial(pick_body, parts),
        out_shape=shape((rows, channels), BF16),
        in_specs=[VMEM] * 3,
        out_specs=VMEM,
        name="pick",
    )(query_frame.reshape(1, query_count), query_pixel, frames)
    stage = 1
    theirs = None
    while stage < devices:
        if theirs is not None:
            mine = pl.pallas_call(
                add_body,
                out_shape=shape((rows, channels), BF16),
                in_specs=[VMEM] * 2,
                out_specs=VMEM,
                name="join",
            )(mine, theirs)
        flip = 2 * stage - 1
        theirs = lax.ppermute(mine, "frame", [(i, i ^ flip) for i in range(devices)])
        stage *= 2
    scale = math.log2(math.e) / math.sqrt(channels)
    normed, features, near, far = pl.pallas_call(
        functools.partial(attend_body, scale),
        out_shape=(
            shape((frame_count, rows, channels), BF16),
            shape((rows, channels), BF16),
            shape((rows, channels), BF16),
            shape((rows, channels), BF16),
        ),
        in_specs=[VMEM] * 3,
        out_specs=(VMEM,) * 4,
        name="attend",
    )(mine, theirs, frames)
    near = lax.ppermute(near, "frame", [(i, i ^ 1) for i in range(devices)])
    pairs = [(i, i + 1) for i in range(1, devices - 1, 2)]
    far = lax.ppermute(far, "frame", pairs + [(b, a) for a, b in pairs])
    blocks = width // LANES
    lines = rows * blocks * frame_count
    own = pl.pallas_call(
        functools.partial(mixer_body, devices),
        out_shape=shape((lines, LANES), BF16),
        in_specs=[VMEM] * 10,
        out_specs=VMEM,
        scratch_shapes=[pltpu.VMEM((lines, LANES), F32)],
        name="mixer",
    )(
        normed,
        features,
        near,
        far,
        in_weight,
        conv_weight,
        up_weight,
        up_other,
        down_weight,
        down_other,
    )
    other = lax.ppermute(own, "split", swap)
    both = pl.pallas_call(
        merge_body,
        out_shape=shape((parts * lines, LANES), BF16),
        in_specs=[ANY] * 2,
        out_specs=ANY,
        scratch_shapes=[pltpu.SemaphoreType.DMA((2,))],
        name="merge",
    )(own, other)
    both = both.reshape(query_count, blocks, frame_count, LANES)
    return both.transpose(0, 2, 1, 3).reshape(query_count, frame_count, width)


def solution(mesh):
    return jax.shard_map(
        on_device,
        mesh=mesh,
        in_specs=(
            P(("dom", "frame"), None, None),
            P(("dom", "query")),
            P(None, ("dom", "query")),
            P(),
            P(),
            P(None, None, "split"),
            P(None, "split", None),
        ),
        out_specs=P(("dom", "query"), "frame", None),
        check_vma=False,
    )
```

time: 103 us -> 78.2 us (0.76); the launches traced: 101 us -> 78 us
  Pallas kernels: 0 us -> 50.4 us
  waiting for transfers between devices: 33.8 us -> 13.7 us
  blocking collectives: 15.8 us -> 0 us
  matrix products: 14.3 us -> 0 us
  between operations: 13.5 us -> 0.05 us
  local copies, waits for them, and re-layouts: 12.1 us -> 4.05 us
  other arithmetic: 5.59 us -> 0 us
  starting transfers between devices: 6.19 us -> 9.82 us
    pallas_call x0 -> x5, Pallas kernels: none -> 50.4 us  [the longest x1 32.9 us: on_device(): pl.pallas_call(merge_body, out_shape=shape((parts * lines, LANES), BF16),...]
    psum x1 -> x0, waiting for transfers between devices: 22.8 us -> none  [on_device(): lax.psum(partial_delta.astype(jnp.bfloat16), 'split').astype(jnp.float32)]
    all_gather x1 -> x0, blocking collectives: 15.8 us -> none  [on_device(): every_slot = lax.all_gather(packed, 'frame', axis=0, tiled=True)]
    dot_general x5 -> x0, matrix products: 11 us -> none  [the longest x1 5.26 us: on_device(): jnp.dot(hidden, down_weight[0], preferred_element_type=jnp.float32)]
    reshape x3 -> x0, local copies, waits for them, and re-layouts: 6.88 us -> none  [the longest x2 4.62 us: on_device(): stream = stream + summed.reshape(query_count, frame_count, width)]
    convert_element_type x3 -> x0, local copies, waits for them, and re-layouts: 4.24 us -> none  [the longest x1 2.05 us: on_device(): rms_scale(stream, 1e-05).astype(jnp.bfloat16).reshape(rows_total, width)]
    ppermute x2 -> x7, starting transfers between devices: 6.19 us -> 9.82 us  [the longest x1 3.54 us: on_device(): other = lax.ppermute(own, 'split', swap)]
    sub x1 -> x0, matrix products: 3.28 us -> none  [on_device(): expd = jnp.exp(scores - peak)]
  transfers between devices with their start and end apart: 3 -> 7, of which waited for: 3 -> 4; matrix products, arithmetic and copies ran while one was open for 0% -> 1% of each run, Pallas kernels for 0% -> 13%
where the time goes in v1:
time: 78.2 us; the launch traced here: 78 us
  Pallas kernels  50.4 us (64%)
  waiting for transfers between devices  13.7 us (18%)
  starting transfers between devices  9.82 us (13%)
  local copies, waits for them, and re-layouts  4.05 us (5%)
    pallas_call x1, Pallas kernels, on_device(): pl.pallas_call(merge_body, out_shape=shape((parts * lines, LANES), BF16),...  32.9 us
    ppermute x2, waiting for transfers between devices, on_device(): lax.ppermute(mine, 'frame', [(i, i ^ flip) for i in range(devices)])  8.76 us
    pallas_call x1, Pallas kernels, on_device(): pl.pallas_call(functools.partial(mixer_body, devices), out_shape=shape((l...  7.52 us
    pallas_call x1, Pallas kernels, on_device(): pl.pallas_call(functools.partial(attend_body, scale), out_shape=(shape((f...  5.7 us
    unnamed x17, local copies, waits for them, and re-layouts  4.05 us
    ppermute x1, starting transfers between devices, on_device(): other = lax.ppermute(own, 'split', swap)  3.54 us
    ppermute x1, waiting for transfers between devices, on_device(): far = lax.ppermute(far, 'frame', pairs + [(b, a) for a, b in pairs])  3.2 us
    pallas_call x1, Pallas kernels, on_device(): pl.pallas_call(functools.partial(pick_body, parts), out_shape=shape((rows...  2.62 us
  transfers between devices with their start and end apart: 7, of which 4 were waited for; matrix products, arithmetic and copies ran while one was open for 1% of the time, Pallas kernels for 13%

profile of v1, /device:TPU:17, one launch (start us, length us, event | category | flops | bytes accessed | tf_op | source)
XLA Modules:
  0.0 78.0 jit_solution(10325580427683182281)
XLA Ops:
  0.0 0.7 collective-permute-start.4
  0.7 2.6 %pick.1.a_ref = bf16[256,256]{1,0:T(8,128)(2,1)} custom-call(s32[1,512]{1,0:T(1,128)} %bitcast.6, s32[2,512]{1,0:T(2,128)} %pixel_ref.1, bf16[2,1024,256]{2,1,0:T(8,128)(2,1)} %frames_ref.3), custom_call_target="tpu_custom_call" | custom-call | tf_op jit(solution)/shard_map/pick/pallas_call | solution.py:180
  3.3 1.3 %collective-permute-start = (bf16[256,256]{1,0:T(8,128)(2,1)}, bf16[256,256]{1,0:T(8,128)(2,1)S(1)}, u32[]{:S(2)}, u32[]{:S(2)}) collective-permute-start(bf16[256,256]{1,0:T(8,128)(2,1)} %pick.1.a_ref), channel_id=1, source_target_pairs={{0,4},{4,0},{8,12},{12,8},{1,5},{5,1},{9,13},{13,9},{2,6},{6,2},{1... | collective-permute-start | bytes 393224 | tf_op jit(solution)/shard_map/ppermute | solution.py:199
  4.6 3.5 %collective-permute-done.b_ref = bf16[256,256]{1,0:T(8,128)(2,1)S(1)} collective-permute-done((bf16[256,256]{1,0:T(8,128)(2,1)}, bf16[256,256]{1,0:T(8,128)(2,1)S(1)}, u32[]{:S(2)}, u32[]{:S(2)}) %collective-permute-start) | collective-permute-done | bytes 131104 | tf_op jit(solution)/shard_map/ppermute | solution.py:199
  8.1 0.7 copy-done.6
  8.7 1.6 %join.1.a_ref = bf16[256,256]{1,0:T(8,128)(2,1)} custom-call(bf16[256,256]{1,0:T(8,128)(2,1)} %pick.1.a_ref, bf16[256,256]{1,0:T(8,128)(2,1)} %copy-done.6), custom_call_target="tpu_custom_call" | custom-call | tf_op jit(solution)/shard_map/join/pallas_call | solution.py:191
  10.3 0.2 collective-permute-start.1
  10.5 5.3 %collective-permute-done.1.b_ref = bf16[256,256]{1,0:T(8,128)(2,1)S(1)} collective-permute-done((bf16[256,256]{1,0:T(8,128)(2,1)}, bf16[256,256]{1,0:T(8,128)(2,1)S(1)}, u32[]{:S(2)}, u32[]{:S(2)}) %collective-permute-start.1) | collective-permute-done | bytes 131104 | tf_op jit(solution)/shard_map/ppermute | solution.py:199
  15.8 0.7 copy-done.5
  16.5 5.7 %attend.1 = (bf16[2,256,256]{2,1,0:T(8,128)(2,1)}, bf16[256,256]{1,0:T(8,128)(2,1)}, bf16[256,256]{1,0:T(8,128)(2,1)}, bf16[256,256]{1,0:T(8,128)(2,1)}) custom-call(bf16[256,256]{1,0:T(8,128)(2,1)} %join.1.a_ref, bf16[256,256]{1,0:T(8,128)(2,1)} %copy-done.5, bf16[2,1024,256]{2,1,0:T(8,128)(2,1)} %frames_ref.3), custom_call_target="tpu_custom_call" | custom-call | tf_op jit(solution)/shard_map/attend/pallas_call | solution.py:202
  22.2 1.8 %collective-permute-start.2 = (bf16[256,256]{1,0:T(8,128)(2,1)}, bf16[256,256]{1,0:T(8,128)(2,1)S(1)}, u32[]{:S(2)}, u32[]{:S(2)}) collective-permute-start(bf16[256,256]{1,0:T(8,128)(2,1)} %get-tuple-element.11), channel_id=1, source_target_pairs={{0,4},{4,0},{8,12},{12,8},{1,5},{5,1},{9,13},{13,9},{2,6},{6,2},{1... | collective-permute-start | bytes 393224 | tf_op jit(solution)/shard_map/ppermute | solution.py:214
  23.9 2.4 %collective-permute-start.3 = (bf16[256,256]{1,0:T(8,128)(2,1)}, bf16[256,256]{1,0:T(8,128)(2,1)S(1)}, u32[]{:S(2)}, u32[]{:S(2)}) collective-permute-start(bf16[256,256]{1,0:T(8,128)(2,1)} %get-tuple-element.12), channel_id=1, source_target_pairs={{4,8},{8,4},{5,9},{9,5},{6,10},{10,6},{7,11},{11,7},{20,24},{24,20... | collective-permute-start | bytes 393224 | tf_op jit(solution)/shard_map/ppermute | solution.py:216
  26.3 0.6 copy.8.taps_ref
  26.9 0.0 collective-permute-done.2.near_ref
  26.9 3.2 %collective-permute-done.3.far_ref = bf16[256,256]{1,0:T(8,128)(2,1)S(1)} collective-permute-done((bf16[256,256]{1,0:T(8,128)(2,1)}, bf16[256,256]{1,0:T(8,128)(2,1)S(1)}, u32[]{:S(2)}, u32[]{:S(2)}) %collective-permute-start.3) | collective-permute-done | bytes 131104 | tf_op jit(solution)/shard_map/ppermute | solution.py:216
  30.1 0.0 collective-permute-done.4.up_b_ref
  30.2 0.6 copy-done.4
  30.8 0.4 copy-done
  31.2 0.4 copy-done.1
  31.5 7.5 %mixer.1.own_ref = bf16[2048,128]{1,0:T(8,128)(2,1)} custom-call(bf16[2,256,256]{2,1,0:T(8,128)(2,1)} %get-tuple-element.9.normed_ref, bf16[256,256]{1,0:T(8,128)(2,1)} %get-tuple-element.10.features_ref, bf16[256,256]{1,0:T(8,128)(2,1)} %copy-done.3, bf16[256,256]{1,0:T(8,128)(2,1)} %copy-done.4, bf16[512,512]{1,0:T(8,128)(2,1)} %in_ref.1, ...), custom_call_target="tpu_custom_call" | custom-call | tf_op jit(solution)/shard_map/mixer/pallas_call | solution.py:219
  39.0 3.5 %collective-permute-start.6 = (bf16[2048,128]{1,0:T(8,128)(2,1)}, bf16[2048,128]{1,0:T(8,128)(2,1)S(1)}, u32[]{:S(2)}, u32[]{:S(2)}) collective-permute-start(bf16[2048,128]{1,0:T(8,128)(2,1)} %mixer.1.own_ref), channel_id=1, source_target_pairs={{0,1},{1,0},{2,3},{3,2},{4,5},{5,4},{6,7},{7,6},{8,9},{9,8},{10,11... | collective-permute-start | bytes 1572872 | tf_op jit(solution)/shard_map/ppermute | solution.py:238
  42.6 1.7 %collective-permute-done.6.other_ref = bf16[2048,128]{1,0:T(8,128)(2,1)S(1)} collective-permute-done((bf16[2048,128]{1,0:T(8,128)(2,1)}, bf16[2048,128]{1,0:T(8,128)(2,1)S(1)}, u32[]{:S(2)}, u32[]{:S(2)}) %collective-permute-start.6) | collective-permute-done | bytes 524320 | tf_op jit(solution)/shard_map/ppermute | solution.py:238
  44.3 0.8 %copy-done.2 = bf16[2048,128]{1,0:T(8,128)(2,1)} copy-done((bf16[2048,128]{1,0:T(8,128)(2,1)}, bf16[2048,128]{1,0:T(8,128)(2,1)S(1)}, u32[]{:S(2)}) %copy-start.2) | copy-done | bytes 524312
  45.1 32.9 %merge.1 = bf16[4096,128]{1,0:T(8,128)(2,1)} custom-call(bf16[2048,128]{1,0:T(8,128)(2,1)} %mixer.1.own_ref, bf16[2048,128]{1,0:T(8,128)(2,1)} %copy-done.2), custom_call_target="tpu_custom_call" | custom-call | tf_op jit(solution)/shard_map/merge/pallas_call | solution.py:239
  (12 shorter events, 0.0 us)
Async XLA Ops:
  0.0 30.1 %collective-permute-start.4 = (bf16[1,512,1024]{2,1,0:T(8,128)(2,1)}, bf16[1,512,1024]{2,1,0:T(8,128)(2,1)S(1)}, u32[]{:S(2)}, u32[]{:S(2)}) collective-permute-start(bf16[1,512,1024]{2,1,0:T(8,128)(2,1)} %up_a_ref.1), channel_id=1, source_target_pairs={{0,1},{1,0},{2,3},{3,2},{4,5},{5,4},{6,7},{7,6},{8,9},{9,8},{10,11... | collective-permute-start | bytes 3145736 | tf_op jit(solution)/shard_map/ppermute | solution.py:177
  0.7 29.5 %collective-permute-start.5 = (bf16[1,1024,512]{2,1,0:T(8,128)(2,1)}, bf16[1,1024,512]{2,1,0:T(8,128)(2,1)S(1)}, u32[]{:S(2)}, u32[]{:S(2)}) collective-permute-start(bf16[1,1024,512]{2,1,0:T(8,128)(2,1)} %down_a_ref.1), channel_id=1, source_target_pairs={{0,1},{1,0},{2,3},{3,2},{4,5},{5,4},{6,7},{7,6},{8,9},{9,8},{10,11... | collective-permute-start | bytes 3145736 | tf_op jit(solution)/shard_map/ppermute | solution.py:178
  3.3 4.8 %collective-permute-start = (bf16[256,256]{1,0:T(8,128)(2,1)}, bf16[256,256]{1,0:T(8,128)(2,1)S(1)}, u32[]{:S(2)}, u32[]{:S(2)}) collective-permute-start(bf16[256,256]{1,0:T(8,128)(2,1)} %pick.1.a_ref), channel_id=1, source_target_pairs={{0,4},{4,0},{8,12},{12,8},{1,5},{5,1},{9,13},{13,9},{2,6},{6,2},{1... | collective-permute-start | bytes 393224 | tf_op jit(solution)/shard_map/ppermute | solution.py:199
  8.1 0.7 copy-start.6
  10.3 5.5 %collective-permute-start.1 = (bf16[256,256]{1,0:T(8,128)(2,1)}, bf16[256,256]{1,0:T(8,128)(2,1)S(1)}, u32[]{:S(2)}, u32[]{:S(2)}) collective-permute-start(bf16[256,256]{1,0:T(8,128)(2,1)} %join.1.a_ref), channel_id=1, source_target_pairs={{0,12},{4,8},{8,4},{12,0},{1,13},{5,9},{9,5},{13,1},{2,14},{6,10},... | collective-permute-start | bytes 393224 | tf_op jit(solution)/shard_map/ppermute | solution.py:199
  15.8 0.7 copy-start.5
  16.5 9.9 %copy-start.7 = (f32[1,3,512]{2,0,1:T(1,128)S(1)}, f32[1,3,512]{2,0,1:T(1,128)}, u32[]{:S(2)}) copy-start(f32[1,3,512]{2,0,1:T(1,128)} %param.11) | copy-start | bytes 18436
  22.2 4.8 %collective-permute-start.2 = (bf16[256,256]{1,0:T(8,128)(2,1)}, bf16[256,256]{1,0:T(8,128)(2,1)S(1)}, u32[]{:S(2)}, u32[]{:S(2)}) collective-permute-start(bf16[256,256]{1,0:T(8,128)(2,1)} %get-tuple-element.11), channel_id=1, source_target_pairs={{0,4},{4,0},{8,12},{12,8},{1,5},{5,1},{9,13},{13,9},{2,6},{6,2},{1... | collective-permute-start | bytes 393224 | tf_op jit(solution)/shard_map/ppermute | solution.py:214
  23.9 6.2 %collective-permute-start.3 = (bf16[256,256]{1,0:T(8,128)(2,1)}, bf16[256,256]{1,0:T(8,128)(2,1)S(1)}, u32[]{:S(2)}, u32[]{:S(2)}) collective-permute-start(bf16[256,256]{1,0:T(8,128)(2,1)} %get-tuple-element.12), channel_id=1, source_target_pairs={{4,8},{8,4},{5,9},{9,5},{6,10},{10,6},{7,11},{11,7},{20,24},{24,20... | collective-permute-start | bytes 393224 | tf_op jit(solution)/shard_map/ppermute | solution.py:216
  26.9 3.2 %copy-start.3 = (bf16[256,256]{1,0:T(8,128)(2,1)}, bf16[256,256]{1,0:T(8,128)(2,1)S(1)}, u32[]{:S(2)}) copy-start(bf16[256,256]{1,0:T(8,128)(2,1)S(1)} %collective-permute-done.2.near_ref) | copy-start | bytes 393220
  30.1 0.6 copy-start.4
  30.1 1.0 %copy-start = (bf16[1,512,1024]{2,1,0:T(8,128)(2,1)}, bf16[1,512,1024]{2,1,0:T(8,128)(2,1)S(1)}, u32[]{:S(2)}) copy-start(bf16[1,512,1024]{2,1,0:T(8,128)(2,1)S(1)} %collective-permute-done.4.up_b_ref) | copy-start | bytes 3145732
  30.2 1.4 %copy-start.1 = (bf16[1,1024,512]{2,1,0:T(8,128)(2,1)}, bf16[1,1024,512]{2,1,0:T(8,128)(2,1)S(1)}, u32[]{:S(2)}) copy-start(bf16[1,1024,512]{2,1,0:T(8,128)(2,1)S(1)} %collective-permute-done.5.down_b_ref) | copy-start | bytes 3145732
  39.0 5.3 %collective-permute-start.6 = (bf16[2048,128]{1,0:T(8,128)(2,1)}, bf16[2048,128]{1,0:T(8,128)(2,1)S(1)}, u32[]{:S(2)}, u32[]{:S(2)}) collective-permute-start(bf16[2048,128]{1,0:T(8,128)(2,1)} %mixer.1.own_ref), channel_id=1, source_target_pairs={{0,1},{1,0},{2,3},{3,2},{4,5},{5,4},{6,7},{7,6},{8,9},{9,8},{10,11... | collective-permute-start | bytes 1572872 | tf_op jit(solution)/shard_map/ppermute | solution.py:238
  44.3 0.8 %copy-start.2 = (bf16[2048,128]{1,0:T(8,128)(2,1)}, bf16[2048,128]{1,0:T(8,128)(2,1)S(1)}, u32[]{:S(2)}) copy-start(bf16[2048,128]{1,0:T(8,128)(2,1)S(1)} %collective-permute-done.6.other_ref) | copy-start | bytes 1572868

commit v2 on v1

--- a/solution.py
+++ b/solution.py
@@ -9,10 +9,19 @@
 from jax.sharding import PartitionSpec as P
 
 LANES = 128
+ROOM = 24 * 1024 * 1024
 BF16 = jnp.bfloat16
 F32 = jnp.float32
 VMEM = pl.BlockSpec(memory_space=pltpu.VMEM)
 ANY = pl.BlockSpec(memory_space=pl.ANY)
+
+
+def held(value):
+    return pltpu.with_memory_space_constraint(value, pltpu.VMEM)
+
+
+def kept(shape, dtype):
+    return pltpu.VMEM(shape, dtype)
 
 
 def dot(a, b):
@@ -126,11 +135,11 @@
     left = level_of(stream_of(before)) * (place > 0).astype(F32)
     right = level_of(stream_of(after)) * (place < devices - 1).astype(F32)
     levels = [left] + levels + [right]
-    taps = taps_ref[0]
+    taps = [taps_ref[:, at : at + width] for at in range(0, taps_ref.shape[1], width)]
     gated = []
     for t in range(frame_count):
         mixed = (
-            taps[0:1] * levels[t] + taps[1:2] * levels[t + 1] + taps[2:3] * levels[t + 2]
+            taps[0] * levels[t] + taps[1] * levels[t + 1] + taps[2] * levels[t + 2]
         )
         streams[t] = streams[t] + mixed
         gated.append((streams[t] * inverse_rms(streams[t], 1e-5)).astype(BF16))
@@ -174,14 +183,15 @@
     assert parts == 2 and devices & (devices - 1) == 0
     rows = query_count // parts
     swap = [(0, 1), (1, 0)]
-    up_other = lax.ppermute(up_weight, "split", swap)
-    down_other = lax.ppermute(down_weight, "split", swap)
-    shape = jax.ShapeDtypeStruct
+    up_other = held(lax.ppermute(up_weight, "split", swap))
+    down_other = held(lax.ppermute(down_weight, "split", swap))
+    frames = held(frames)
     mine = pl.pallas_call(
         functools.partial(pick_body, parts),
-        out_shape=shape((rows, channels), BF16),
+        out_shape=kept((rows, channels), BF16),
         in_specs=[VMEM] * 3,
         out_specs=VMEM,
+        compiler_params=pltpu.CompilerParams(vmem_limit_bytes=ROOM),
         name="pick",
     )(query_frame.reshape(1, query_count), query_pixel, frames)
     stage = 1
@@ -190,58 +200,62 @@
         if theirs is not None:
             mine = pl.pallas_call(
                 add_body,
-                out_shape=shape((rows, channels), BF16),
+                out_shape=kept((rows, channels), BF16),
                 in_specs=[VMEM] * 2,
                 out_specs=VMEM,
-                name="join",
+                compiler_params=pltpu.CompilerParams(vmem_limit_bytes=ROOM),
+        name="join",
             )(mine, theirs)
         flip = 2 * stage - 1
-        theirs = lax.ppermute(mine, "frame", [(i, i ^ flip) for i in range(devices)])
+        theirs = held(lax.ppermute(mine, "frame", [(i, i ^ flip) for i in range(devices)]))
         stage *= 2
     scale = math.log2(math.e) / math.sqrt(channels)
     normed, features, near, far = pl.pallas_call(
         functools.partial(attend_body, scale),
         out_shape=(
-            shape((frame_count, rows, channels), BF16),
-            shape((rows, channels), BF16),
-            shape((rows, channels), BF16),
-            shape((rows, channels), BF16),
+            kept((frame_count, rows, channels), BF16),
+            kept((rows, channels), BF16),
+            kept((rows, channels), BF16),
+            kept((rows, channels), BF16),
         ),
         in_specs=[VMEM] * 3,
         out_specs=(VMEM,) * 4,
+        compiler_params=pltpu.CompilerParams(vmem_limit_bytes=ROOM),
         name="attend",
     )(mine, theirs, frames)
-    near = lax.ppermute(near, "frame", [(i, i ^ 1) for i in range(devices)])
+    near = held(lax.ppermute(near, "frame", [(i, i ^ 1) for i in range(devices)]))
     pairs = [(i, i + 1) for i in range(1, devices - 1, 2)]
-    far = lax.ppermute(far, "frame", pairs + [(b, a) for a, b in pairs])
+    far = held(lax.ppermute(far, "frame", pairs + [(b, a) for a, b in pairs]))
     blocks = width // LANES
     lines = rows * blocks * frame_count
     own = pl.pallas_call(
         functools.partial(mixer_body, devices),
-        out_shape=shape((lines, LANES), BF16),
+        out_shape=kept((lines, LANES), BF16),
         in_specs=[VMEM] * 10,
         out_specs=VMEM,
         scratch_shapes=[pltpu.VMEM((lines, LANES), F32)],
+        compiler_params=pltpu.CompilerParams(vmem_limit_bytes=ROOM),
         name="mixer",
     )(
         normed,
         features,
         near,
         far,
-        in_weight,
-        conv_weight,
-        up_weight,
+        held(in_weight),
+        held(conv_weight.reshape(1, conv_weight.shape[1] * width)),
+        held(up_weight),
         up_other,
-        down_weight,
+        held(down_weight),
         down_other,
     )
-    other = lax.ppermute(own, "split", swap)
+    other = held(lax.ppermute(own, "split", swap))
     both = pl.pallas_call(
         merge_body,
-        out_shape=shape((parts * lines, LANES), BF16),
-        in_specs=[ANY] * 2,
+        out_shape=jax.ShapeDtypeStruct((parts * lines, LANES), BF16),
+        in_specs=[VMEM] * 2,
         out_specs=ANY,
         scratch_shapes=[pltpu.SemaphoreType.DMA((2,))],
+        compiler_params=pltpu.CompilerParams(vmem_limit_bytes=ROOM),
         name="merge",
     )(own, other)
     both = both.reshape(query_count, blocks, frame_count, LANES)

time: 78.2 us -> 37.1 us (0.47)
  Pallas kernels: 50.4 us -> 9.31 us
    pallas_call x5, Pallas kernels: 50.4 us -> 9.31 us  [the longest x1 4.09 us: on_device(): pl.pallas_call(functools.partial(mixer_body, devices), out_shape=kept((li...]
    unnamed x17 -> x16, local copies, waits for them, and re-layouts: 4.05 us -> 3.83 us
  transfers between devices with their start and end apart: 7 -> 7, of which waited for: 4 -> 4; matrix products, arithmetic and copies ran while one was open for 1% -> 0% of each run, Pallas kernels for 13% -> 12%
where the time goes in v2:
time: 37.1 us; the launch traced here: 36.8 us
  waiting for transfers between devices  13.3 us (36%)
  starting transfers between devices  10.2 us (27%)
  Pallas kernels  9.31 us (25%)
  local copies, waits for them, and re-layouts  3.83 us (10%)
    ppermute x2, waiting for transfers between devices, on_device(): lax.ppermute(mine, 'frame', [(i, i ^ flip) for i in range(devices)])  8.23 us
    pallas_call x1, Pallas kernels, on_device(): pl.pallas_call(functools.partial(mixer_body, devices), out_shape=kept((li...  4.09 us
    unnamed x16, local copies, waits for them, and re-layouts  3.83 us
    ppermute x1, starting transfers between devices, on_device(): other = held(lax.ppermute(own, 'split', swap))  3.62 us
    ppermute x1, waiting for transfers between devices, on_device(): far = held(lax.ppermute(far, 'frame', pairs + [(b, a) for a, b in pairs]))  3.58 us
    pallas_call x1, Pallas kernels, on_device(): pl.pallas_call(functools.partial(attend_body, scale), out_shape=(kept((fr...  3.53 us
    ppermute x1, starting transfers between devices, on_device(): far = held(lax.ppermute(far, 'frame', pairs + [(b, a) for a, b in pairs]))  2.4 us
    ppermute x1, starting transfers between devices, on_device(): lax.ppermute(near, 'frame', [(i, i ^ 1) for i in range(devices)])  1.93 us
  transfers between devices with their start and end apart: 7, of which 4 were waited for; matrix products, arithmetic and copies ran while one was open for 0% of the time, Pallas kernels for 12%

profile of v2, /device:TPU:17, one launch (start us, length us, event | category | flops | bytes accessed | tf_op | source)
XLA Modules:
  0.0 36.8 jit_solution(3239331072568933356)
XLA Ops:
  0.0 0.7 %collective-permute-start.4 = (bf16[1,512,1024]{2,1,0:T(8,128)(2,1)}, bf16[1,512,1024]{2,1,0:T(8,128)(2,1)S(1)}, u32[]{:S(2)}, u32[]{:S(2)}) collective-permute-start(bf16[1,512,1024]{2,1,0:T(8,128)(2,1)} %up_a_ref.1), channel_id=1, source_target_pairs={{0,1},{1,0},{2,3},{3,2},{4,5},{5,4},{6,7},{7,6},{8,9},{9,8},{10,11... | collective-permute-start | bytes 3145736 | tf_op jit(solution)/shard_map/ppermute | solution.py:186
  0.7 1.2 %copy-done = bf16[2,1024,256]{2,1,0:T(8,128)(2,1)S(1)} copy-done((bf16[2,1024,256]{2,1,0:T(8,128)(2,1)S(1)}, bf16[2,1024,256]{2,1,0:T(8,128)(2,1)}, u32[]{:S(2)}) %copy-start) | copy-done | bytes 1048600
  1.9 0.7 %copy-done.6 = s32[2,512]{1,0:T(2,128)S(1)} copy-done((s32[2,512]{1,0:T(2,128)S(1)}, s32[2,512]{1,0:T(2,128)}, u32[]{:S(2)}) %copy-start.6) | copy-done | bytes 4120
  2.6 0.7 %copy-done.7 = s32[512]{0:T(512)S(1)} copy-done((s32[512]{0:T(512)S(1)}, s32[512]{0:T(512)}, u32[]{:S(2)}) %copy-start.7) | copy-done | bytes 2072
  3.3 0.7 %pick.1.a_ref = bf16[256,256]{1,0:T(8,128)(2,1)S(1)} custom-call(s32[1,512]{1,0:T(1,128)S(1)} %bitcast.8, s32[2,512]{1,0:T(2,128)S(1)} %copy-done.6, bf16[2,1024,256]{2,1,0:T(8,128)(2,1)S(1)} %copy-done), custom_call_target="tpu_custom_call" | custom-call | tf_op jit(solution)/shard_map/pick/pallas_call | solution.py:189
  4.0 0.0 copy-start.2
  4.0 1.4 %collective-permute-start = (bf16[256,256]{1,0:T(8,128)(2,1)S(1)}, bf16[256,256]{1,0:T(8,128)(2,1)S(1)}, u32[]{:S(2)}, u32[]{:S(2)}) collective-permute-start(bf16[256,256]{1,0:T(8,128)(2,1)S(1)} %pick.1.a_ref), channel_id=1, source_target_pairs={{0,4},{4,0},{8,12},{12,8},{1,5},{5,1},{9,13},{13,9},{2,6},{6,2},{1... | collective-permute-start | bytes 393224 | tf_op jit(solution)/shard_map/ppermute | solution.py:210
  5.4 3.2 %collective-permute-done.b_ref = bf16[256,256]{1,0:T(8,128)(2,1)S(1)} collective-permute-done((bf16[256,256]{1,0:T(8,128)(2,1)S(1)}, bf16[256,256]{1,0:T(8,128)(2,1)S(1)}, u32[]{:S(2)}, u32[]{:S(2)}) %collective-permute-start) | collective-permute-done | bytes 131104 | tf_op jit(solution)/shard_map/ppermute | solution.py:210
  8.6 0.0 copy-start.4
  8.6 0.2 collective-permute-start.1
  8.9 5.0 %collective-permute-done.1.b_ref = bf16[256,256]{1,0:T(8,128)(2,1)S(1)} collective-permute-done((bf16[256,256]{1,0:T(8,128)(2,1)S(1)}, bf16[256,256]{1,0:T(8,128)(2,1)S(1)}, u32[]{:S(2)}, u32[]{:S(2)}) %collective-permute-start.1) | collective-permute-done | bytes 131104 | tf_op jit(solution)/shard_map/ppermute | solution.py:210
  13.9 3.5 %attend.1 = (bf16[2,256,256]{2,1,0:T(8,128)(2,1)S(1)}, bf16[256,256]{1,0:T(8,128)(2,1)S(1)}, bf16[256,256]{1,0:T(8,128)(2,1)S(1)}, bf16[256,256]{1,0:T(8,128)(2,1)S(1)}) custom-call(bf16[256,256]{1,0:T(8,128)(2,1)S(1)} %join.1.a_ref, bf16[256,256]{1,0:T(8,128)(2,1)S(1)} %collective-permute-done.1.b_ref, bf16[2,1024,256]{2,1,0:T(8,128)(2,1)S(1)} %copy-done.1), custom_call_target="tpu_custom_call" | custom-call | tf_op jit(solution)/shard_map/attend/pallas_call | solution.py:213
  17.4 0.0 copy-start.5
  17.4 1.9 %collective-permute-start.2 = (bf16[256,256]{1,0:T(8,128)(2,1)S(1)}, bf16[256,256]{1,0:T(8,128)(2,1)S(1)}, u32[]{:S(2)}, u32[]{:S(2)}) collective-permute-start(bf16[256,256]{1,0:T(8,128)(2,1)S(1)} %get-tuple-element.11), channel_id=1, source_target_pairs={{0,4},{4,0},{8,12},{12,8},{1,5},{5,1},{9,13},{13,9},{2,6},{6,2},{1... | collective-permute-start | bytes 393224 | tf_op jit(solution)/shard_map/ppermute | solution.py:226
  19.3 2.4 %collective-permute-start.3 = (bf16[256,256]{1,0:T(8,128)(2,1)S(1)}, bf16[256,256]{1,0:T(8,128)(2,1)S(1)}, u32[]{:S(2)}, u32[]{:S(2)}) collective-permute-start(bf16[256,256]{1,0:T(8,128)(2,1)S(1)} %get-tuple-element.12), channel_id=1, source_target_pairs={{4,8},{8,4},{5,9},{9,5},{6,10},{10,6},{7,11},{11,7},{20,24},{24,20... | collective-permute-start | bytes 393224 | tf_op jit(solution)/shard_map/ppermute | solution.py:228
  21.8 3.6 %collective-permute-done.3.far_ref = bf16[256,256]{1,0:T(8,128)(2,1)S(1)} collective-permute-done((bf16[256,256]{1,0:T(8,128)(2,1)S(1)}, bf16[256,256]{1,0:T(8,128)(2,1)S(1)}, u32[]{:S(2)}, u32[]{:S(2)}) %collective-permute-start.3) | collective-permute-done | bytes 131104 | tf_op jit(solution)/shard_map/ppermute | solution.py:228
  25.3 0.0 collective-permute-done.4.up_b_ref
  25.3 0.0 collective-permute-done.5.down_b_ref
  25.4 0.0 copy-start.3
  25.4 1.2 %copy-done.3 = bf16[1,1024,512]{2,1,0:T(8,128)(2,1)S(1)} copy-done((bf16[1,1024,512]{2,1,0:T(8,128)(2,1)S(1)}, bf16[1,1024,512]{2,1,0:T(8,128)(2,1)}, u32[]{:S(2)}) %copy-start.3) | copy-done | bytes 1048600
  26.6 4.1 %mixer.1.own_ref = bf16[2048,128]{1,0:T(8,128)(2,1)S(1)} custom-call(bf16[2,256,256]{2,1,0:T(8,128)(2,1)S(1)} %get-tuple-element.9.normed_ref, bf16[256,256]{1,0:T(8,128)(2,1)S(1)} %get-tuple-element.10.features_ref, bf16[256,256]{1,0:T(8,128)(2,1)S(1)} %collective-permute-done.2.near_ref, bf16[256,256]{1,0:T(8,128)(2,1)S(1)} %collective-permute-done.3.far_ref, ...), custom_call_target="tpu_custom_call" | custom-call | tf_op jit(solution)/shard_map/mixer/pallas_call | solution.py:231
  30.7 3.6 %collective-permute-start.6 = (bf16[2048,128]{1,0:T(8,128)(2,1)S(1)}, bf16[2048,128]{1,0:T(8,128)(2,1)S(1)}, u32[]{:S(2)}, u32[]{:S(2)}) collective-permute-start(bf16[2048,128]{1,0:T(8,128)(2,1)S(1)} %mixer.1.own_ref), channel_id=1, source_target_pairs={{0,1},{1,0},{2,3},{3,2},{4,5},{5,4},{6,7},{7,6},{8,9},{9,8},{10,11... | collective-permute-start | bytes 1572872 | tf_op jit(solution)/shard_map/ppermute | solution.py:251
  34.3 1.5 %collective-permute-done.6.other_ref = bf16[2048,128]{1,0:T(8,128)(2,1)S(1)} collective-permute-done((bf16[2048,128]{1,0:T(8,128)(2,1)S(1)}, bf16[2048,128]{1,0:T(8,128)(2,1)S(1)}, u32[]{:S(2)}, u32[]{:S(2)}) %collective-permute-start.6) | collective-permute-done | bytes 524320 | tf_op jit(solution)/shard_map/ppermute | solution.py:251
  35.8 1.0 %merge.1 = bf16[4096,128]{1,0:T(8,128)(2,1)} custom-call(bf16[2048,128]{1,0:T(8,128)(2,1)S(1)} %mixer.1.own_ref, bf16[2048,128]{1,0:T(8,128)(2,1)S(1)} %collective-permute-done.6.other_ref), custom_call_target="tpu_custom_call" | custom-call | tf_op jit(solution)/shard_map/merge/pallas_call | solution.py:252
  (11 shorter events, 0.0 us)
Async XLA Ops:
  0.0 25.3 %collective-permute-start.4 = (bf16[1,512,1024]{2,1,0:T(8,128)(2,1)}, bf16[1,512,1024]{2,1,0:T(8,128)(2,1)S(1)}, u32[]{:S(2)}, u32[]{:S(2)}) collective-permute-start(bf16[1,512,1024]{2,1,0:T(8,128)(2,1)} %up_a_ref.1), channel_id=1, source_target_pairs={{0,1},{1,0},{2,3},{3,2},{4,5},{5,4},{6,7},{7,6},{8,9},{9,8},{10,11... | collective-permute-start | bytes 3145736 | tf_op jit(solution)/shard_map/ppermute | solution.py:186
  0.7 24.7 %collective-permute-start.5 = (bf16[1,1024,512]{2,1,0:T(8,128)(2,1)}, bf16[1,1024,512]{2,1,0:T(8,128)(2,1)S(1)}, u32[]{:S(2)}, u32[]{:S(2)}) collective-permute-start(bf16[1,1024,512]{2,1,0:T(8,128)(2,1)} %down_a_ref.1), channel_id=1, source_target_pairs={{0,1},{1,0},{2,3},{3,2},{4,5},{5,4},{6,7},{7,6},{8,9},{9,8},{10,11... | collective-permute-start | bytes 3145736 | tf_op jit(solution)/shard_map/ppermute | solution.py:187
  0.7 1.2 %copy-start = (bf16[2,1024,256]{2,1,0:T(8,128)(2,1)S(1)}, bf16[2,1024,256]{2,1,0:T(8,128)(2,1)}, u32[]{:S(2)}) copy-start(bf16[2,1024,256]{2,1,0:T(8,128)(2,1)} %frames_ref.3) | copy-start | bytes 3145732
  1.9 0.7 %copy-start.6 = (s32[2,512]{1,0:T(2,128)S(1)}, s32[2,512]{1,0:T(2,128)}, u32[]{:S(2)}) copy-start(s32[2,512]{1,0:T(2,128)} %pixel_ref.1) | copy-start | bytes 12292
  2.6 0.7 %copy-start.7 = (s32[512]{0:T(512)S(1)}, s32[512]{0:T(512)}, u32[]{:S(2)}) copy-start(s32[512]{0:T(512)} %param.8) | copy-start | bytes 6148
  3.3 10.6 %copy-start.1 = (bf16[2,1024,256]{2,1,0:T(8,128)(2,1)S(1)}, bf16[2,1024,256]{2,1,0:T(8,128)(2,1)}, u32[]{:S(2)}) copy-start(bf16[2,1024,256]{2,1,0:T(8,128)(2,1)} %frames_ref.3) | copy-start | bytes 3145732
  4.0 21.4 %copy-start.2 = (bf16[1,512,1024]{2,1,0:T(8,128)(2,1)S(1)}, bf16[1,512,1024]{2,1,0:T(8,128)(2,1)}, u32[]{:S(2)}) copy-start(bf16[1,512,1024]{2,1,0:T(8,128)(2,1)} %up_a_ref.1) | copy-start | bytes 3145732
  4.0 4.6 %collective-permute-start = (bf16[256,256]{1,0:T(8,128)(2,1)S(1)}, bf16[256,256]{1,0:T(8,128)(2,1)S(1)}, u32[]{:S(2)}, u32[]{:S(2)}) collective-permute-start(bf16[256,256]{1,0:T(8,128)(2,1)S(1)} %pick.1.a_ref), channel_id=1, source_target_pairs={{0,4},{4,0},{8,12},{12,8},{1,5},{5,1},{9,13},{13,9},{2,6},{6,2},{1... | collective-permute-start | bytes 393224 | tf_op jit(solution)/shard_map/ppermute | solution.py:210
  8.6 16.7 %copy-start.4 = (bf16[512,512]{1,0:T(8,128)(2,1)S(1)}, bf16[512,512]{1,0:T(8,128)(2,1)}, u32[]{:S(2)}) copy-start(bf16[512,512]{1,0:T(8,128)(2,1)} %in_ref.1) | copy-start | bytes 1572868
  8.6 5.2 %collective-permute-start.1 = (bf16[256,256]{1,0:T(8,128)(2,1)S(1)}, bf16[256,256]{1,0:T(8,128)(2,1)S(1)}, u32[]{:S(2)}, u32[]{:S(2)}) collective-permute-start(bf16[256,256]{1,0:T(8,128)(2,1)S(1)} %join.1.a_ref), channel_id=1, source_target_pairs={{0,12},{4,8},{8,4},{12,0},{1,13},{5,9},{9,5},{13,1},{2,14},{6,10},... | collective-permute-start | bytes 393224 | tf_op jit(solution)/shard_map/ppermute | solution.py:210
  17.4 8.0 %copy-start.5 = (f32[1,3,512]{2,0,1:T(1,128)S(1)}, f32[1,3,512]{2,0,1:T(1,128)}, u32[]{:S(2)}) copy-start(f32[1,3,512]{2,0,1:T(1,128)} %param.11) | copy-start | bytes 18436
  17.4 4.3 %collective-permute-start.2 = (bf16[256,256]{1,0:T(8,128)(2,1)S(1)}, bf16[256,256]{1,0:T(8,128)(2,1)S(1)}, u32[]{:S(2)}, u32[]{:S(2)}) collective-permute-start(bf16[256,256]{1,0:T(8,128)(2,1)S(1)} %get-tuple-element.11), channel_id=1, source_target_pairs={{0,4},{4,0},{8,12},{12,8},{1,5},{5,1},{9,13},{13,9},{2,6},{6,2},{1... | collective-permute-start | bytes 393224 | tf_op jit(solution)/shard_map/ppermute | solution.py:226
  19.3 6.0 %collective-permute-start.3 = (bf16[256,256]{1,0:T(8,128)(2,1)S(1)}, bf16[256,256]{1,0:T(8,128)(2,1)S(1)}, u32[]{:S(2)}, u32[]{:S(2)}) collective-permute-start(bf16[256,256]{1,0:T(8,128)(2,1)S(1)} %get-tuple-element.12), channel_id=1, source_target_pairs={{4,8},{8,4},{5,9},{9,5},{6,10},{10,6},{7,11},{11,7},{20,24},{24,20... | collective-permute-start | bytes 393224 | tf_op jit(solution)/shard_map/ppermute | solution.py:228
  25.4 1.2 %copy-start.3 = (bf16[1,1024,512]{2,1,0:T(8,128)(2,1)S(1)}, bf16[1,1024,512]{2,1,0:T(8,128)(2,1)}, u32[]{:S(2)}) copy-start(bf16[1,1024,512]{2,1,0:T(8,128)(2,1)} %down_a_ref.1) | copy-start | bytes 3145732
  30.7 5.2 %collective-permute-start.6 = (bf16[2048,128]{1,0:T(8,128)(2,1)S(1)}, bf16[2048,128]{1,0:T(8,128)(2,1)S(1)}, u32[]{:S(2)}, u32[]{:S(2)}) collective-permute-start(bf16[2048,128]{1,0:T(8,128)(2,1)S(1)} %mixer.1.own_ref), channel_id=1, source_target_pairs={{0,1},{1,0},{2,3},{3,2},{4,5},{5,4},{6,7},{7,6},{8,9},{9,8},{10,11... | collective-permute-start | bytes 1572872 | tf_op jit(solution)/shard_map/ppermute | solution.py:251

commit v3 on v2

v3 whole, which is shorter than its diff:
```python
import functools
import math

import jax
import jax.numpy as jnp
from jax import lax
from jax.experimental import pallas as pl
from jax.experimental.pallas import tpu as pltpu
from jax.sharding import PartitionSpec as P

LANES = 128
ROOM = 20 * 1024 * 1024
BF16 = jnp.bfloat16
F32 = jnp.float32
VMEM = pl.BlockSpec(memory_space=pltpu.VMEM)
HBM = pl.BlockSpec(memory_space=pltpu.HBM)


def held(value):
    return pltpu.with_memory_space_constraint(value, pltpu.VMEM)


def fixed(value):
    return pltpu.with_memory_space_constraint(value, pltpu.HBM)


def kept(shape, dtype):
    return pltpu.VMEM(shape, dtype)


def call(body, name, out, count, scratch=(), in_specs=None, out_specs=None):
    many = isinstance(out, tuple)
    if out_specs is None:
        out_specs = (VMEM,) * len(out) if many else VMEM
    return pl.pallas_call(
        body,
        out_shape=out,
        in_specs=[VMEM] * count if in_specs is None else in_specs,
        out_specs=out_specs,
        scratch_shapes=list(scratch),
        compiler_params=pltpu.CompilerParams(vmem_limit_bytes=ROOM),
        name=name,
    )


def dot(a, b):
    return jnp.dot(a, b, preferred_element_type=F32)


def dot_t(a, b):
    return lax.dot_general(a, b, (((1,), (1,)), ((), ())), preferred_element_type=F32)


def my_part(whole, part, parts):
    size = whole.shape[-1] // parts
    mine = whole[:, :size]
    for at in range(1, parts):
        mine = jnp.where(part == at, whole[:, at * size : (at + 1) * size], mine)
    return mine


def is_even():
    return lax.rem(lax.axis_index("frame"), 2) == 0


def near_frame():
    return 1 - lax.rem(lax.axis_index("frame"), 2)


def inverse_rms(values, epsilon):
    return lax.rsqrt(jnp.mean(values * values, axis=-1, keepdims=True) + epsilon)


def level_of(stream):
    return (stream * inverse_rms(stream, 1e-5)).astype(BF16).astype(F32)


def pick_body(parts, frame_hbm, pixel_hbm, frames_hbm, out_ref, frame_ref, pixel_ref, frames_ref, sems):
    frame_count, pixel_count, _ = frames_ref.shape
    loads = [
        pltpu.make_async_copy(frame_hbm, frame_ref, sems.at[0]),
        pltpu.make_async_copy(pixel_hbm, pixel_ref, sems.at[1]),
    ]
    maps = [
        pltpu.make_async_copy(frames_hbm.at[t], frames_ref.at[t], sems.at[2 + t])
        for t in range(frame_count)
    ]
    for copy in loads + maps:
        copy.start()
    for copy in loads:
        copy.wait()
    part = lax.axis_index("split")
    first = lax.axis_index("frame") * frame_count
    side = math.isqrt(pixel_count)
    pixel = pixel_ref[...]
    local = my_part(frame_ref[...], part, parts) - first
    row = my_part(pixel[0:1], part, parts)
    col = my_part(pixel[1:2], part, parts)
    owned = (local >= 0) & (local < frame_count)
    place = jnp.where(owned, local * pixel_count + row * side + col, -1)
    count = place.shape[1]
    place = jnp.transpose(jnp.broadcast_to(place, (8, count)))[:, :1]
    chunk = min(512, pixel_count)
    order = lax.broadcasted_iota(jnp.int32, (count, chunk), 1)
    total = None
    for t in range(frame_count):
        maps[t].wait()
        for at in range(0, pixel_count, chunk):
            start = t * pixel_count + at
            hot = jnp.where(order == place - start, 1.0, 0.0).astype(BF16)
            part_sum = dot(hot, frames_ref[t, at : at + chunk, :])
            total = part_sum if total is None else total + part_sum
    out_ref[...] = total.astype(BF16)


def join_body(a_ref, b_ref, out_ref):
    out_ref[...] = a_ref[...] + b_ref[...]


def attend(features, frames_ref, t, scale, score_ref, weight_ref, sum_ref):
    rows = features.shape[0]
    pixel_count = frames_ref.shape[1]
    chunk = min(256, pixel_count)
    step = 32
    for at in range(0, pixel_count, chunk):
        score_ref[:, at : at + chunk] = dot_t(features, frames_ref[t, at : at + chunk, :])
    for at in range(0, rows, step):
        scores = score_ref[at : at + step, :]
        peak = jnp.max(scores, axis=-1, keepdims=True)
        expd = jnp.exp2((scores - peak) * scale)
        total = jnp.sum(expd, axis=-1, keepdims=True)
        sum_ref[at : at + step, :] = jnp.broadcast_to(total, (step, LANES))
        weight_ref[at : at + step, :] = expd.astype(BF16)
    pooled = dot(weight_ref[...], frames_ref[t])
    total = sum_ref[:, :1]
    mean = jnp.mean(pooled * pooled, axis=-1, keepdims=True)
    return (pooled * lax.rsqrt(mean + 1e-6 * total * total)).astype(BF16)


def near_body(scale, a_ref, b_ref, frames_ref, features_ref, normed_ref, *scratch):
    features = a_ref[...] + b_ref[...]
    features_ref[...] = features
    normed_ref[...] = attend(features, frames_ref, near_frame(), scale, *scratch)


def far_body(scale, features_ref, frames_ref, normed_ref, *scratch):
    normed_ref[...] = attend(features_ref[...], frames_ref, 1 - near_frame(), scale, *scratch)


def taps_of(taps_ref):
    width = taps_ref.shape[1] // 3
    first, middle, last = (taps_ref[:, k * width : (k + 1) * width] for k in range(3))
    even = is_even()
    return jnp.where(even, last, first), middle, jnp.where(even, first, last)


def own_body(features_ref, near_ref, far_ref, in_ref, taps_ref, base_ref, near_out, far_out):
    channels = features_ref.shape[1]
    near_tap, middle, far_tap = taps_of(taps_ref)
    base = dot(features_ref[...], in_ref[channels:, :])
    base_ref[...] = base
    near = dot(near_ref[...], in_ref[:channels, :]) + base
    far = dot(far_ref[...], in_ref[:channels, :]) + base
    near_level, far_level = level_of(near), level_of(far)
    near_out[...] = near + middle * near_level + far_tap * far_level
    far_out[...] = far + middle * far_level + near_tap * near_level


def mix(stream, ups, downs, hidden_ref):
    gated = (stream * inverse_rms(stream, 1e-5)).astype(BF16)
    base = 0
    total = None
    for up_ref, down_ref in zip(ups, downs):
        units = up_ref.shape[2]
        step = min(256, units)
        for at in range(0, units, step):
            x = dot(gated, up_ref[0, :, at : at + step])
            inner = x * (x * x * (0.044715 * math.sqrt(2 / math.pi)) + math.sqrt(2 / math.pi))
            hidden_ref[:, base + at : base + at + step] = (x + x * jnp.tanh(inner)).astype(BF16)
        base += units
    base = 0
    for up_ref, down_ref in zip(ups, downs):
        units = up_ref.shape[2]
        part = dot(hidden_ref[:, base : base + units], down_ref[0])
        total = part if total is None else total + part
        base += units
    return stream + 0.5 * total


def mixed_stream(halo_ref, own_ref, base_ref, in_ref, tap, inside):
    channels = halo_ref.shape[1]
    halo = level_of(dot(halo_ref[...], in_ref[:channels, :]) + base_ref[...])
    return own_ref[...] + jnp.where(inside, tap, 0.0) * halo


def mix_near_body(
    devices, halo_ref, own_ref, base_ref, in_ref, taps_ref, up_a, up_b, down_a, down_b, out_ref, hidden_ref
):
    place = lax.axis_index("frame")
    inside = jnp.logical_not(is_even()) | (place < devices - 1)
    tap, _, _ = taps_of(taps_ref)
    stream = mixed_stream(halo_ref, own_ref, base_ref, in_ref, tap, inside)
    out_ref[...] = mix(stream, (up_a, up_b), (down_a, down_b), hidden_ref)


def mix_far_body(
    devices,
    halo_ref,
    own_ref,
    base_ref,
    in_ref,
    taps_ref,
    up_a,
    up_b,
    down_a,
    down_b,
    near_ref,
    out_ref,
    hidden_ref,
    line_ref,
):
    place = lax.axis_index("frame")
    even = is_even()
    inside = jnp.where(even, place > 0, place < devices - 1)
    _, _, tap = taps_of(taps_ref)
    stream = mixed_stream(halo_ref, own_ref, base_ref, in_ref, tap, inside)
    far = mix(stream, (up_a, up_b), (down_a, down_b), hidden_ref)
    near = near_ref[...]
    rows, width = far.shape
    blocks = width // LANES
    for t, value in ((0, jnp.where(even, far, near)), (1, jnp.where(even, near, far))):
        for b in range(blocks):
            line_ref[pl.ds(b * 2 + t, rows, stride=blocks * 2), :] = value[
                :, b * LANES : (b + 1) * LANES
            ]
    out_ref[...] = line_ref[...].astype(BF16)


def merge_body(own_ref, other_ref, out_ref, sems):
    rows = own_ref.shape[0]
    part = lax.axis_index("split")
    own = pltpu.make_async_copy(own_ref, out_ref.at[pl.ds(part * rows, rows)], sems.at[0])
    other = pltpu.make_async_copy(
        other_ref, out_ref.at[pl.ds((1 - part) * rows, rows)], sems.at[1]
    )
    own.start()
    other.start()
    own.wait()
    other.wait()


def on_device(frames, query_frame, query_pixel, in_weight, conv_weight, up_weight, down_weight):
    frame_count, pixel_count, channels = frames.shape
    query_count = query_frame.shape[0]
    width = in_weight.shape[1]
    units = up_weight.shape[2]
    parts = lax.axis_size("split")
    devices = lax.axis_size("frame")
    assert parts == 2 and frame_count == 2 and devices > 1 and devices & (devices - 1) == 0
    rows = query_count // parts
    swap = [(0, 1), (1, 0)]
    flips = lambda mask: [(i, i ^ mask) for i in range(devices)]
    up_other = held(lax.ppermute(up_weight, "split", swap))
    down_other = held(lax.ppermute(down_weight, "split", swap))
    mine = call(
        functools.partial(pick_body, parts),
        "pick",
        kept((rows, channels), BF16),
        3,
        scratch=(
            pltpu.VMEM((1, query_count), jnp.int32),
            pltpu.VMEM(query_pixel.shape, jnp.int32),
            pltpu.VMEM(frames.shape, BF16),
            pltpu.SemaphoreType.DMA((2 + frame_count,)),
        ),
        in_specs=[HBM] * 3,
    )(*(fixed(x) for x in (query_frame.reshape(1, query_count), query_pixel, frames)))
    theirs = held(lax.ppermute(mine, "frame", flips(1)))
    stage = 2
    while stage < devices:
        mine = call(join_body, "join", kept((rows, channels), BF16), 2)(mine, theirs)
        theirs = held(lax.ppermute(mine, "frame", flips(2 * stage - 1)))
        stage *= 2
    frames = held(frames)
    in_weight = held(in_weight)
    taps = held(conv_weight.reshape(1, conv_weight.shape[1] * width))
    weights = (held(up_weight), up_other, held(down_weight), down_other)
    scale = math.log2(math.e) / math.sqrt(channels)
    attention_scratch = (
        pltpu.VMEM((rows, pixel_count), F32),
        pltpu.VMEM((rows, pixel_count), BF16),
        pltpu.VMEM((rows, LANES), F32),
    )
    small = kept((rows, channels), BF16)
    wide = kept((rows, width), F32)
    features, near = call(
        functools.partial(near_body, scale), "near", (small, small), 3, attention_scratch
    )(mine, theirs, frames)
    near_halo = held(lax.ppermute(near, "frame", flips(1)))
    far = call(functools.partial(far_body, scale), "far", small, 2, attention_scratch)(
        features, frames
    )
    pairs = [(i, i + 1) for i in range(1, devices - 1, 2)]
    far_halo = held(lax.ppermute(far, "frame", pairs + [(b, a) for a, b in pairs]))
    base, own_near, own_far = call(own_body, "own", (wide,) * 3, 5)(
        features, near, far, in_weight, taps
    )
    hidden = pltpu.VMEM((rows, parts * units), BF16)
    near = call(functools.partial(mix_near_body, devices), "mix_near", wide, 9, (hidden,))(
        near_halo, own_near, base, in_weight, taps, *weights
    )
    blocks = width // LANES
    lines = rows * blocks * frame_count
    own = call(
        functools.partial(mix_far_body, devices),
        "mix_far",
        kept((lines, LANES), BF16),
        10,
        (hidden, pltpu.VMEM((lines, LANES), F32)),
    )(far_halo, own_far, base, in_weight, taps, *weights, near)
    other = held(lax.ppermute(own, "split", swap))
    both = call(
        merge_body,
        "merge",
        jax.ShapeDtypeStruct((parts * lines, LANES), BF16),
        2,
        (pltpu.SemaphoreType.DMA((2,)),),
        out_specs=HBM,
    )(own, other)
    both = both.reshape(query_count, blocks, frame_count, LANES)
    return both.transpose(0, 2, 1, 3).reshape(query_count, frame_count, width)


def solution(mesh):
    return jax.shard_map(
        on_device,
        mesh=mesh,
        in_specs=(
            P(("dom", "frame"), None, None),
            P(("dom", "query")),
            P(None, ("dom", "query")),
            P(),
            P(),
            P(None, None, "split"),
            P(None, "split", None),
        ),
        out_specs=P(("dom", "query"), "frame", None),
        check_vma=False,
    )
```

time: 37.1 us -> 31 us (0.84)
  local copies, waits for them, and re-layouts: 3.83 us -> 0.02 us
  waiting for transfers between devices: 13.3 us -> 10.7 us
    unnamed x16 -> x10, local copies, waits for them, and re-layouts: 3.83 us -> 0.02 us
    ppermute x4, waiting for transfers between devices: 11.8 us -> 9.17 us  [the longest x1 5.12 us: on_device(): theirs = held(lax.ppermute(mine, 'frame', flips(2 * stage - 1)))]
    pallas_call x5 -> x8, Pallas kernels: 9.31 us -> 9.57 us  [the longest x1 2.03 us: on_device(): call(functools.partial(pick_body, parts), 'pick', kept((rows, channels),...]
  transfers between devices with their start and end apart: 7 -> 7, of which waited for: 4 -> 4; matrix products, arithmetic and copies ran while one was open for 0% -> 0% of each run, Pallas kernels for 12% -> 22%
where the time goes in v3:
time: 31 us; the launch traced here: 30.8 us
  waiting for transfers between devices  10.7 us (35%)
  starting transfers between devices  10.4 us (34%)
  Pallas kernels  9.57 us (31%)
    ppermute x1, waiting for transfers between devices, on_device(): theirs = held(lax.ppermute(mine, 'frame', flips(2 * stage - 1)))  5.12 us
    ppermute x1, starting transfers between devices, on_device(): other = held(lax.ppermute(own, 'split', swap))  3.85 us
    ppermute x1, waiting for transfers between devices, on_device(): theirs = held(lax.ppermute(mine, 'frame', flips(1)))  3.31 us
    ppermute x1, starting transfers between devices, on_device(): lax.ppermute(far, 'frame', pairs + [(b, a) for a, b in pairs])  2.43 us
    pallas_call x1, Pallas kernels, on_device(): call(functools.partial(pick_body, parts), 'pick', kept((rows, channels),...  2.03 us
    pallas_call x1, Pallas kernels, on_device(): call(functools.partial(mix_far_body, devices), 'mix_far', kept((lines, LA...  1.95 us
    pallas_call x1, Pallas kernels, on_device(): call(functools.partial(mix_near_body, devices), 'mix_near', wide, 9, (hid...  1.81 us
    ppermute x1, starting transfers between devices, on_device(): near_halo = held(lax.ppermute(near, 'frame', flips(1)))  1.79 us
  transfers between devices with their start and end apart: 7, of which 4 were waited for; matrix products, arithmetic and copies ran while one was open for 0% of the time, Pallas kernels for 22%

profile of v3, /device:TPU:17, one launch (start us, length us, event | category | flops | bytes accessed | tf_op | source)
XLA Modules:
  0.0 30.8 jit_solution(4249047575123930525)
XLA Ops:
  0.0 0.7 %collective-permute-start.3 = (bf16[1,512,1024]{2,1,0:T(8,128)(2,1)}, bf16[1,512,1024]{2,1,0:T(8,128)(2,1)S(1)}, u32[]{:S(2)}, u32[]{:S(2)}) collective-permute-start(bf16[1,512,1024]{2,1,0:T(8,128)(2,1)} %up_a.3), channel_id=1, source_target_pairs={{0,1},{1,0},{2,3},{3,2},{4,5},{5,4},{6,7},{7,6},{8,9},{9,8},{10,11... | collective-permute-start | bytes 3145736 | tf_op jit(solution)/shard_map/ppermute | solution.py:263
  0.7 0.1 collective-permute-start.4
  0.7 2.0 %pick.1.a_ref = bf16[256,256]{1,0:T(8,128)(2,1)S(1)} custom-call(s32[1,512]{1,0:T(1,128)} %bitcast.10, s32[2,512]{1,0:T(2,128)} %pixel_hbm.1, bf16[2,1024,256]{2,1,0:T(8,128)(2,1)} %frames_ref.3), custom_call_target="tpu_custom_call" | custom-call | tf_op jit(solution)/shard_map/pick/pallas_call | solution.py:265
  2.8 1.4 %collective-permute-start = (bf16[256,256]{1,0:T(8,128)(2,1)S(1)}, bf16[256,256]{1,0:T(8,128)(2,1)S(1)}, u32[]{:S(2)}, u32[]{:S(2)}) collective-permute-start(bf16[256,256]{1,0:T(8,128)(2,1)S(1)} %pick.1.a_ref), channel_id=1, source_target_pairs={{0,4},{4,0},{8,12},{12,8},{1,5},{5,1},{9,13},{13,9},{2,6},{6,2},{1... | collective-permute-start | bytes 393224 | tf_op jit(solution)/shard_map/ppermute | solution.py:278
  4.1 3.3 %collective-permute-done.b_ref = bf16[256,256]{1,0:T(8,128)(2,1)S(1)} collective-permute-done((bf16[256,256]{1,0:T(8,128)(2,1)S(1)}, bf16[256,256]{1,0:T(8,128)(2,1)S(1)}, u32[]{:S(2)}, u32[]{:S(2)}) %collective-permute-start) | collective-permute-done | bytes 131104 | tf_op jit(solution)/shard_map/ppermute | solution.py:278
  7.5 0.2 collective-permute-start.1
  7.7 5.1 %collective-permute-done.1.b_ref = bf16[256,256]{1,0:T(8,128)(2,1)S(1)} collective-permute-done((bf16[256,256]{1,0:T(8,128)(2,1)S(1)}, bf16[256,256]{1,0:T(8,128)(2,1)S(1)}, u32[]{:S(2)}, u32[]{:S(2)}) %collective-permute-start.1) | collective-permute-done | bytes 131104 | tf_op jit(solution)/shard_map/ppermute | solution.py:282
  12.8 0.0 copy-done
  12.8 1.1 %near.1 = (bf16[256,256]{1,0:T(8,128)(2,1)S(1)}, bf16[256,256]{1,0:T(8,128)(2,1)S(1)}) custom-call(bf16[256,256]{1,0:T(8,128)(2,1)S(1)} %join.1.a_ref, bf16[256,256]{1,0:T(8,128)(2,1)S(1)} %collective-permute-done.1.b_ref, bf16[2,1024,256]{2,1,0:T(8,128)(2,1)S(1)} %copy-done), custom_call_target="tpu_custom_call" | custom-call | tf_op jit(solution)/shard_map/near/pallas_call | solution.py:296
  13.9 1.8 %collective-permute-start.5 = (bf16[256,256]{1,0:T(8,128)(2,1)S(1)}, bf16[256,256]{1,0:T(8,128)(2,1)S(1)}, u32[]{:S(2)}, u32[]{:S(2)}) collective-permute-start(bf16[256,256]{1,0:T(8,128)(2,1)S(1)} %get-tuple-element.11.near_ref), channel_id=1, source_target_pairs={{0,4},{4,0},{8,12},{12,8},{1,5},{5,1},{9,13},{13,9},{2,6},{6,2},{1... | collective-permute-start | bytes 393224 | tf_op jit(solution)/shard_map/ppermute | solution.py:299
  15.7 1.1 %far.1.far_ref = bf16[256,256]{1,0:T(8,128)(2,1)S(1)} custom-call(bf16[256,256]{1,0:T(8,128)(2,1)S(1)} %get-tuple-element.10.features_ref, bf16[2,1024,256]{2,1,0:T(8,128)(2,1)S(1)} %copy-done), custom_call_target="tpu_custom_call" | custom-call | tf_op jit(solution)/shard_map/far/pallas_call | solution.py:300
  16.8 2.4 %collective-permute-start.2 = (bf16[256,256]{1,0:T(8,128)(2,1)S(1)}, bf16[256,256]{1,0:T(8,128)(2,1)S(1)}, u32[]{:S(2)}, u32[]{:S(2)}) collective-permute-start(bf16[256,256]{1,0:T(8,128)(2,1)S(1)} %far.1.far_ref), channel_id=1, source_target_pairs={{4,8},{8,4},{5,9},{9,5},{6,10},{10,6},{7,11},{11,7},{20,24},{24,20... | collective-permute-start | bytes 393224 | tf_op jit(solution)/shard_map/ppermute | solution.py:304
  19.2 0.0 copy-done.4
  19.2 0.0 copy-done.1
  19.2 0.6 %own.1 = (f32[256,512]{1,0:T(8,128)S(1)}, f32[256,512]{1,0:T(8,128)S(1)}, f32[256,512]{1,0:T(8,128)S(1)}) custom-call(bf16[256,256]{1,0:T(8,128)(2,1)S(1)} %get-tuple-element.10.features_ref, bf16[256,256]{1,0:T(8,128)(2,1)S(1)} %get-tuple-element.11.near_ref, bf16[256,256]{1,0:T(8,128)(2,1)S(1)} %far.1.far_ref, bf16[512,512]{1,0:T(8,128)(2,1)S(1)} %copy-done.1, ...), custom_call_target="tpu_custom_call" | custom-call | tf_op jit(solution)/shard_map/own/pallas_call | solution.py:305
  19.9 0.0 collective-permute-done.5.halo_ref
  19.9 0.0 collective-permute-done.3.up_b
  19.9 0.0 collective-permute-done.4.down_b
  19.9 1.8 %mix_near.1.near_ref = f32[256,512]{1,0:T(8,128)S(1)} custom-call(bf16[256,256]{1,0:T(8,128)(2,1)S(1)} %collective-permute-done.5.halo_ref, f32[256,512]{1,0:T(8,128)S(1)} %get-tuple-element.14.own_ref, f32[256,512]{1,0:T(8,128)S(1)} %get-tuple-element.13.base_ref, bf16[512,512]{1,0:T(8,128)(2,1)S(1)} %copy-done.1, f32[1,1536]{1,0:T(1,128)S(1)} %bitcast.8, ...), custom_call_target="tpu_custom_call" | custom-call | tf_op jit(solution)/shard_map/mix_near/pallas_call | solution.py:309
  21.8 0.7 %collective-permute-done.2.halo_ref = bf16[256,256]{1,0:T(8,128)(2,1)S(1)} collective-permute-done((bf16[256,256]{1,0:T(8,128)(2,1)S(1)}, bf16[256,256]{1,0:T(8,128)(2,1)S(1)}, u32[]{:S(2)}, u32[]{:S(2)}) %collective-permute-start.2) | collective-permute-done | bytes 131104 | tf_op jit(solution)/shard_map/ppermute | solution.py:304
  22.5 2.0 %mix_far.1.own_ref = bf16[2048,128]{1,0:T(8,128)(2,1)S(1)} custom-call(bf16[256,256]{1,0:T(8,128)(2,1)S(1)} %collective-permute-done.2.halo_ref, f32[256,512]{1,0:T(8,128)S(1)} %get-tuple-element.12.own_ref, f32[256,512]{1,0:T(8,128)S(1)} %get-tuple-element.13.base_ref, bf16[512,512]{1,0:T(8,128)(2,1)S(1)} %copy-done.1, f32[1,1536]{1,0:T(1,128)S(1)} %bitcast.9, ...), custom_call_target="tpu_custom_call" | custom-call | tf_op jit(solution)/shard_map/mix_far/pallas_call | solution.py:314
  24.5 3.9 %collective-permute-start.6 = (bf16[2048,128]{1,0:T(8,128)(2,1)S(1)}, bf16[2048,128]{1,0:T(8,128)(2,1)S(1)}, u32[]{:S(2)}, u32[]{:S(2)}) collective-permute-start(bf16[2048,128]{1,0:T(8,128)(2,1)S(1)} %mix_far.1.own_ref), channel_id=1, source_target_pairs={{0,1},{1,0},{2,3},{3,2},{4,5},{5,4},{6,7},{7,6},{8,9},{9,8},{10,11... | collective-permute-start | bytes 1572872 | tf_op jit(solution)/shard_map/ppermute | solution.py:321
  28.3 1.5 %collective-permute-done.6.other_ref = bf16[2048,128]{1,0:T(8,128)(2,1)S(1)} collective-permute-done((bf16[2048,128]{1,0:T(8,128)(2,1)S(1)}, bf16[2048,128]{1,0:T(8,128)(2,1)S(1)}, u32[]{:S(2)}, u32[]{:S(2)}) %collective-permute-start.6) | collective-permute-done | bytes 524320 | tf_op jit(solution)/shard_map/ppermute | solution.py:321
  29.8 1.0 %merge.1 = bf16[4096,128]{1,0:T(8,128)(2,1)} custom-call(bf16[2048,128]{1,0:T(8,128)(2,1)S(1)} %mix_far.1.own_ref, bf16[2048,128]{1,0:T(8,128)(2,1)S(1)} %collective-permute-done.6.other_ref), custom_call_target="tpu_custom_call" | custom-call | tf_op jit(solution)/shard_map/merge/pallas_call | solution.py:322
  (8 shorter events, 0.0 us)
Async XLA Ops:
  0.0 12.8 %copy-start = (bf16[2,1024,256]{2,1,0:T(8,128)(2,1)S(1)}, bf16[2,1024,256]{2,1,0:T(8,128)(2,1)}, u32[]{:S(2)}) copy-start(bf16[2,1024,256]{2,1,0:T(8,128)(2,1)} %frames_ref.3) | copy-start | bytes 3145732
  0.0 19.9 %collective-permute-start.3 = (bf16[1,512,1024]{2,1,0:T(8,128)(2,1)}, bf16[1,512,1024]{2,1,0:T(8,128)(2,1)S(1)}, u32[]{:S(2)}, u32[]{:S(2)}) collective-permute-start(bf16[1,512,1024]{2,1,0:T(8,128)(2,1)} %up_a.3), channel_id=1, source_target_pairs={{0,1},{1,0},{2,3},{3,2},{4,5},{5,4},{6,7},{7,6},{8,9},{9,8},{10,11... | collective-permute-start | bytes 3145736 | tf_op jit(solution)/shard_map/ppermute | solution.py:263
  0.7 19.2 %collective-permute-start.4 = (bf16[1,1024,512]{2,1,0:T(8,128)(2,1)}, bf16[1,1024,512]{2,1,0:T(8,128)(2,1)S(1)}, u32[]{:S(2)}, u32[]{:S(2)}) collective-permute-start(bf16[1,1024,512]{2,1,0:T(8,128)(2,1)} %down_a.3), channel_id=1, source_target_pairs={{0,1},{1,0},{2,3},{3,2},{4,5},{5,4},{6,7},{7,6},{8,9},{9,8},{10,11... | collective-permute-start | bytes 3145736 | tf_op jit(solution)/shard_map/ppermute | solution.py:264
  2.8 4.7 %collective-permute-start = (bf16[256,256]{1,0:T(8,128)(2,1)S(1)}, bf16[256,256]{1,0:T(8,128)(2,1)S(1)}, u32[]{:S(2)}, u32[]{:S(2)}) collective-permute-start(bf16[256,256]{1,0:T(8,128)(2,1)S(1)} %pick.1.a_ref), channel_id=1, source_target_pairs={{0,4},{4,0},{8,12},{12,8},{1,5},{5,1},{9,13},{13,9},{2,6},{6,2},{1... | collective-permute-start | bytes 393224 | tf_op jit(solution)/shard_map/ppermute | solution.py:278
  7.5 5.4 %collective-permute-start.1 = (bf16[256,256]{1,0:T(8,128)(2,1)S(1)}, bf16[256,256]{1,0:T(8,128)(2,1)S(1)}, u32[]{:S(2)}, u32[]{:S(2)}) collective-permute-start(bf16[256,256]{1,0:T(8,128)(2,1)S(1)} %join.1.a_ref), channel_id=1, source_target_pairs={{0,12},{4,8},{8,4},{12,0},{1,13},{5,9},{9,5},{13,1},{2,14},{6,10},... | collective-permute-start | bytes 393224 | tf_op jit(solution)/shard_map/ppermute | solution.py:282
  12.8 6.4 %copy-start.4 = (f32[1,3,512]{2,0,1:T(1,128)S(1)}, f32[1,3,512]{2,0,1:T(1,128)}, u32[]{:S(2)}) copy-start(f32[1,3,512]{2,0,1:T(1,128)} %param.11) | copy-start | bytes 18436
  12.8 7.1 %copy-start.3 = (bf16[1,1024,512]{2,1,0:T(8,128)(2,1)S(1)}, bf16[1,1024,512]{2,1,0:T(8,128)(2,1)}, u32[]{:S(2)}) copy-start(bf16[1,1024,512]{2,1,0:T(8,128)(2,1)} %down_a.3) | copy-start | bytes 3145732
  13.9 6.0 %collective-permute-start.5 = (bf16[256,256]{1,0:T(8,128)(2,1)S(1)}, bf16[256,256]{1,0:T(8,128)(2,1)S(1)}, u32[]{:S(2)}, u32[]{:S(2)}) collective-permute-start(bf16[256,256]{1,0:T(8,128)(2,1)S(1)} %get-tuple-element.11.near_ref), channel_id=1, source_target_pairs={{0,4},{4,0},{8,12},{12,8},{1,5},{5,1},{9,13},{13,9},{2,6},{6,2},{1... | collective-permute-start | bytes 393224 | tf_op jit(solution)/shard_map/ppermute | solution.py:299
  15.7 3.5 %copy-start.1 = (bf16[512,512]{1,0:T(8,128)(2,1)S(1)}, bf16[512,512]{1,0:T(8,128)(2,1)}, u32[]{:S(2)}) copy-start(bf16[512,512]{1,0:T(8,128)(2,1)} %in_ref.5) | copy-start | bytes 1572868
  15.7 4.2 %copy-start.2 = (bf16[1,512,1024]{2,1,0:T(8,128)(2,1)S(1)}, bf16[1,512,1024]{2,1,0:T(8,128)(2,1)}, u32[]{:S(2)}) copy-start(bf16[1,512,1024]{2,1,0:T(8,128)(2,1)} %up_a.3) | copy-start | bytes 3145732
  16.8 5.7 %collective-permute-start.2 = (bf16[256,256]{1,0:T(8,128)(2,1)S(1)}, bf16[256,256]{1,0:T(8,128)(2,1)S(1)}, u32[]{:S(2)}, u32[]{:S(2)}) collective-permute-start(bf16[256,256]{1,0:T(8,128)(2,1)S(1)} %far.1.far_ref), channel_id=1, source_target_pairs={{4,8},{8,4},{5,9},{9,5},{6,10},{10,6},{7,11},{11,7},{20,24},{24,20... | collective-permute-start | bytes 393224 | tf_op jit(solution)/shard_map/ppermute | solution.py:304
  24.5 5.4 %collective-permute-start.6 = (bf16[2048,128]{1,0:T(8,128)(2,1)S(1)}, bf16[2048,128]{1,0:T(8,128)(2,1)S(1)}, u32[]{:S(2)}, u32[]{:S(2)}) collective-permute-start(bf16[2048,128]{1,0:T(8,128)(2,1)S(1)} %mix_far.1.own_ref), channel_id=1, source_target_pairs={{0,1},{1,0},{2,3},{3,2},{4,5},{5,4},{6,7},{7,6},{8,9},{9,8},{10,11... | collective-permute-start | bytes 1572872 | tf_op jit(solution)/shard_map/ppermute | solution.py:321

commit v4 on v3

--- a/solution.py
+++ b/solution.py
@@ -8,6 +8,7 @@
 from jax.experimental.pallas import tpu as pltpu
 from jax.sharding import PartitionSpec as P
 
+
 LANES = 128
 ROOM = 20 * 1024 * 1024
 BF16 = jnp.bfloat16
@@ -28,7 +29,7 @@
     return pltpu.VMEM(shape, dtype)
 
 
-def call(body, name, out, count, scratch=(), in_specs=None, out_specs=None):
+def call(body, out, count, scratch=(), in_specs=None, out_specs=None, aliases=None):
     many = isinstance(out, tuple)
     if out_specs is None:
         out_specs = (VMEM,) * len(out) if many else VMEM
@@ -38,8 +39,8 @@
         in_specs=[VMEM] * count if in_specs is None else in_specs,
         out_specs=out_specs,
         scratch_shapes=list(scratch),
+        input_output_aliases=aliases or {},
         compiler_params=pltpu.CompilerParams(vmem_limit_bytes=ROOM),
-        name=name,
     )
 
 
@@ -75,15 +76,21 @@
     return (stream * inverse_rms(stream, 1e-5)).astype(BF16).astype(F32)
 
 
-def pick_body(parts, frame_hbm, pixel_hbm, frames_hbm, out_ref, frame_ref, pixel_ref, frames_ref, sems):
+def pick_body(
+    parts, frame_hbm, pixel_hbm, frames_hbm, out_ref, frames_ref, frame_ref, pixel_ref, sems
+):
     frame_count, pixel_count, _ = frames_ref.shape
     loads = [
         pltpu.make_async_copy(frame_hbm, frame_ref, sems.at[0]),
         pltpu.make_async_copy(pixel_hbm, pixel_ref, sems.at[1]),
     ]
+    chunk = min(512, pixel_count)
+    spots = [(t, at) for t in range(frame_count) for at in range(0, pixel_count, chunk)]
     maps = [
-        pltpu.make_async_copy(frames_hbm.at[t], frames_ref.at[t], sems.at[2 + t])
-        for t in range(frame_count)
+        pltpu.make_async_copy(
+            frames_hbm.at[t, pl.ds(at, chunk)], frames_ref.at[t, pl.ds(at, chunk)], sems.at[2 + k]
+        )
+        for k, (t, at) in enumerate(spots)
     ]
     for copy in loads + maps:
         copy.start()
@@ -100,16 +107,13 @@
     place = jnp.where(owned, local * pixel_count + row * side + col, -1)
     count = place.shape[1]
     place = jnp.transpose(jnp.broadcast_to(place, (8, count)))[:, :1]
-    chunk = min(512, pixel_count)
     order = lax.broadcasted_iota(jnp.int32, (count, chunk), 1)
     total = None
-    for t in range(frame_count):
-        maps[t].wait()
-        for at in range(0, pixel_count, chunk):
-            start = t * pixel_count + at
-            hot = jnp.where(order == place - start, 1.0, 0.0).astype(BF16)
-            part_sum = dot(hot, frames_ref[t, at : at + chunk, :])
-            total = part_sum if total is None else total + part_sum
+    for copy, (t, at) in zip(maps, spots):
+        hot = jnp.where(order == place - (t * pixel_count + at), 1.0, 0.0).astype(BF16)
+        copy.wait()
+        part_sum = dot(hot, frames_ref[t, at : at + chunk, :])
+        total = part_sum if total is None else total + part_sum
     out_ref[...] = total.astype(BF16)
 
 
@@ -236,17 +240,30 @@
     out_ref[...] = line_ref[...].astype(BF16)
 
 
-def merge_body(own_ref, other_ref, out_ref, sems):
-    rows = own_ref.shape[0]
-    part = lax.axis_index("split")
-    own = pltpu.make_async_copy(own_ref, out_ref.at[pl.ds(part * rows, rows)], sems.at[0])
-    other = pltpu.make_async_copy(
-        other_ref, out_ref.at[pl.ds((1 - part) * rows, rows)], sems.at[1]
-    )
-    own.start()
-    other.start()
-    own.wait()
-    other.wait()
+def copy_lines(source_ref, target_ref, first, sems):
+    rows = source_ref.shape[0]
+    count = sems.shape[0]
+    size = rows // count
+    copies = [
+        pltpu.make_async_copy(
+            source_ref.at[pl.ds(k * size, size)],
+            target_ref.at[pl.ds(first + k * size, size)],
+            sems.at[k],
+        )
+        for k in range(count)
+    ]
+    for copy in copies:
+        copy.start()
+    for copy in copies:
+        copy.wait()
+
+
+def place_body(own_ref, out_ref, sems):
+    copy_lines(own_ref, out_ref, lax.axis_index("split") * own_ref.shape[0], sems)
+
+
+def merge_body(other_ref, _, out_ref, sems):
+    copy_lines(other_ref, out_ref, (1 - lax.axis_index("split")) * other_ref.shape[0], sems)
 
 
 def on_device(frames, query_frame, query_pixel, in_weight, conv_weight, up_weight, down_weight):
@@ -260,28 +277,26 @@
     rows = query_count // parts
     swap = [(0, 1), (1, 0)]
     flips = lambda mask: [(i, i ^ mask) for i in range(devices)]
-    up_other = held(lax.ppermute(up_weight, "split", swap))
-    down_other = held(lax.ppermute(down_weight, "split", swap))
-    mine = call(
+    mine, frames = call(
         functools.partial(pick_body, parts),
-        "pick",
-        kept((rows, channels), BF16),
+        (kept((rows, channels), BF16), kept(frames.shape, BF16)),
         3,
         scratch=(
             pltpu.VMEM((1, query_count), jnp.int32),
             pltpu.VMEM(query_pixel.shape, jnp.int32),
-            pltpu.VMEM(frames.shape, BF16),
-            pltpu.SemaphoreType.DMA((2 + frame_count,)),
+            pltpu.SemaphoreType.DMA((2 + frame_count * pixel_count // min(512, pixel_count),)),
         ),
         in_specs=[HBM] * 3,
     )(*(fixed(x) for x in (query_frame.reshape(1, query_count), query_pixel, frames)))
-    theirs = held(lax.ppermute(mine, "frame", flips(1)))
+    theirs = lax.ppermute(mine, "frame", flips(1))
+    up_other = lax.ppermute(up_weight, "split", swap)
+    down_other = lax.ppermute(down_weight, "split", swap)
+    theirs, up_other, down_other = held(theirs), held(up_other), held(down_other)
     stage = 2
     while stage < devices:
-        mine = call(join_body, "join", kept((rows, channels), BF16), 2)(mine, theirs)
+        mine = call(join_body, kept((rows, channels), BF16), 2)(mine, theirs)
         theirs = held(lax.ppermute(mine, "frame", flips(2 * stage - 1)))
         stage *= 2
-    frames = held(frames)
     in_weight = held(in_weight)
     taps = held(conv_weight.reshape(1, conv_weight.shape[1] * width))
     weights = (held(up_weight), up_other, held(down_weight), down_other)
@@ -294,39 +309,36 @@
     small = kept((rows, channels), BF16)
     wide = kept((rows, width), F32)
     features, near = call(
-        functools.partial(near_body, scale), "near", (small, small), 3, attention_scratch
+        functools.partial(near_body, scale), (small, small), 3, attention_scratch
     )(mine, theirs, frames)
     near_halo = held(lax.ppermute(near, "frame", flips(1)))
-    far = call(functools.partial(far_body, scale), "far", small, 2, attention_scratch)(
-        features, frames
-    )
-    pairs = [(i, i + 1) for i in range(1, devices - 1, 2)]
-    far_halo = held(lax.ppermute(far, "frame", pairs + [(b, a) for a, b in pairs]))
-    base, own_near, own_far = call(own_body, "own", (wide,) * 3, 5)(
-        features, near, far, in_weight, taps
-    )
+    far = call(functools.partial(far_body, scale), small, 2, attention_scratch)(features, frames)
+    pairs = [
+        (parts * i + c, parts * (i + 1) + c) for i in range(1, devices - 1, 2) for c in range(parts)
+    ] + [(parts * i, parts * i + 1) for i in (0, devices - 1)]
+    far_halo = held(
+        lax.ppermute(far, ("frame", "split"), pairs + [(b, a) for a, b in pairs])
+    )
+    base, own_near, own_far = call(own_body, (wide,) * 3, 5)(features, near, far, in_weight, taps)
     hidden = pltpu.VMEM((rows, parts * units), BF16)
-    near = call(functools.partial(mix_near_body, devices), "mix_near", wide, 9, (hidden,))(
+    near = call(functools.partial(mix_near_body, devices), wide, 9, (hidden,))(
         near_halo, own_near, base, in_weight, taps, *weights
     )
     blocks = width // LANES
     lines = rows * blocks * frame_count
     own = call(
         functools.partial(mix_far_body, devices),
-        "mix_far",
         kept((lines, LANES), BF16),
         10,
         (hidden, pltpu.VMEM((lines, LANES), F32)),
     )(far_halo, own_far, base, in_weight, taps, *weights, near)
     other = held(lax.ppermute(own, "split", swap))
+    whole = jax.ShapeDtypeStruct((parts * lines, LANES), BF16)
+    moves = (pltpu.SemaphoreType.DMA((4,)),)
+    both = call(place_body, whole, 1, moves, out_specs=HBM)(own)
     both = call(
-        merge_body,
-        "merge",
-        jax.ShapeDtypeStruct((parts * lines, LANES), BF16),
-        2,
-        (pltpu.SemaphoreType.DMA((2,)),),
-        out_specs=HBM,
-    )(own, other)
+        merge_body, whole, 2, moves, in_specs=[VMEM, HBM], out_specs=HBM, aliases={1: 0}
+    )(other, both)
     both = both.reshape(query_count, blocks, frame_count, LANES)
     return both.transpose(0, 2, 1, 3).reshape(query_count, frame_count, width)
 

time: 31 us -> 29.4 us (0.948); the launches traced: 30.8 us -> 28.9 us
  starting transfers between devices: 10.4 us -> 8.84 us
  waiting for transfers between devices: 10.7 us -> 9.76 us
  Pallas kernels: 9.57 us -> 10.2 us
    ppermute x4, starting transfers between devices: 4.53 us -> 2.63 us  [the longest x1 1.36 us: on_device(): theirs = lax.ppermute(mine, 'frame', flips(1))]
    ppermute x1, waiting for transfers between devices: 1.54 us -> 0.71 us  [on_device(): other = held(lax.ppermute(own, 'split', swap))]
    pallas_call x8 -> x9, Pallas kernels: 9.57 us -> 10.2 us  [the longest x1 2.04 us: on_device(): call(functools.partial(pick_body, parts), (kept((rows, channels), BF16),...]
  transfers between devices with their start and end apart: 7 -> 7, of which waited for: 4 -> 4; matrix products, arithmetic and copies ran while one was open for 0% -> 0% of each run, Pallas kernels for 22% -> 26%
where the time goes in v4:
time: 29.4 us; the launch traced here: 28.9 us
  Pallas kernels  10.2 us (35%)
  waiting for transfers between devices  9.76 us (33%)
  starting transfers between devices  8.84 us (30%)
    ppermute x1, waiting for transfers between devices, on_device(): theirs = held(lax.ppermute(mine, 'frame', flips(2 * stage - 1)))  4.98 us
    ppermute x1, starting transfers between devices, on_device(): other = held(lax.ppermute(own, 'split', swap))  4.05 us
    ppermute x1, waiting for transfers between devices, on_device(): theirs = lax.ppermute(mine, 'frame', flips(1))  3.25 us
    pallas_call x1, Pallas kernels, on_device(): call(functools.partial(pick_body, parts), (kept((rows, channels), BF16),...  2.04 us
    pallas_call x1, Pallas kernels, on_device(): call(functools.partial(mix_far_body, devices), kept((lines, LANES), BF16)...  1.95 us
    ppermute x1, starting transfers between devices, on_device(): near_halo = held(lax.ppermute(near, 'frame', flips(1)))  1.93 us
    pallas_call x1, Pallas kernels, on_device(): call(functools.partial(mix_near_body, devices), wide, 9, (hidden,))  1.79 us
    ppermute x1, starting transfers between devices, on_device(): theirs = lax.ppermute(mine, 'frame', flips(1))  1.36 us
  transfers between devices with their start and end apart: 7, of which 4 were waited for; matrix products, arithmetic and copies ran while one was open for 0% of the time, Pallas kernels for 26%

profile of v4, /device:TPU:17, one launch (start us, length us, event | category | flops | bytes accessed | tf_op | source)
XLA Modules:
  0.0 28.9 jit_solution(14348694425606838783)
XLA Ops:
  0.0 0.7 %collective-permute-start.3 = (bf16[1,512,1024]{2,1,0:T(8,128)(2,1)}, bf16[1,512,1024]{2,1,0:T(8,128)(2,1)S(1)}, u32[]{:S(2)}, u32[]{:S(2)}) collective-permute-start(bf16[1,512,1024]{2,1,0:T(8,128)(2,1)} %up_a.3), channel_id=1, source_target_pairs={{0,1},{1,0},{2,3},{3,2},{4,5},{5,4},{6,7},{7,6},{8,9},{9,8},{10,11... | collective-permute-start | bytes 3145736 | tf_op jit(solution)/shard_map/ppermute | solution.py:292
  0.7 0.0 collective-permute-start.4
  0.7 2.0 %shard_map.73 = (bf16[256,256]{1,0:T(8,128)(2,1)S(1)}, bf16[2,1024,256]{2,1,0:T(8,128)(2,1)S(1)}) custom-call(s32[1,512]{1,0:T(1,128)} %bitcast.10, s32[2,512]{1,0:T(2,128)} %pixel_hbm.1, bf16[2,1024,256]{2,1,0:T(8,128)(2,1)} %frames_hbm.1), custom_call_target="tpu_custom_call" | custom-call | tf_op jit(solution)/shard_map/pallas_call | solution.py:280
  2.7 1.4 %collective-permute-start = (bf16[256,256]{1,0:T(8,128)(2,1)S(1)}, bf16[256,256]{1,0:T(8,128)(2,1)S(1)}, u32[]{:S(2)}, u32[]{:S(2)}) collective-permute-start(bf16[256,256]{1,0:T(8,128)(2,1)S(1)} %get-tuple-element.12.a_ref), channel_id=1, source_target_pairs={{0,4},{4,0},{8,12},{12,8},{1,5},{5,1},{9,13},{13,9},{2,6},{6,2},{1... | collective-permute-start | bytes 393224 | tf_op jit(solution)/shard_map/ppermute | solution.py:291
  4.1 3.2 %collective-permute-done.b_ref = bf16[256,256]{1,0:T(8,128)(2,1)S(1)} collective-permute-done((bf16[256,256]{1,0:T(8,128)(2,1)S(1)}, bf16[256,256]{1,0:T(8,128)(2,1)S(1)}, u32[]{:S(2)}, u32[]{:S(2)}) %collective-permute-start) | collective-permute-done | bytes 131104 | tf_op jit(solution)/shard_map/ppermute | solution.py:291
  7.4 0.2 collective-permute-start.1
  7.6 5.0 %collective-permute-done.1.b_ref = bf16[256,256]{1,0:T(8,128)(2,1)S(1)} collective-permute-done((bf16[256,256]{1,0:T(8,128)(2,1)S(1)}, bf16[256,256]{1,0:T(8,128)(2,1)S(1)}, u32[]{:S(2)}, u32[]{:S(2)}) %collective-permute-start.1) | collective-permute-done | bytes 131104 | tf_op jit(solution)/shard_map/ppermute | solution.py:298
  12.6 1.1 %shard_map.75 = (bf16[256,256]{1,0:T(8,128)(2,1)S(1)}, bf16[256,256]{1,0:T(8,128)(2,1)S(1)}) custom-call(bf16[256,256]{1,0:T(8,128)(2,1)S(1)} %shard_map.74.a_ref, bf16[256,256]{1,0:T(8,128)(2,1)S(1)} %collective-permute-done.1.b_ref, bf16[2,1024,256]{2,1,0:T(8,128)(2,1)S(1)} %get-tuple-element.13.frames_ref), custom_call_target="tpu_custom_call" | custom-call | tf_op jit(solution)/shard_map/pallas_call | solution.py:311
  13.7 1.9 %collective-permute-start.5 = (bf16[256,256]{1,0:T(8,128)(2,1)S(1)}, bf16[256,256]{1,0:T(8,128)(2,1)S(1)}, u32[]{:S(2)}, u32[]{:S(2)}) collective-permute-start(bf16[256,256]{1,0:T(8,128)(2,1)S(1)} %get-tuple-element.15.near_ref), channel_id=1, source_target_pairs={{0,4},{4,0},{8,12},{12,8},{1,5},{5,1},{9,13},{13,9},{2,6},{6,2},{1... | collective-permute-start | bytes 393224 | tf_op jit(solution)/shard_map/ppermute | solution.py:314
  15.6 1.1 %shard_map.76.far_ref = bf16[256,256]{1,0:T(8,128)(2,1)S(1)} custom-call(bf16[256,256]{1,0:T(8,128)(2,1)S(1)} %get-tuple-element.14.features_ref, bf16[2,1024,256]{2,1,0:T(8,128)(2,1)S(1)} %get-tuple-element.13.frames_ref), custom_call_target="tpu_custom_call" | custom-call | tf_op jit(solution)/shard_map/pallas_call | solution.py:315
  16.7 0.6 %collective-permute-start.2 = (bf16[256,256]{1,0:T(8,128)(2,1)S(1)}, bf16[256,256]{1,0:T(8,128)(2,1)S(1)}, u32[]{:S(2)}, u32[]{:S(2)}) collective-permute-start(bf16[256,256]{1,0:T(8,128)(2,1)S(1)} %shard_map.76.far_ref), channel_id=1, source_target_pairs={{4,8},{5,9},{0,1},{12,13},{8,4},{9,5},{1,0},{13,12},{6,10},{7,11},... | collective-permute-start | bytes 393224 | tf_op jit(solution)/shard_map/ppermute | solution.py:320
  17.3 0.0 copy-done.3
  17.3 0.0 copy-done
  17.3 0.6 %shard_map.77 = (f32[256,512]{1,0:T(8,128)S(1)}, f32[256,512]{1,0:T(8,128)S(1)}, f32[256,512]{1,0:T(8,128)S(1)}) custom-call(bf16[256,256]{1,0:T(8,128)(2,1)S(1)} %get-tuple-element.14.features_ref, bf16[256,256]{1,0:T(8,128)(2,1)S(1)} %get-tuple-element.15.near_ref, bf16[256,256]{1,0:T(8,128)(2,1)S(1)} %shard_map.76.far_ref, bf16[512,512]{1,0:T(8,128)(2,1)S(1)} %copy-done, ...), custom_call_target="tpu_custom_call" | custom-call | tf_op jit(solution)/shard_map/pallas_call | solution.py:322
  17.9 0.0 collective-permute-done.5.halo_ref
  17.9 0.0 collective-permute-done.3.up_b
  17.9 0.0 collective-permute-done.4.down_b
  18.0 1.8 %shard_map.78.near_ref = f32[256,512]{1,0:T(8,128)S(1)} custom-call(bf16[256,256]{1,0:T(8,128)(2,1)S(1)} %collective-permute-done.5.halo_ref, f32[256,512]{1,0:T(8,128)S(1)} %get-tuple-element.18.own_ref, f32[256,512]{1,0:T(8,128)S(1)} %get-tuple-element.17.base_ref, bf16[512,512]{1,0:T(8,128)(2,1)S(1)} %copy-done, f32[1,1536]{1,0:T(1,128)S(1)} %bitcast.8, ...), custom_call_target="tpu_custom_call" | custom-call | tf_op jit(solution)/shard_map/pallas_call | solution.py:324
  19.8 0.8 %collective-permute-done.2.halo_ref = bf16[256,256]{1,0:T(8,128)(2,1)S(1)} collective-permute-done((bf16[256,256]{1,0:T(8,128)(2,1)S(1)}, bf16[256,256]{1,0:T(8,128)(2,1)S(1)}, u32[]{:S(2)}, u32[]{:S(2)}) %collective-permute-start.2) | collective-permute-done | bytes 131104 | tf_op jit(solution)/shard_map/ppermute | solution.py:320
  20.5 2.0 %shard_map.79.own_ref = bf16[2048,128]{1,0:T(8,128)(2,1)S(1)} custom-call(bf16[256,256]{1,0:T(8,128)(2,1)S(1)} %collective-permute-done.2.halo_ref, f32[256,512]{1,0:T(8,128)S(1)} %get-tuple-element.16.own_ref, f32[256,512]{1,0:T(8,128)S(1)} %get-tuple-element.17.base_ref, bf16[512,512]{1,0:T(8,128)(2,1)S(1)} %copy-done, f32[1,1536]{1,0:T(1,128)S(1)} %bitcast.9, ...), custom_call_target="tpu_custom_call" | custom-call | tf_op jit(solution)/shard_map/pallas_call | solution.py:329
  22.5 4.0 %collective-permute-start.6 = (bf16[2048,128]{1,0:T(8,128)(2,1)S(1)}, bf16[2048,128]{1,0:T(8,128)(2,1)S(1)}, u32[]{:S(2)}, u32[]{:S(2)}) collective-permute-start(bf16[2048,128]{1,0:T(8,128)(2,1)S(1)} %shard_map.79.own_ref), channel_id=1, source_target_pairs={{0,1},{1,0},{2,3},{3,2},{4,5},{5,4},{6,7},{7,6},{8,9},{9,8},{10,11... | collective-permute-start | bytes 1572872 | tf_op jit(solution)/shard_map/ppermute | solution.py:335
  26.6 0.8 %shard_map.80._ = bf16[4096,128]{1,0:T(8,128)(2,1)} custom-call(bf16[2048,128]{1,0:T(8,128)(2,1)S(1)} %shard_map.79.own_ref), custom_call_target="tpu_custom_call" | custom-call | tf_op jit(solution)/shard_map/pallas_call | solution.py:338
  27.4 0.7 %collective-permute-done.6.other_ref = bf16[2048,128]{1,0:T(8,128)(2,1)S(1)} collective-permute-done((bf16[2048,128]{1,0:T(8,128)(2,1)S(1)}, bf16[2048,128]{1,0:T(8,128)(2,1)S(1)}, u32[]{:S(2)}, u32[]{:S(2)}) %collective-permute-start.6) | collective-permute-done | bytes 524320 | tf_op jit(solution)/shard_map/ppermute | solution.py:335
  28.1 0.8 %shard_map.81 = bf16[4096,128]{1,0:T(8,128)(2,1)} custom-call(bf16[2048,128]{1,0:T(8,128)(2,1)S(1)} %collective-permute-done.6.other_ref, bf16[4096,128]{1,0:T(8,128)(2,1)} %shard_map.80._), custom_call_target="tpu_custom_call", output_to_operand_aliasing={{}: (1, {})} | custom-call | tf_op jit(solution)/shard_map/pallas_call | solution.py:339
  (7 shorter events, 0.0 us)
Async XLA Ops:
  0.0 17.9 %collective-permute-start.3 = (bf16[1,512,1024]{2,1,0:T(8,128)(2,1)}, bf16[1,512,1024]{2,1,0:T(8,128)(2,1)S(1)}, u32[]{:S(2)}, u32[]{:S(2)}) collective-permute-start(bf16[1,512,1024]{2,1,0:T(8,128)(2,1)} %up_a.3), channel_id=1, source_target_pairs={{0,1},{1,0},{2,3},{3,2},{4,5},{5,4},{6,7},{7,6},{8,9},{9,8},{10,11... | collective-permute-start | bytes 3145736 | tf_op jit(solution)/shard_map/ppermute | solution.py:292
  0.7 17.3 %collective-permute-start.4 = (bf16[1,1024,512]{2,1,0:T(8,128)(2,1)}, bf16[1,1024,512]{2,1,0:T(8,128)(2,1)S(1)}, u32[]{:S(2)}, u32[]{:S(2)}) collective-permute-start(bf16[1,1024,512]{2,1,0:T(8,128)(2,1)} %down_a.3), channel_id=1, source_target_pairs={{0,1},{1,0},{2,3},{3,2},{4,5},{5,4},{6,7},{7,6},{8,9},{9,8},{10,11... | collective-permute-start | bytes 3145736 | tf_op jit(solution)/shard_map/ppermute | solution.py:293
  2.7 4.6 %collective-permute-start = (bf16[256,256]{1,0:T(8,128)(2,1)S(1)}, bf16[256,256]{1,0:T(8,128)(2,1)S(1)}, u32[]{:S(2)}, u32[]{:S(2)}) collective-permute-start(bf16[256,256]{1,0:T(8,128)(2,1)S(1)} %get-tuple-element.12.a_ref), channel_id=1, source_target_pairs={{0,4},{4,0},{8,12},{12,8},{1,5},{5,1},{9,13},{13,9},{2,6},{6,2},{1... | collective-permute-start | bytes 393224 | tf_op jit(solution)/shard_map/ppermute | solution.py:291
  7.4 5.2 %collective-permute-start.1 = (bf16[256,256]{1,0:T(8,128)(2,1)S(1)}, bf16[256,256]{1,0:T(8,128)(2,1)S(1)}, u32[]{:S(2)}, u32[]{:S(2)}) collective-permute-start(bf16[256,256]{1,0:T(8,128)(2,1)S(1)} %shard_map.74.a_ref), channel_id=1, source_target_pairs={{0,12},{4,8},{8,4},{12,0},{1,13},{5,9},{9,5},{13,1},{2,14},{6,10},... | collective-permute-start | bytes 393224 | tf_op jit(solution)/shard_map/ppermute | solution.py:298
  12.6 4.7 %copy-start.3 = (f32[1,3,512]{2,0,1:T(1,128)S(1)}, f32[1,3,512]{2,0,1:T(1,128)}, u32[]{:S(2)}) copy-start(f32[1,3,512]{2,0,1:T(1,128)} %param.11) | copy-start | bytes 18436
  12.6 5.4 %copy-start.2 = (bf16[1,1024,512]{2,1,0:T(8,128)(2,1)S(1)}, bf16[1,1024,512]{2,1,0:T(8,128)(2,1)}, u32[]{:S(2)}) copy-start(bf16[1,1024,512]{2,1,0:T(8,128)(2,1)} %down_a.3) | copy-start | bytes 3145732
  13.7 4.3 %collective-permute-start.5 = (bf16[256,256]{1,0:T(8,128)(2,1)S(1)}, bf16[256,256]{1,0:T(8,128)(2,1)S(1)}, u32[]{:S(2)}, u32[]{:S(2)}) collective-permute-start(bf16[256,256]{1,0:T(8,128)(2,1)S(1)} %get-tuple-element.15.near_ref), channel_id=1, source_target_pairs={{0,4},{4,0},{8,12},{12,8},{1,5},{5,1},{9,13},{13,9},{2,6},{6,2},{1... | collective-permute-start | bytes 393224 | tf_op jit(solution)/shard_map/ppermute | solution.py:314
  15.6 1.7 %copy-start = (bf16[512,512]{1,0:T(8,128)(2,1)S(1)}, bf16[512,512]{1,0:T(8,128)(2,1)}, u32[]{:S(2)}) copy-start(bf16[512,512]{1,0:T(8,128)(2,1)} %in_ref.5) | copy-start | bytes 1572868
  15.6 2.4 %copy-start.1 = (bf16[1,512,1024]{2,1,0:T(8,128)(2,1)S(1)}, bf16[1,512,1024]{2,1,0:T(8,128)(2,1)}, u32[]{:S(2)}) copy-start(bf16[1,512,1024]{2,1,0:T(8,128)(2,1)} %up_a.3) | copy-start | bytes 3145732
  16.7 3.9 %collective-permute-start.2 = (bf16[256,256]{1,0:T(8,128)(2,1)S(1)}, bf16[256,256]{1,0:T(8,128)(2,1)S(1)}, u32[]{:S(2)}, u32[]{:S(2)}) collective-permute-start(bf16[256,256]{1,0:T(8,128)(2,1)S(1)} %shard_map.76.far_ref), channel_id=1, source_target_pairs={{4,8},{5,9},{0,1},{12,13},{8,4},{9,5},{1,0},{13,12},{6,10},{7,11},... | collective-permute-start | bytes 393224 | tf_op jit(solution)/shard_map/ppermute | solution.py:320
  22.5 5.6 %collective-permute-start.6 = (bf16[2048,128]{1,0:T(8,128)(2,1)S(1)}, bf16[2048,128]{1,0:T(8,128)(2,1)S(1)}, u32[]{:S(2)}, u32[]{:S(2)}) collective-permute-start(bf16[2048,128]{1,0:T(8,128)(2,1)S(1)} %shard_map.79.own_ref), channel_id=1, source_target_pairs={{0,1},{1,0},{2,3},{3,2},{4,5},{5,4},{6,7},{7,6},{8,9},{9,8},{10,11... | collective-permute-start | bytes 1572872 | tf_op jit(solution)/shard_map/ppermute | solution.py:335

commit v5 on v4

--- a/solution.py
+++ b/solution.py
@@ -77,7 +77,16 @@
 
 
 def pick_body(
-    parts, frame_hbm, pixel_hbm, frames_hbm, out_ref, frames_ref, frame_ref, pixel_ref, sems
+    parts,
+    frame_hbm,
+    pixel_hbm,
+    frames_hbm,
+    out_ref,
+    frames_ref,
+    outer_ref,
+    frame_ref,
+    pixel_ref,
+    sems,
 ):
     frame_count, pixel_count, _ = frames_ref.shape
     loads = [
@@ -92,11 +101,16 @@
         )
         for k, (t, at) in enumerate(spots)
     ]
-    for copy in loads + maps:
+    part = lax.axis_index("split")
+    share = outer_ref.shape[0]
+    side_of_pair = lax.rem(lax.axis_index("query"), 2)
+    outer = pltpu.make_async_copy(
+        frames_hbm.at[1 - near_frame(), pl.ds((2 * part + side_of_pair) * share, share)], outer_ref, sems.at[2 + len(maps)]
+    )
+    for copy in loads + maps + [outer]:
         copy.start()
     for copy in loads:
         copy.wait()
-    part = lax.axis_index("split")
     first = lax.axis_index("frame") * frame_count
     side = math.isqrt(pixel_count)
     pixel = pixel_ref[...]
@@ -115,40 +129,53 @@
         part_sum = dot(hot, frames_ref[t, at : at + chunk, :])
         total = part_sum if total is None else total + part_sum
     out_ref[...] = total.astype(BF16)
+    outer.wait()
 
 
 def join_body(a_ref, b_ref, out_ref):
     out_ref[...] = a_ref[...] + b_ref[...]
 
 
-def attend(features, frames_ref, t, scale, score_ref, weight_ref, sum_ref):
+def attend(features, maps, scale, scratch):
+    score_ref, weight_ref, sum_ref = scratch
     rows = features.shape[0]
-    pixel_count = frames_ref.shape[1]
-    chunk = min(256, pixel_count)
     step = 32
-    for at in range(0, pixel_count, chunk):
-        score_ref[:, at : at + chunk] = dot_t(features, frames_ref[t, at : at + chunk, :])
-    for at in range(0, rows, step):
-        scores = score_ref[at : at + step, :]
-        peak = jnp.max(scores, axis=-1, keepdims=True)
-        expd = jnp.exp2((scores - peak) * scale)
-        total = jnp.sum(expd, axis=-1, keepdims=True)
-        sum_ref[at : at + step, :] = jnp.broadcast_to(total, (step, LANES))
-        weight_ref[at : at + step, :] = expd.astype(BF16)
-    pooled = dot(weight_ref[...], frames_ref[t])
-    total = sum_ref[:, :1]
-    mean = jnp.mean(pooled * pooled, axis=-1, keepdims=True)
-    return (pooled * lax.rsqrt(mean + 1e-6 * total * total)).astype(BF16)
+    for k, blocks in enumerate(maps):
+        at = 0
+        for block in blocks:
+            score_ref[k, :, at : at + block.shape[0]] = dot_t(features, block[...])
+            at += block.shape[0]
+    for k in range(len(maps)):
+        for at in range(0, rows, step):
+            scores = score_ref[k, at : at + step, :]
+            peak = jnp.max(scores, axis=-1, keepdims=True)
+            expd = jnp.exp2((scores - peak) * scale)
+            total = jnp.sum(expd, axis=-1, keepdims=True)
+            sum_ref[k, at : at + step, :] = jnp.broadcast_to(total, (step, LANES))
+            weight_ref[k, at : at + step, :] = expd.astype(BF16)
+    out = []
+    for k, blocks in enumerate(maps):
+        at = 0
+        pooled = None
+        for block in blocks:
+            part = dot(weight_ref[k, :, at : at + block.shape[0]], block[...])
+            pooled = part if pooled is None else pooled + part
+            at += block.shape[0]
+        total = sum_ref[k, :, :1]
+        mean = jnp.mean(pooled * pooled, axis=-1, keepdims=True)
+        out.append((pooled * lax.rsqrt(mean + 1e-6 * total * total)).astype(BF16))
+    return out
 
 
 def near_body(scale, a_ref, b_ref, frames_ref, features_ref, normed_ref, *scratch):
     features = a_ref[...] + b_ref[...]
     features_ref[...] = features
-    normed_ref[...] = attend(features, frames_ref, near_frame(), scale, *scratch)
+    (normed_ref[...],) = attend(features, [[frames_ref.at[near_frame()]]], scale, scratch)
 
 
 def far_body(scale, features_ref, frames_ref, normed_ref, *scratch):
-    normed_ref[...] = attend(features_ref[...], frames_ref, 1 - near_frame(), scale, *scratch)
+    maps = [[frames_ref.at[1 - near_frame()]]]
+    (normed_ref[...],) = attend(features_ref[...], maps, scale, scratch)
 
 
 def taps_of(taps_ref):
@@ -158,16 +185,38 @@
     return jnp.where(even, last, first), middle, jnp.where(even, first, last)
 
 
-def own_body(features_ref, near_ref, far_ref, in_ref, taps_ref, base_ref, near_out, far_out):
-    channels = features_ref.shape[1]
+def own_body(
+    devices,
+    scale,
+    features_ref,
+    near_ref,
+    far_ref,
+    a_ref,
+    b_ref,
+    c_ref,
+    d_ref,
+    in_ref,
+    taps_ref,
+    base_ref,
+    near_out,
+    far_out,
+    *scratch,
+):
+    features = features_ref[...]
+    channels = features.shape[1]
     near_tap, middle, far_tap = taps_of(taps_ref)
-    base = dot(features_ref[...], in_ref[channels:, :])
+    place = lax.axis_index("frame")
+    inside = jnp.where(is_even(), place > 0, place < devices - 1)
+    base = dot(features, in_ref[channels:, :])
     base_ref[...] = base
     near = dot(near_ref[...], in_ref[:channels, :]) + base
     far = dot(far_ref[...], in_ref[:channels, :]) + base
     near_level, far_level = level_of(near), level_of(far)
     near_out[...] = near + middle * near_level + far_tap * far_level
     far_out[...] = far + middle * far_level + near_tap * near_level
+    (halo,) = attend(features, [[a_ref, b_ref, c_ref, d_ref]], scale, scratch)
+    halo = level_of(dot(halo, in_ref[:channels, :]) + base_ref[...])
+    far_out[...] += jnp.where(inside, far_tap, 0.0) * halo
 
 
 def mix(stream, ups, downs, hidden_ref):
@@ -191,23 +240,11 @@
     return stream + 0.5 * total
 
 
-def mixed_stream(halo_ref, own_ref, base_ref, in_ref, tap, inside):
-    channels = halo_ref.shape[1]
-    halo = level_of(dot(halo_ref[...], in_ref[:channels, :]) + base_ref[...])
-    return own_ref[...] + jnp.where(inside, tap, 0.0) * halo
+def mix_far_body(own_ref, up_a, up_b, down_a, down_b, out_ref, hidden_ref):
+    out_ref[...] = mix(own_ref[...], (up_a, up_b), (down_a, down_b), hidden_ref)
 
 
 def mix_near_body(
-    devices, halo_ref, own_ref, base_ref, in_ref, taps_ref, up_a, up_b, down_a, down_b, out_ref, hidden_ref
-):
-    place = lax.axis_index("frame")
-    inside = jnp.logical_not(is_even()) | (place < devices - 1)
-    tap, _, _ = taps_of(taps_ref)
-    stream = mixed_stream(halo_ref, own_ref, base_ref, in_ref, tap, inside)
-    out_ref[...] = mix(stream, (up_a, up_b), (down_a, down_b), hidden_ref)
-
-
-def mix_far_body(
     devices,
     halo_ref,
     own_ref,
@@ -218,18 +255,20 @@
     up_b,
     down_a,
     down_b,
-    near_ref,
+    far_ref,
     out_ref,
     hidden_ref,
     line_ref,
 ):
+    channels = halo_ref.shape[1]
     place = lax.axis_index("frame")
     even = is_even()
-    inside = jnp.where(even, place > 0, place < devices - 1)
-    _, _, tap = taps_of(taps_ref)
-    stream = mixed_stream(halo_ref, own_ref, base_ref, in_ref, tap, inside)
-    far = mix(stream, (up_a, up_b), (down_a, down_b), hidden_ref)
-    near = near_ref[...]
+    inside = jnp.logical_not(even) | (place < devices - 1)
+    tap, _, _ = taps_of(taps_ref)
+    halo = level_of(dot(halo_ref[...], in_ref[:channels, :]) + base_ref[...])
+    stream = own_ref[...] + jnp.where(inside, tap, 0.0) * halo
+    near = mix(stream, (up_a, up_b), (down_a, down_b), hidden_ref)
+    far = far_ref[...]
     rows, width = far.shape
     blocks = width // LANES
     for t, value in ((0, jnp.where(even, far, near)), (1, jnp.where(even, near, far))):
@@ -277,61 +316,72 @@
     rows = query_count // parts
     swap = [(0, 1), (1, 0)]
     flips = lambda mask: [(i, i ^ mask) for i in range(devices)]
-    mine, frames = call(
+    mine, frames, outer = call(
         functools.partial(pick_body, parts),
-        (kept((rows, channels), BF16), kept(frames.shape, BF16)),
+        (
+            kept((rows, channels), BF16),
+            kept(frames.shape, BF16),
+            kept((pixel_count // parts // 2, channels), BF16),
+        ),
         3,
         scratch=(
             pltpu.VMEM((1, query_count), jnp.int32),
             pltpu.VMEM(query_pixel.shape, jnp.int32),
-            pltpu.SemaphoreType.DMA((2 + frame_count * pixel_count // min(512, pixel_count),)),
+            pltpu.SemaphoreType.DMA((3 + frame_count * pixel_count // min(512, pixel_count),)),
         ),
         in_specs=[HBM] * 3,
     )(*(fixed(x) for x in (query_frame.reshape(1, query_count), query_pixel, frames)))
-    theirs = lax.ppermute(mine, "frame", flips(1))
+    pairs = [
+        (parts * i + c, parts * (i + 1) + c) for i in range(1, devices - 1, 2) for c in range(parts)
+    ] + [(parts * i, parts * i + 1) for i in (0, devices - 1)]
+    masks = [2 * (1 << k) - 1 for k in range(devices.bit_length() - 1)]
+    theirs = lax.ppermute(mine, "frame", flips(masks[0]))
+    outer = lax.ppermute(outer, ("frame", "split"), pairs + [(b, a) for a, b in pairs])
     up_other = lax.ppermute(up_weight, "split", swap)
     down_other = lax.ppermute(down_weight, "split", swap)
     theirs, up_other, down_other = held(theirs), held(up_other), held(down_other)
-    stage = 2
-    while stage < devices:
+    outer = held(outer)
+    for mask in masks[1:]:
         mine = call(join_body, kept((rows, channels), BF16), 2)(mine, theirs)
-        theirs = held(lax.ppermute(mine, "frame", flips(2 * stage - 1)))
-        stage *= 2
+        theirs = lax.ppermute(mine, "frame", flips(mask))
+        theirs = held(theirs)
+    groups = lax.axis_size("query")
+    assert groups % 2 == 0
+    outer_b = lax.ppermute(outer, "query", [(g, g ^ 1) for g in range(groups)])
+    outer_b = held(outer_b)
+    outer_c = lax.ppermute(outer, "split", swap)
+    outer_d = lax.ppermute(outer_b, "split", swap)
+    outers = (outer, outer_b, held(outer_c), held(outer_d))
     in_weight = held(in_weight)
     taps = held(conv_weight.reshape(1, conv_weight.shape[1] * width))
     weights = (held(up_weight), up_other, held(down_weight), down_other)
     scale = math.log2(math.e) / math.sqrt(channels)
-    attention_scratch = (
-        pltpu.VMEM((rows, pixel_count), F32),
-        pltpu.VMEM((rows, pixel_count), BF16),
-        pltpu.VMEM((rows, LANES), F32),
+    attention = lambda count: (
+        pltpu.VMEM((count, rows, pixel_count), F32),
+        pltpu.VMEM((count, rows, pixel_count), BF16),
+        pltpu.VMEM((count, rows, LANES), F32),
     )
     small = kept((rows, channels), BF16)
     wide = kept((rows, width), F32)
     features, near = call(
-        functools.partial(near_body, scale), (small, small), 3, attention_scratch
+        functools.partial(near_body, scale), (small, small), 3, attention(1)
     )(mine, theirs, frames)
-    near_halo = held(lax.ppermute(near, "frame", flips(1)))
-    far = call(functools.partial(far_body, scale), small, 2, attention_scratch)(features, frames)
-    pairs = [
-        (parts * i + c, parts * (i + 1) + c) for i in range(1, devices - 1, 2) for c in range(parts)
-    ] + [(parts * i, parts * i + 1) for i in (0, devices - 1)]
-    far_halo = held(
-        lax.ppermute(far, ("frame", "split"), pairs + [(b, a) for a, b in pairs])
-    )
-    base, own_near, own_far = call(own_body, (wide,) * 3, 5)(features, near, far, in_weight, taps)
+    near_halo = lax.ppermute(near, "frame", flips(1))
+    near_halo = held(near_halo)
+    far = call(functools.partial(far_body, scale), small, 2, attention(1))(features, frames)
+    base, own_near, own_far = call(
+        functools.partial(own_body, devices, scale), (wide,) * 3, 9, attention(1)
+    )(features, near, far, *outers, in_weight, taps)
     hidden = pltpu.VMEM((rows, parts * units), BF16)
-    near = call(functools.partial(mix_near_body, devices), wide, 9, (hidden,))(
-        near_halo, own_near, base, in_weight, taps, *weights
-    )
+    far = call(mix_far_body, wide, 5, (hidden,))(own_far, *weights)
     blocks = width // LANES
     lines = rows * blocks * frame_count
     own = call(
-        functools.partial(mix_far_body, devices),
+        functools.partial(mix_near_body, devices),
         kept((lines, LANES), BF16),
         10,
         (hidden, pltpu.VMEM((lines, LANES), F32)),
-    )(far_halo, own_far, base, in_weight, taps, *weights, near)
+    )(near_halo, own_near, base, in_weight, taps, *weights, far)
     other = held(lax.ppermute(own, "split", swap))
     whole = jax.ShapeDtypeStruct((parts * lines, LANES), BF16)
     moves = (pltpu.SemaphoreType.DMA((4,)),)

time: 29.4 us -> 30.2 us (1.027)
  the two profiles are of different devices: /device:TPU:17 before, /device:TPU:0 now
where the time goes in v5:
time: 30.2 us; the launch traced here: 30.1 us
  starting transfers between devices  12.6 us (42%)
  Pallas kernels  11 us (36%)
  waiting for transfers between devices  6.24 us (21%)
    ppermute x1, starting transfers between devices, on_device(): theirs = lax.ppermute(mine, 'frame', flips(masks[0]))  4.14 us
    ppermute x1, waiting for transfers between devices, on_device(): theirs = lax.ppermute(mine, 'frame', flips(mask))  3.28 us
    ppermute x1, starting transfers between devices, on_device(): theirs = lax.ppermute(mine, 'frame', flips(mask))  3.04 us
    ppermute x1, starting transfers between devices, on_device(): near_halo = lax.ppermute(near, 'frame', flips(1))  2.31 us
    pallas_call x1, Pallas kernels, on_device(): call(functools.partial(pick_body, parts), (kept((rows, channels), BF16),...  2.05 us
    pallas_call x1, Pallas kernels, on_device(): call(functools.partial(mix_near_body, devices), kept((lines, LANES), BF16...  1.96 us
    ppermute x1, waiting for transfers between devices, on_device(): theirs = lax.ppermute(mine, 'frame', flips(masks[0]))  1.88 us
    pallas_call x1, Pallas kernels, on_device(): call(functools.partial(own_body, devices, scale), (wide,) * 3, 9, attenti...  1.76 us
  transfers between devices with their start and end apart: 10, of which 3 were waited for; matrix products, arithmetic and copies ran while one was open for 0% of the time, Pallas kernels for 27%

profile of v5, /device:TPU:0, one launch (start us, length us, event | category | flops | bytes accessed | tf_op | source)
XLA Modules:
  0.0 30.1 jit_solution(9611554327245777868)
XLA Ops:
  0.0 0.5 %collective-permute-start.7 = (bf16[1,512,1024]{2,1,0:T(8,128)(2,1)}, bf16[1,512,1024]{2,1,0:T(8,128)(2,1)S(1)}, u32[]{:S(2)}, u32[]{:S(2)}) collective-permute-start(bf16[1,512,1024]{2,1,0:T(8,128)(2,1)} %up_a.3), channel_id=1, source_target_pairs={{0,1},{1,0},{2,3},{3,2},{4,5},{5,4},{6,7},{7,6},{8,9},{9,8},{10,11... | collective-permute-start | bytes 3145736 | tf_op jit(solution)/shard_map/ppermute | solution.py:340
  0.5 0.0 collective-permute-start.8
  0.5 2.0 %shard_map.73 = (bf16[256,256]{1,0:T(8,128)(2,1)S(1)}, bf16[2,1024,256]{2,1,0:T(8,128)(2,1)S(1)}, bf16[256,256]{1,0:T(8,128)(2,1)S(1)}) custom-call(s32[1,512]{1,0:T(1,128)} %bitcast.9, s32[2,512]{1,0:T(2,128)} %pixel_hbm.1, bf16[2,1024,256]{2,1,0:T(8,128)(2,1)} %frames_hbm.1), custom_call_target="tpu_custom_call" | custom-call | tf_op jit(solution)/shard_map/pallas_call | solution.py:319
  2.6 0.6 %collective-permute-start.3 = (bf16[256,256]{1,0:T(8,128)(2,1)S(1)}, bf16[256,256]{1,0:T(8,128)(2,1)S(1)}, u32[]{:S(2)}, u32[]{:S(2)}) collective-permute-start(bf16[256,256]{1,0:T(8,128)(2,1)S(1)} %get-tuple-element.17), channel_id=1, source_target_pairs={{4,8},{5,9},{0,1},{12,13},{8,4},{9,5},{1,0},{13,12},{6,10},{7,11},... | collective-permute-start | bytes 393224 | tf_op jit(solution)/shard_map/ppermute | solution.py:339
  3.1 4.1 %collective-permute-start = (bf16[256,256]{1,0:T(8,128)(2,1)S(1)}, bf16[256,256]{1,0:T(8,128)(2,1)S(1)}, u32[]{:S(2)}, u32[]{:S(2)}) collective-permute-start(bf16[256,256]{1,0:T(8,128)(2,1)S(1)} %get-tuple-element.13.a_ref), channel_id=1, source_target_pairs={{0,4},{4,0},{8,12},{12,8},{1,5},{5,1},{9,13},{13,9},{2,6},{6,2},{1... | collective-permute-start | bytes 393224 | tf_op jit(solution)/shard_map/ppermute | solution.py:338
  7.3 1.5 %collective-permute-start.4 = (bf16[256,256]{1,0:T(8,128)(2,1)S(1)}, bf16[256,256]{1,0:T(8,128)(2,1)S(1)}, u32[]{:S(2)}, u32[]{:S(2)}) collective-permute-start(bf16[256,256]{1,0:T(8,128)(2,1)S(1)} %collective-permute-done.3.a_ref), channel_id=1, source_target_pairs={{0,2},{2,0},{1,3},{3,1},{4,6},{6,4},{5,7},{7,5},{8,10},{10,8},{9,1... | collective-permute-start | bytes 393224 | tf_op jit(solution)/shard_map/ppermute | solution.py:350
  8.8 1.9 %collective-permute-done.b_ref = bf16[256,256]{1,0:T(8,128)(2,1)S(1)} collective-permute-done((bf16[256,256]{1,0:T(8,128)(2,1)S(1)}, bf16[256,256]{1,0:T(8,128)(2,1)S(1)}, u32[]{:S(2)}, u32[]{:S(2)}) %collective-permute-start) | collective-permute-done | bytes 131104 | tf_op jit(solution)/shard_map/ppermute | solution.py:338
  10.7 3.0 %collective-permute-start.1 = (bf16[256,256]{1,0:T(8,128)(2,1)S(1)}, bf16[256,256]{1,0:T(8,128)(2,1)S(1)}, u32[]{:S(2)}, u32[]{:S(2)}) collective-permute-start(bf16[256,256]{1,0:T(8,128)(2,1)S(1)} %shard_map.74.a_ref), channel_id=1, source_target_pairs={{0,12},{4,8},{8,4},{12,0},{1,13},{5,9},{9,5},{13,1},{2,14},{6,10},... | collective-permute-start | bytes 393224 | tf_op jit(solution)/shard_map/ppermute | solution.py:346
  13.7 0.0 collective-permute-start.5
  13.7 0.0 collective-permute-done.4.b_ref
  13.7 0.5 %collective-permute-start.6 = (bf16[256,256]{1,0:T(8,128)(2,1)S(1)}, bf16[256,256]{1,0:T(8,128)(2,1)S(1)}, u32[]{:S(2)}, u32[]{:S(2)}) collective-permute-start(bf16[256,256]{1,0:T(8,128)(2,1)S(1)} %collective-permute-done.4.b_ref), channel_id=1, source_target_pairs={{0,1},{1,0},{2,3},{3,2},{4,5},{5,4},{6,7},{7,6},{8,9},{9,8},{10,11... | collective-permute-start | bytes 393224 | tf_op jit(solution)/shard_map/ppermute | solution.py:353
  14.2 3.3 %collective-permute-done.1.b_ref = bf16[256,256]{1,0:T(8,128)(2,1)S(1)} collective-permute-done((bf16[256,256]{1,0:T(8,128)(2,1)S(1)}, bf16[256,256]{1,0:T(8,128)(2,1)S(1)}, u32[]{:S(2)}, u32[]{:S(2)}) %collective-permute-start.1) | collective-permute-done | bytes 131104 | tf_op jit(solution)/shard_map/ppermute | solution.py:346
  17.5 1.1 %shard_map.75 = (bf16[256,256]{1,0:T(8,128)(2,1)S(1)}, bf16[256,256]{1,0:T(8,128)(2,1)S(1)}) custom-call(bf16[256,256]{1,0:T(8,128)(2,1)S(1)} %shard_map.74.a_ref, bf16[256,256]{1,0:T(8,128)(2,1)S(1)} %collective-permute-done.1.b_ref, bf16[2,1024,256]{2,1,0:T(8,128)(2,1)S(1)} %get-tuple-element.14.frames_ref), custom_call_target="tpu_custom_call" | custom-call | tf_op jit(solution)/shard_map/pallas_call | solution.py:366
  18.6 2.3 %collective-permute-start.2 = (bf16[256,256]{1,0:T(8,128)(2,1)S(1)}, bf16[256,256]{1,0:T(8,128)(2,1)S(1)}, u32[]{:S(2)}, u32[]{:S(2)}) collective-permute-start(bf16[256,256]{1,0:T(8,128)(2,1)S(1)} %get-tuple-element.15.near_ref), channel_id=1, source_target_pairs={{0,4},{4,0},{8,12},{12,8},{1,5},{5,1},{9,13},{13,9},{2,6},{6,2},{1... | collective-permute-start | bytes 393224 | tf_op jit(solution)/shard_map/ppermute | solution.py:369
  20.9 1.1 %shard_map.76.far_ref = bf16[256,256]{1,0:T(8,128)(2,1)S(1)} custom-call(bf16[256,256]{1,0:T(8,128)(2,1)S(1)} %get-tuple-element.16.features_ref, bf16[2,1024,256]{2,1,0:T(8,128)(2,1)S(1)} %get-tuple-element.14.frames_ref), custom_call_target="tpu_custom_call" | custom-call | tf_op jit(solution)/shard_map/pallas_call | solution.py:371
  22.0 0.0 copy-start
  22.0 0.0 collective-permute-done.5.c_ref
  22.0 1.8 %shard_map.77 = (f32[256,512]{1,0:T(8,128)S(1)}, f32[256,512]{1,0:T(8,128)S(1)}, f32[256,512]{1,0:T(8,128)S(1)}) custom-call(bf16[256,256]{1,0:T(8,128)(2,1)S(1)} %get-tuple-element.16.features_ref, bf16[256,256]{1,0:T(8,128)(2,1)S(1)} %get-tuple-element.15.near_ref, bf16[256,256]{1,0:T(8,128)(2,1)S(1)} %shard_map.76.far_ref, ...), custom_call_target="tpu_custom_call" | custom-call | tf_op jit(solution)/shard_map/pallas_call | solution.py:372
  23.8 1.5 %shard_map.78.far_ref = f32[256,512]{1,0:T(8,128)S(1)} custom-call(f32[256,512]{1,0:T(8,128)S(1)} %get-tuple-element.20.own_ref, bf16[1,512,1024]{2,1,0:T(8,128)(2,1)S(1)} %copy-done, bf16[1,512,1024]{2,1,0:T(8,128)(2,1)S(1)} %collective-permute-done.7.up_b, bf16[1,1024,512]{2,1,0:T(8,128)(2,1)S(1)} %copy-done.1, ...), custom_call_target="tpu_custom_call" | custom-call | tf_op jit(solution)/shard_map/pallas_call | solution.py:376
  25.3 2.0 %shard_map.79.own_ref = bf16[2048,128]{1,0:T(8,128)(2,1)S(1)} custom-call(bf16[256,256]{1,0:T(8,128)(2,1)S(1)} %collective-permute-done.2.halo_ref, f32[256,512]{1,0:T(8,128)S(1)} %get-tuple-element.18.own_ref, f32[256,512]{1,0:T(8,128)S(1)} %get-tuple-element.19.base_ref, bf16[512,512]{1,0:T(8,128)(2,1)S(1)} %copy-done.2, f32[1,1536]{1,0:T(1,128)S(1)} %bitcast.8, ...), custom_call_target="tpu_custom_call" | custom-call | tf_op jit(solution)/shard_map/pallas_call | solution.py:379
  27.3 0.1 collective-permute-start.9
  27.4 0.8 %shard_map.80._ = bf16[4096,128]{1,0:T(8,128)(2,1)} custom-call(bf16[2048,128]{1,0:T(8,128)(2,1)S(1)} %shard_map.79.own_ref), custom_call_target="tpu_custom_call" | custom-call | tf_op jit(solution)/shard_map/pallas_call | solution.py:388
  28.2 1.1 %collective-permute-done.9.other_ref = bf16[2048,128]{1,0:T(8,128)(2,1)S(1)} collective-permute-done((bf16[2048,128]{1,0:T(8,128)(2,1)S(1)}, bf16[2048,128]{1,0:T(8,128)(2,1)S(1)}, u32[]{:S(2)}, u32[]{:S(2)}) %collective-permute-start.9) | collective-permute-done | bytes 524320 | tf_op jit(solution)/shard_map/ppermute | solution.py:385
  29.3 0.8 %shard_map.81 = bf16[4096,128]{1,0:T(8,128)(2,1)} custom-call(bf16[2048,128]{1,0:T(8,128)(2,1)S(1)} %collective-permute-done.9.other_ref, bf16[4096,128]{1,0:T(8,128)(2,1)} %shard_map.80._), custom_call_target="tpu_custom_call", output_to_operand_aliasing={{}: (1, {})} | custom-call | tf_op jit(solution)/shard_map/pallas_call | solution.py:389
  (13 shorter events, 0.0 us)
Async XLA Ops:
  0.0 23.8 %collective-permute-start.7 = (bf16[1,512,1024]{2,1,0:T(8,128)(2,1)}, bf16[1,512,1024]{2,1,0:T(8,128)(2,1)S(1)}, u32[]{:S(2)}, u32[]{:S(2)}) collective-permute-start(bf16[1,512,1024]{2,1,0:T(8,128)(2,1)} %up_a.3), channel_id=1, source_target_pairs={{0,1},{1,0},{2,3},{3,2},{4,5},{5,4},{6,7},{7,6},{8,9},{9,8},{10,11... | collective-permute-start | bytes 3145736 | tf_op jit(solution)/shard_map/ppermute | solution.py:340
  0.5 23.3 %collective-permute-start.8 = (bf16[1,1024,512]{2,1,0:T(8,128)(2,1)}, bf16[1,1024,512]{2,1,0:T(8,128)(2,1)S(1)}, u32[]{:S(2)}, u32[]{:S(2)}) collective-permute-start(bf16[1,1024,512]{2,1,0:T(8,128)(2,1)} %down_a.3), channel_id=1, source_target_pairs={{0,1},{1,0},{2,3},{3,2},{4,5},{5,4},{6,7},{7,6},{8,9},{9,8},{10,11... | collective-permute-start | bytes 3145736 | tf_op jit(solution)/shard_map/ppermute | solution.py:341
  2.6 4.7 %collective-permute-start.3 = (bf16[256,256]{1,0:T(8,128)(2,1)S(1)}, bf16[256,256]{1,0:T(8,128)(2,1)S(1)}, u32[]{:S(2)}, u32[]{:S(2)}) collective-permute-start(bf16[256,256]{1,0:T(8,128)(2,1)S(1)} %get-tuple-element.17), channel_id=1, source_target_pairs={{4,8},{5,9},{0,1},{12,13},{8,4},{9,5},{1,0},{13,12},{6,10},{7,11},... | collective-permute-start | bytes 393224 | tf_op jit(solution)/shard_map/ppermute | solution.py:339
  3.1 7.5 %collective-permute-start = (bf16[256,256]{1,0:T(8,128)(2,1)S(1)}, bf16[256,256]{1,0:T(8,128)(2,1)S(1)}, u32[]{:S(2)}, u32[]{:S(2)}) collective-permute-start(bf16[256,256]{1,0:T(8,128)(2,1)S(1)} %get-tuple-element.13.a_ref), channel_id=1, source_target_pairs={{0,4},{4,0},{8,12},{12,8},{1,5},{5,1},{9,13},{13,9},{2,6},{6,2},{1... | collective-permute-start | bytes 393224 | tf_op jit(solution)/shard_map/ppermute | solution.py:338
  7.3 6.4 %collective-permute-start.4 = (bf16[256,256]{1,0:T(8,128)(2,1)S(1)}, bf16[256,256]{1,0:T(8,128)(2,1)S(1)}, u32[]{:S(2)}, u32[]{:S(2)}) collective-permute-start(bf16[256,256]{1,0:T(8,128)(2,1)S(1)} %collective-permute-done.3.a_ref), channel_id=1, source_target_pairs={{0,2},{2,0},{1,3},{3,1},{4,6},{6,4},{5,7},{7,5},{8,10},{10,8},{9,1... | collective-permute-start | bytes 393224 | tf_op jit(solution)/shard_map/ppermute | solution.py:350
  10.7 6.8 %collective-permute-start.1 = (bf16[256,256]{1,0:T(8,128)(2,1)S(1)}, bf16[256,256]{1,0:T(8,128)(2,1)S(1)}, u32[]{:S(2)}, u32[]{:S(2)}) collective-permute-start(bf16[256,256]{1,0:T(8,128)(2,1)S(1)} %shard_map.74.a_ref), channel_id=1, source_target_pairs={{0,12},{4,8},{8,4},{12,0},{1,13},{5,9},{9,5},{13,1},{2,14},{6,10},... | collective-permute-start | bytes 393224 | tf_op jit(solution)/shard_map/ppermute | solution.py:346
  13.7 8.3 %collective-permute-start.5 = (bf16[256,256]{1,0:T(8,128)(2,1)S(1)}, bf16[256,256]{1,0:T(8,128)(2,1)S(1)}, u32[]{:S(2)}, u32[]{:S(2)}) collective-permute-start(bf16[256,256]{1,0:T(8,128)(2,1)S(1)} %collective-permute-done.3.a_ref), channel_id=1, source_target_pairs={{0,1},{1,0},{2,3},{3,2},{4,5},{5,4},{6,7},{7,6},{8,9},{9,8},{10,11... | collective-permute-start | bytes 393224 | tf_op jit(solution)/shard_map/ppermute | solution.py:352
  13.7 8.3 %collective-permute-start.6 = (bf16[256,256]{1,0:T(8,128)(2,1)S(1)}, bf16[256,256]{1,0:T(8,128)(2,1)S(1)}, u32[]{:S(2)}, u32[]{:S(2)}) collective-permute-start(bf16[256,256]{1,0:T(8,128)(2,1)S(1)} %collective-permute-done.4.b_ref), channel_id=1, source_target_pairs={{0,1},{1,0},{2,3},{3,2},{4,5},{5,4},{6,7},{7,6},{8,9},{9,8},{10,11... | collective-permute-start | bytes 393224 | tf_op jit(solution)/shard_map/ppermute | solution.py:353
  17.5 4.5 %copy-start.2 = (bf16[512,512]{1,0:T(8,128)(2,1)S(1)}, bf16[512,512]{1,0:T(8,128)(2,1)}, u32[]{:S(2)}) copy-start(bf16[512,512]{1,0:T(8,128)(2,1)} %in_ref.3) | copy-start | bytes 1572868
  18.6 6.7 %collective-permute-start.2 = (bf16[256,256]{1,0:T(8,128)(2,1)S(1)}, bf16[256,256]{1,0:T(8,128)(2,1)S(1)}, u32[]{:S(2)}, u32[]{:S(2)}) collective-permute-start(bf16[256,256]{1,0:T(8,128)(2,1)S(1)} %get-tuple-element.15.near_ref), channel_id=1, source_target_pairs={{0,4},{4,0},{8,12},{12,8},{1,5},{5,1},{9,13},{13,9},{2,6},{6,2},{1... | collective-permute-start | bytes 393224 | tf_op jit(solution)/shard_map/ppermute | solution.py:369
  20.9 1.1 %copy-start.3 = (f32[1,3,512]{2,0,1:T(1,128)S(1)}, f32[1,3,512]{2,0,1:T(1,128)}, u32[]{:S(2)}) copy-start(f32[1,3,512]{2,0,1:T(1,128)} %param.11) | copy-start | bytes 18436
  20.9 2.9 %copy-start.1 = (bf16[1,1024,512]{2,1,0:T(8,128)(2,1)S(1)}, bf16[1,1024,512]{2,1,0:T(8,128)(2,1)}, u32[]{:S(2)}) copy-start(bf16[1,1024,512]{2,1,0:T(8,128)(2,1)} %down_a.3) | copy-start | bytes 3145732
  22.0 1.9 %copy-start = (bf16[1,512,1024]{2,1,0:T(8,128)(2,1)S(1)}, bf16[1,512,1024]{2,1,0:T(8,128)(2,1)}, u32[]{:S(2)}) copy-start(bf16[1,512,1024]{2,1,0:T(8,128)(2,1)} %up_a.3) | copy-start | bytes 3145732
  27.3 2.0 %collective-permute-start.9 = (bf16[2048,128]{1,0:T(8,128)(2,1)S(1)}, bf16[2048,128]{1,0:T(8,128)(2,1)S(1)}, u32[]{:S(2)}, u32[]{:S(2)}) collective-permute-start(bf16[2048,128]{1,0:T(8,128)(2,1)S(1)} %shard_map.79.own_ref), channel_id=1, source_target_pairs={{0,1},{1,0},{2,3},{3,2},{4,5},{5,4},{6,7},{7,6},{8,9},{9,8},{10,11... | collective-permute-start | bytes 1572872 | tf_op jit(solution)/shard_map/ppermute | solution.py:385

commit v6 on v5

--- a/solution.py
+++ b/solution.py
@@ -94,12 +94,12 @@
         pltpu.make_async_copy(pixel_hbm, pixel_ref, sems.at[1]),
     ]
     chunk = min(512, pixel_count)
-    spots = [(t, at) for t in range(frame_count) for at in range(0, pixel_count, chunk)]
+    spots = [(at, t) for at in range(0, pixel_count, chunk) for t in range(frame_count)]
     maps = [
         pltpu.make_async_copy(
             frames_hbm.at[t, pl.ds(at, chunk)], frames_ref.at[t, pl.ds(at, chunk)], sems.at[2 + k]
         )
-        for k, (t, at) in enumerate(spots)
+        for k, (at, t) in enumerate(spots)
     ]
     part = lax.axis_index("split")
     share = outer_ref.shape[0]
@@ -117,18 +117,32 @@
     local = my_part(frame_ref[...], part, parts) - first
     row = my_part(pixel[0:1], part, parts)
     col = my_part(pixel[1:2], part, parts)
-    owned = (local >= 0) & (local < frame_count)
-    place = jnp.where(owned, local * pixel_count + row * side + col, -1)
+    place = row * side + col
     count = place.shape[1]
-    place = jnp.transpose(jnp.broadcast_to(place, (8, count)))[:, :1]
-    order = lax.broadcasted_iota(jnp.int32, (count, chunk), 1)
-    total = None
-    for copy, (t, at) in zip(maps, spots):
-        hot = jnp.where(order == place - (t * pixel_count + at), 1.0, 0.0).astype(BF16)
-        copy.wait()
-        part_sum = dot(hot, frames_ref[t, at : at + chunk, :])
-        total = part_sum if total is None else total + part_sum
-    out_ref[...] = total.astype(BF16)
+    line = lax.broadcasted_iota(jnp.int32, (8, count), 0)
+    both = jnp.transpose(jnp.where(line == 0, place, local))
+    place = jnp.broadcast_to(both[:, :1], (count, LANES))
+    local = jnp.broadcast_to(both[:, 1:2], (count, LANES))
+    order = lax.broadcasted_iota(jnp.int32, (count, LANES), 1)
+    totals = [None] * frame_count
+    for at in range(0, pixel_count, chunk):
+        hot = jnp.concatenate(
+            [
+                jnp.where(place == order + k, 1.0, 0.0).astype(BF16)
+                for k in range(at, at + chunk, LANES)
+            ],
+            axis=1,
+        )
+        for t in range(frame_count):
+            maps[spots.index((at, t))].wait()
+        for t in range(frame_count):
+            part_sum = dot(hot, frames_ref[t, at : at + chunk, :])
+            totals[t] = part_sum if at == 0 else totals[t] + part_sum
+    for b in range(0, out_ref.shape[1], LANES):
+        picked = jnp.zeros((count, LANES), F32)
+        for t in range(frame_count):
+            picked = jnp.where(local == t, totals[t][:, b : b + LANES], picked)
+        out_ref[:, b : b + LANES] = picked.astype(BF16)
     outer.wait()
 
 

time: 30.2 us -> 29.9 us (0.990)
    pallas_call x1, Pallas kernels: 2.05 us -> 1.72 us  [on_device(): call(functools.partial(pick_body, parts), (kept((rows, channels), BF16),...]
where the time goes in v6:
time: 29.9 us; the launch traced here: 29.8 us
  starting transfers between devices  12.6 us (42%)
  Pallas kernels  10.7 us (36%)
  waiting for transfers between devices  6.24 us (21%)
    ppermute x1, starting transfers between devices, on_device(): theirs = lax.ppermute(mine, 'frame', flips(masks[0]))  4.14 us
    ppermute x1, waiting for transfers between devices, on_device(): theirs = lax.ppermute(mine, 'frame', flips(mask))  3.27 us
    ppermute x1, starting transfers between devices, on_device(): theirs = lax.ppermute(mine, 'frame', flips(mask))  3.04 us
    ppermute x1, starting transfers between devices, on_device(): near_halo = lax.ppermute(near, 'frame', flips(1))  2.31 us
    pallas_call x1, Pallas kernels, on_device(): call(functools.partial(mix_near_body, devices), kept((lines, LANES), BF16...  1.96 us
    ppermute x1, waiting for transfers between devices, on_device(): theirs = lax.ppermute(mine, 'frame', flips(masks[0]))  1.89 us
    pallas_call x1, Pallas kernels, on_device(): call(functools.partial(own_body, devices, scale), (wide,) * 3, 9, attenti...  1.76 us
    pallas_call x1, Pallas kernels, on_device(): call(functools.partial(pick_body, parts), (kept((rows, channels), BF16),...  1.72 us
  transfers between devices with their start and end apart: 10, of which 3 were waited for; matrix products, arithmetic and copies ran while one was open for 0% of the time, Pallas kernels for 27%

profile of v6, /device:TPU:0, one launch (start us, length us, event | category | flops | bytes accessed | tf_op | source)
XLA Modules:
  0.0 29.8 jit_solution(6901791112119633505)
XLA Ops:
  0.0 0.5 %collective-permute-start.7 = (bf16[1,512,1024]{2,1,0:T(8,128)(2,1)}, bf16[1,512,1024]{2,1,0:T(8,128)(2,1)S(1)}, u32[]{:S(2)}, u32[]{:S(2)}) collective-permute-start(bf16[1,512,1024]{2,1,0:T(8,128)(2,1)} %up_a.3), channel_id=1, source_target_pairs={{0,1},{1,0},{2,3},{3,2},{4,5},{5,4},{6,7},{7,6},{8,9},{9,8},{10,11... | collective-permute-start | bytes 3145736 | tf_op jit(solution)/shard_map/ppermute | solution.py:354
  0.5 0.0 collective-permute-start.8
  0.5 1.7 %shard_map.73 = (bf16[256,256]{1,0:T(8,128)(2,1)S(1)}, bf16[2,1024,256]{2,1,0:T(8,128)(2,1)S(1)}, bf16[256,256]{1,0:T(8,128)(2,1)S(1)}) custom-call(s32[1,512]{1,0:T(1,128)} %bitcast.9, s32[2,512]{1,0:T(2,128)} %pixel_hbm.1, bf16[2,1024,256]{2,1,0:T(8,128)(2,1)} %frames_hbm.1), custom_call_target="tpu_custom_call" | custom-call | tf_op jit(solution)/shard_map/pallas_call | solution.py:333
  2.2 0.6 %collective-permute-start.3 = (bf16[256,256]{1,0:T(8,128)(2,1)S(1)}, bf16[256,256]{1,0:T(8,128)(2,1)S(1)}, u32[]{:S(2)}, u32[]{:S(2)}) collective-permute-start(bf16[256,256]{1,0:T(8,128)(2,1)S(1)} %get-tuple-element.17), channel_id=1, source_target_pairs={{4,8},{5,9},{0,1},{12,13},{8,4},{9,5},{1,0},{13,12},{6,10},{7,11},... | collective-permute-start | bytes 393224 | tf_op jit(solution)/shard_map/ppermute | solution.py:353
  2.8 4.1 %collective-permute-start = (bf16[256,256]{1,0:T(8,128)(2,1)S(1)}, bf16[256,256]{1,0:T(8,128)(2,1)S(1)}, u32[]{:S(2)}, u32[]{:S(2)}) collective-permute-start(bf16[256,256]{1,0:T(8,128)(2,1)S(1)} %get-tuple-element.13.a_ref), channel_id=1, source_target_pairs={{0,4},{4,0},{8,12},{12,8},{1,5},{5,1},{9,13},{13,9},{2,6},{6,2},{1... | collective-permute-start | bytes 393224 | tf_op jit(solution)/shard_map/ppermute | solution.py:352
  6.9 0.0 collective-permute-done.3.a_ref
  6.9 1.5 %collective-permute-start.4 = (bf16[256,256]{1,0:T(8,128)(2,1)S(1)}, bf16[256,256]{1,0:T(8,128)(2,1)S(1)}, u32[]{:S(2)}, u32[]{:S(2)}) collective-permute-start(bf16[256,256]{1,0:T(8,128)(2,1)S(1)} %collective-permute-done.3.a_ref), channel_id=1, source_target_pairs={{0,2},{2,0},{1,3},{3,1},{4,6},{6,4},{5,7},{7,5},{8,10},{10,8},{9,1... | collective-permute-start | bytes 393224 | tf_op jit(solution)/shard_map/ppermute | solution.py:364
  8.4 1.9 %collective-permute-done.b_ref = bf16[256,256]{1,0:T(8,128)(2,1)S(1)} collective-permute-done((bf16[256,256]{1,0:T(8,128)(2,1)S(1)}, bf16[256,256]{1,0:T(8,128)(2,1)S(1)}, u32[]{:S(2)}, u32[]{:S(2)}) %collective-permute-start) | collective-permute-done | bytes 131104 | tf_op jit(solution)/shard_map/ppermute | solution.py:352
  10.3 3.0 %collective-permute-start.1 = (bf16[256,256]{1,0:T(8,128)(2,1)S(1)}, bf16[256,256]{1,0:T(8,128)(2,1)S(1)}, u32[]{:S(2)}, u32[]{:S(2)}) collective-permute-start(bf16[256,256]{1,0:T(8,128)(2,1)S(1)} %shard_map.74.a_ref), channel_id=1, source_target_pairs={{0,12},{4,8},{8,4},{12,0},{1,13},{5,9},{9,5},{13,1},{2,14},{6,10},... | collective-permute-start | bytes 393224 | tf_op jit(solution)/shard_map/ppermute | solution.py:360
  13.4 0.0 collective-permute-start.5
  13.4 0.0 collective-permute-done.4.b_ref
  13.4 0.5 %collective-permute-start.6 = (bf16[256,256]{1,0:T(8,128)(2,1)S(1)}, bf16[256,256]{1,0:T(8,128)(2,1)S(1)}, u32[]{:S(2)}, u32[]{:S(2)}) collective-permute-start(bf16[256,256]{1,0:T(8,128)(2,1)S(1)} %collective-permute-done.4.b_ref), channel_id=1, source_target_pairs={{0,1},{1,0},{2,3},{3,2},{4,5},{5,4},{6,7},{7,6},{8,9},{9,8},{10,11... | collective-permute-start | bytes 393224 | tf_op jit(solution)/shard_map/ppermute | solution.py:367
  13.9 3.3 %collective-permute-done.1.b_ref = bf16[256,256]{1,0:T(8,128)(2,1)S(1)} collective-permute-done((bf16[256,256]{1,0:T(8,128)(2,1)S(1)}, bf16[256,256]{1,0:T(8,128)(2,1)S(1)}, u32[]{:S(2)}, u32[]{:S(2)}) %collective-permute-start.1) | collective-permute-done | bytes 131104 | tf_op jit(solution)/shard_map/ppermute | solution.py:360
  17.2 1.1 %shard_map.75 = (bf16[256,256]{1,0:T(8,128)(2,1)S(1)}, bf16[256,256]{1,0:T(8,128)(2,1)S(1)}) custom-call(bf16[256,256]{1,0:T(8,128)(2,1)S(1)} %shard_map.74.a_ref, bf16[256,256]{1,0:T(8,128)(2,1)S(1)} %collective-permute-done.1.b_ref, bf16[2,1024,256]{2,1,0:T(8,128)(2,1)S(1)} %get-tuple-element.14.frames_ref), custom_call_target="tpu_custom_call" | custom-call | tf_op jit(solution)/shard_map/pallas_call | solution.py:380
  18.3 2.3 %collective-permute-start.2 = (bf16[256,256]{1,0:T(8,128)(2,1)S(1)}, bf16[256,256]{1,0:T(8,128)(2,1)S(1)}, u32[]{:S(2)}, u32[]{:S(2)}) collective-permute-start(bf16[256,256]{1,0:T(8,128)(2,1)S(1)} %get-tuple-element.15.near_ref), channel_id=1, source_target_pairs={{0,4},{4,0},{8,12},{12,8},{1,5},{5,1},{9,13},{13,9},{2,6},{6,2},{1... | collective-permute-start | bytes 393224 | tf_op jit(solution)/shard_map/ppermute | solution.py:383
  20.6 1.1 %shard_map.76.far_ref = bf16[256,256]{1,0:T(8,128)(2,1)S(1)} custom-call(bf16[256,256]{1,0:T(8,128)(2,1)S(1)} %get-tuple-element.16.features_ref, bf16[2,1024,256]{2,1,0:T(8,128)(2,1)S(1)} %get-tuple-element.14.frames_ref), custom_call_target="tpu_custom_call" | custom-call | tf_op jit(solution)/shard_map/pallas_call | solution.py:385
  21.6 0.0 copy-start
  21.7 1.8 %shard_map.77 = (f32[256,512]{1,0:T(8,128)S(1)}, f32[256,512]{1,0:T(8,128)S(1)}, f32[256,512]{1,0:T(8,128)S(1)}) custom-call(bf16[256,256]{1,0:T(8,128)(2,1)S(1)} %get-tuple-element.16.features_ref, bf16[256,256]{1,0:T(8,128)(2,1)S(1)} %get-tuple-element.15.near_ref, bf16[256,256]{1,0:T(8,128)(2,1)S(1)} %shard_map.76.far_ref, ...), custom_call_target="tpu_custom_call" | custom-call | tf_op jit(solution)/shard_map/pallas_call | solution.py:386
  23.5 1.5 %shard_map.78.far_ref = f32[256,512]{1,0:T(8,128)S(1)} custom-call(f32[256,512]{1,0:T(8,128)S(1)} %get-tuple-element.20.own_ref, bf16[1,512,1024]{2,1,0:T(8,128)(2,1)S(1)} %copy-done, bf16[1,512,1024]{2,1,0:T(8,128)(2,1)S(1)} %collective-permute-done.7.up_b, bf16[1,1024,512]{2,1,0:T(8,128)(2,1)S(1)} %copy-done.1, ...), custom_call_target="tpu_custom_call" | custom-call | tf_op jit(solution)/shard_map/pallas_call | solution.py:390
  25.0 2.0 %shard_map.79.own_ref = bf16[2048,128]{1,0:T(8,128)(2,1)S(1)} custom-call(bf16[256,256]{1,0:T(8,128)(2,1)S(1)} %collective-permute-done.2.halo_ref, f32[256,512]{1,0:T(8,128)S(1)} %get-tuple-element.18.own_ref, f32[256,512]{1,0:T(8,128)S(1)} %get-tuple-element.19.base_ref, bf16[512,512]{1,0:T(8,128)(2,1)S(1)} %copy-done.2, f32[1,1536]{1,0:T(1,128)S(1)} %bitcast.8, ...), custom_call_target="tpu_custom_call" | custom-call | tf_op jit(solution)/shard_map/pallas_call | solution.py:393
  27.0 0.1 collective-permute-start.9
  27.0 0.8 %shard_map.80._ = bf16[4096,128]{1,0:T(8,128)(2,1)} custom-call(bf16[2048,128]{1,0:T(8,128)(2,1)S(1)} %shard_map.79.own_ref), custom_call_target="tpu_custom_call" | custom-call | tf_op jit(solution)/shard_map/pallas_call | solution.py:402
  27.9 1.1 %collective-permute-done.9.other_ref = bf16[2048,128]{1,0:T(8,128)(2,1)S(1)} collective-permute-done((bf16[2048,128]{1,0:T(8,128)(2,1)S(1)}, bf16[2048,128]{1,0:T(8,128)(2,1)S(1)}, u32[]{:S(2)}, u32[]{:S(2)}) %collective-permute-start.9) | collective-permute-done | bytes 524320 | tf_op jit(solution)/shard_map/ppermute | solution.py:399
  28.9 0.8 %shard_map.81 = bf16[4096,128]{1,0:T(8,128)(2,1)} custom-call(bf16[2048,128]{1,0:T(8,128)(2,1)S(1)} %collective-permute-done.9.other_ref, bf16[4096,128]{1,0:T(8,128)(2,1)} %shard_map.80._), custom_call_target="tpu_custom_call", output_to_operand_aliasing={{}: (1, {})} | custom-call | tf_op jit(solution)/shard_map/pallas_call | solution.py:403
  (13 shorter events, 0.0 us)
Async XLA Ops:
  0.0 23.5 %collective-permute-start.7 = (bf16[1,512,1024]{2,1,0:T(8,128)(2,1)}, bf16[1,512,1024]{2,1,0:T(8,128)(2,1)S(1)}, u32[]{:S(2)}, u32[]{:S(2)}) collective-permute-start(bf16[1,512,1024]{2,1,0:T(8,128)(2,1)} %up_a.3), channel_id=1, source_target_pairs={{0,1},{1,0},{2,3},{3,2},{4,5},{5,4},{6,7},{7,6},{8,9},{9,8},{10,11... | collective-permute-start | bytes 3145736 | tf_op jit(solution)/shard_map/ppermute | solution.py:354
  0.5 23.0 %collective-permute-start.8 = (bf16[1,1024,512]{2,1,0:T(8,128)(2,1)}, bf16[1,1024,512]{2,1,0:T(8,128)(2,1)S(1)}, u32[]{:S(2)}, u32[]{:S(2)}) collective-permute-start(bf16[1,1024,512]{2,1,0:T(8,128)(2,1)} %down_a.3), channel_id=1, source_target_pairs={{0,1},{1,0},{2,3},{3,2},{4,5},{5,4},{6,7},{7,6},{8,9},{9,8},{10,11... | collective-permute-start | bytes 3145736 | tf_op jit(solution)/shard_map/ppermute | solution.py:355
  2.2 4.7 %collective-permute-start.3 = (bf16[256,256]{1,0:T(8,128)(2,1)S(1)}, bf16[256,256]{1,0:T(8,128)(2,1)S(1)}, u32[]{:S(2)}, u32[]{:S(2)}) collective-permute-start(bf16[256,256]{1,0:T(8,128)(2,1)S(1)} %get-tuple-element.17), channel_id=1, source_target_pairs={{4,8},{5,9},{0,1},{12,13},{8,4},{9,5},{1,0},{13,12},{6,10},{7,11},... | collective-permute-start | bytes 393224 | tf_op jit(solution)/shard_map/ppermute | solution.py:353
  2.8 7.5 %collective-permute-start = (bf16[256,256]{1,0:T(8,128)(2,1)S(1)}, bf16[256,256]{1,0:T(8,128)(2,1)S(1)}, u32[]{:S(2)}, u32[]{:S(2)}) collective-permute-start(bf16[256,256]{1,0:T(8,128)(2,1)S(1)} %get-tuple-element.13.a_ref), channel_id=1, source_target_pairs={{0,4},{4,0},{8,12},{12,8},{1,5},{5,1},{9,13},{13,9},{2,6},{6,2},{1... | collective-permute-start | bytes 393224 | tf_op jit(solution)/shard_map/ppermute | solution.py:352
  6.9 6.4 %collective-permute-start.4 = (bf16[256,256]{1,0:T(8,128)(2,1)S(1)}, bf16[256,256]{1,0:T(8,128)(2,1)S(1)}, u32[]{:S(2)}, u32[]{:S(2)}) collective-permute-start(bf16[256,256]{1,0:T(8,128)(2,1)S(1)} %collective-permute-done.3.a_ref), channel_id=1, source_target_pairs={{0,2},{2,0},{1,3},{3,1},{4,6},{6,4},{5,7},{7,5},{8,10},{10,8},{9,1... | collective-permute-start | bytes 393224 | tf_op jit(solution)/shard_map/ppermute | solution.py:364
  10.3 6.8 %collective-permute-start.1 = (bf16[256,256]{1,0:T(8,128)(2,1)S(1)}, bf16[256,256]{1,0:T(8,128)(2,1)S(1)}, u32[]{:S(2)}, u32[]{:S(2)}) collective-permute-start(bf16[256,256]{1,0:T(8,128)(2,1)S(1)} %shard_map.74.a_ref), channel_id=1, source_target_pairs={{0,12},{4,8},{8,4},{12,0},{1,13},{5,9},{9,5},{13,1},{2,14},{6,10},... | collective-permute-start | bytes 393224 | tf_op jit(solution)/shard_map/ppermute | solution.py:360
  13.4 8.3 %collective-permute-start.5 = (bf16[256,256]{1,0:T(8,128)(2,1)S(1)}, bf16[256,256]{1,0:T(8,128)(2,1)S(1)}, u32[]{:S(2)}, u32[]{:S(2)}) collective-permute-start(bf16[256,256]{1,0:T(8,128)(2,1)S(1)} %collective-permute-done.3.a_ref), channel_id=1, source_target_pairs={{0,1},{1,0},{2,3},{3,2},{4,5},{5,4},{6,7},{7,6},{8,9},{9,8},{10,11... | collective-permute-start | bytes 393224 | tf_op jit(solution)/shard_map/ppermute | solution.py:366
  13.4 8.3 %collective-permute-start.6 = (bf16[256,256]{1,0:T(8,128)(2,1)S(1)}, bf16[256,256]{1,0:T(8,128)(2,1)S(1)}, u32[]{:S(2)}, u32[]{:S(2)}) collective-permute-start(bf16[256,256]{1,0:T(8,128)(2,1)S(1)} %collective-permute-done.4.b_ref), channel_id=1, source_target_pairs={{0,1},{1,0},{2,3},{3,2},{4,5},{5,4},{6,7},{7,6},{8,9},{9,8},{10,11... | collective-permute-start | bytes 393224 | tf_op jit(solution)/shard_map/ppermute | solution.py:367
  17.2 4.5 %copy-start.2 = (bf16[512,512]{1,0:T(8,128)(2,1)S(1)}, bf16[512,512]{1,0:T(8,128)(2,1)}, u32[]{:S(2)}) copy-start(bf16[512,512]{1,0:T(8,128)(2,1)} %in_ref.3) | copy-start | bytes 1572868
  18.3 6.7 %collective-permute-start.2 = (bf16[256,256]{1,0:T(8,128)(2,1)S(1)}, bf16[256,256]{1,0:T(8,128)(2,1)S(1)}, u32[]{:S(2)}, u32[]{:S(2)}) collective-permute-start(bf16[256,256]{1,0:T(8,128)(2,1)S(1)} %get-tuple-element.15.near_ref), channel_id=1, source_target_pairs={{0,4},{4,0},{8,12},{12,8},{1,5},{5,1},{9,13},{13,9},{2,6},{6,2},{1... | collective-permute-start | bytes 393224 | tf_op jit(solution)/shard_map/ppermute | solution.py:383
  20.6 1.1 %copy-start.3 = (f32[1,3,512]{2,0,1:T(1,128)S(1)}, f32[1,3,512]{2,0,1:T(1,128)}, u32[]{:S(2)}) copy-start(f32[1,3,512]{2,0,1:T(1,128)} %param.11) | copy-start | bytes 18436
  20.6 2.9 %copy-start.1 = (bf16[1,1024,512]{2,1,0:T(8,128)(2,1)S(1)}, bf16[1,1024,512]{2,1,0:T(8,128)(2,1)}, u32[]{:S(2)}) copy-start(bf16[1,1024,512]{2,1,0:T(8,128)(2,1)} %down_a.3) | copy-start | bytes 3145732
  21.6 1.9 %copy-start = (bf16[1,512,1024]{2,1,0:T(8,128)(2,1)S(1)}, bf16[1,512,1024]{2,1,0:T(8,128)(2,1)}, u32[]{:S(2)}) copy-start(bf16[1,512,1024]{2,1,0:T(8,128)(2,1)} %up_a.3) | copy-start | bytes 3145732
  27.0 2.0 %collective-permute-start.9 = (bf16[2048,128]{1,0:T(8,128)(2,1)S(1)}, bf16[2048,128]{1,0:T(8,128)(2,1)S(1)}, u32[]{:S(2)}, u32[]{:S(2)}) collective-permute-start(bf16[2048,128]{1,0:T(8,128)(2,1)S(1)} %shard_map.79.own_ref), channel_id=1, source_target_pairs={{0,1},{1,0},{2,3},{3,2},{4,5},{5,4},{6,7},{7,6},{8,9},{9,8},{10,11... | collective-permute-start | bytes 1572872 | tf_op jit(solution)/shard_map/ppermute | solution.py:399

commit v7 on v6

--- a/solution.py
+++ b/solution.py
@@ -46,10 +46,6 @@
 
 def dot(a, b):
     return jnp.dot(a, b, preferred_element_type=F32)
-
-
-def dot_t(a, b):
-    return lax.dot_general(a, b, (((1,), (1,)), ((), ())), preferred_element_type=F32)
 
 
 def my_part(whole, part, parts):
@@ -150,46 +146,62 @@
     out_ref[...] = a_ref[...] + b_ref[...]
 
 
-def attend(features, maps, scale, scratch):
+def attend_split(features, blocks, scale, scratch):
+    rows, size = features.shape
+    sums = [pltpu.ACC(k % 2)((rows, size), F32) for k in range(len(blocks))]
+    return pl.run_scoped(functools.partial(attend_units, features, blocks, scale, scratch), *sums)
+
+
+def attend_units(features, blocks, scale, scratch, *sums):
     score_ref, weight_ref, sum_ref = scratch
-    rows = features.shape[0]
+    rows, size = features.shape
     step = 32
-    for k, blocks in enumerate(maps):
-        at = 0
-        for block in blocks:
-            score_ref[k, :, at : at + block.shape[0]] = dot_t(features, block[...])
-            at += block.shape[0]
-    for k in range(len(maps)):
-        for at in range(0, rows, step):
-            scores = score_ref[k, at : at + step, :]
-            peak = jnp.max(scores, axis=-1, keepdims=True)
-            expd = jnp.exp2((scores - peak) * scale)
-            total = jnp.sum(expd, axis=-1, keepdims=True)
-            sum_ref[k, at : at + step, :] = jnp.broadcast_to(total, (step, LANES))
-            weight_ref[k, at : at + step, :] = expd.astype(BF16)
-    out = []
-    for k, blocks in enumerate(maps):
-        at = 0
-        pooled = None
-        for block in blocks:
-            part = dot(weight_ref[k, :, at : at + block.shape[0]], block[...])
-            pooled = part if pooled is None else pooled + part
-            at += block.shape[0]
-        total = sum_ref[k, :, :1]
-        mean = jnp.mean(pooled * pooled, axis=-1, keepdims=True)
-        out.append((pooled * lax.rsqrt(mean + 1e-6 * total * total)).astype(BF16))
-    return out
+    for j, block in enumerate(blocks):
+        unit, slot = j % 2, j // 2
+        at = j * size
+        acc = sums[j]
+        pltpu.matmul_push_rhs(block[...], slot % 2, unit, transpose=True)
+        pltpu.matmul_acc_lhs(acc, features, load_staged_rhs=slot % 2)
+        score_ref[0, :, at : at + size] = pltpu.matmul_pop(acc)
+    for at in range(0, rows, step):
+        scores = score_ref[0, at : at + step, :]
+        peak = jnp.max(scores, axis=-1, keepdims=True)
+        expd = jnp.exp2((scores - peak) * scale)
+        total = jnp.sum(expd, axis=-1, keepdims=True)
+        sum_ref[0, at : at + step, :] = jnp.broadcast_to(total, (step, LANES))
+        weight_ref[0, at : at + step, :] = expd.astype(BF16)
+    for j, block in enumerate(blocks):
+        unit, slot = j % 2, j // 2
+        at = j * size
+        pltpu.matmul_push_rhs(block[...], slot % 2, unit)
+        pltpu.matmul_acc_lhs(
+            sums[unit], weight_ref[0, :, at : at + size], load_staged_rhs=slot % 2
+        )
+    pooled = pltpu.matmul_pop(sums[0]) + pltpu.matmul_pop(sums[1])
+    total = sum_ref[0, :, :1]
+    mean = jnp.mean(pooled * pooled, axis=-1, keepdims=True)
+    return (pooled * lax.rsqrt(mean + 1e-6 * total * total)).astype(BF16)
+
+
+def blocks_of(frames_ref, t):
+    size = frames_ref.shape[2]
+    return [frames_ref.at[t, pl.ds(at, size)] for at in range(0, frames_ref.shape[1], size)]
 
 
 def near_body(scale, a_ref, b_ref, frames_ref, features_ref, normed_ref, *scratch):
     features = a_ref[...] + b_ref[...]
     features_ref[...] = features
-    (normed_ref[...],) = attend(features, [[frames_ref.at[near_frame()]]], scale, scratch)
+    normed_ref[...] = attend_split(features, blocks_of(frames_ref, near_frame()), scale, scratch)
 
 
 def far_body(scale, features_ref, frames_ref, normed_ref, *scratch):
-    maps = [[frames_ref.at[1 - near_frame()]]]
-    (normed_ref[...],) = attend(features_ref[...], maps, scale, scratch)
+    blocks = blocks_of(frames_ref, 1 - near_frame())
+    normed_ref[...] = attend_split(features_ref[...], blocks, scale, scratch)
+
+
+def halo_body(scale, features_ref, a_ref, b_ref, c_ref, d_ref, normed_ref, *scratch):
+    blocks = [a_ref, b_ref, c_ref, d_ref]
+    normed_ref[...] = attend_split(features_ref[...], blocks, scale, scratch)
 
 
 def taps_of(taps_ref):
@@ -199,38 +211,22 @@
     return jnp.where(even, last, first), middle, jnp.where(even, first, last)
 
 
-def own_body(
-    devices,
-    scale,
-    features_ref,
-    near_ref,
-    far_ref,
-    a_ref,
-    b_ref,
-    c_ref,
-    d_ref,
-    in_ref,
-    taps_ref,
-    base_ref,
-    near_out,
-    far_out,
-    *scratch,
-):
-    features = features_ref[...]
-    channels = features.shape[1]
+def own_body(features_ref, near_ref, far_ref, in_ref, taps_ref, base_ref, near_out, far_out):
+    channels = features_ref.shape[1]
     near_tap, middle, far_tap = taps_of(taps_ref)
-    place = lax.axis_index("frame")
-    inside = jnp.where(is_even(), place > 0, place < devices - 1)
-    base = dot(features, in_ref[channels:, :])
+    base = dot(features_ref[...], in_ref[channels:, :])
     base_ref[...] = base
     near = dot(near_ref[...], in_ref[:channels, :]) + base
     far = dot(far_ref[...], in_ref[:channels, :]) + base
     near_level, far_level = level_of(near), level_of(far)
     near_out[...] = near + middle * near_level + far_tap * far_level
     far_out[...] = far + middle * far_level + near_tap * near_level
-    (halo,) = attend(features, [[a_ref, b_ref, c_ref, d_ref]], scale, scratch)
-    halo = level_of(dot(halo, in_ref[:channels, :]) + base_ref[...])
-    far_out[...] += jnp.where(inside, far_tap, 0.0) * halo
+
+
+def with_halo(halo_ref, own_ref, base_ref, in_ref, tap, inside):
+    channels = halo_ref.shape[1]
+    halo = level_of(dot(halo_ref[...], in_ref[:channels, :]) + base_ref[...])
+    return own_ref[...] + jnp.where(inside, tap, 0.0) * halo
 
 
 def mix(stream, ups, downs, hidden_ref):
@@ -254,8 +250,14 @@
     return stream + 0.5 * total
 
 
-def mix_far_body(own_ref, up_a, up_b, down_a, down_b, out_ref, hidden_ref):
-    out_ref[...] = mix(own_ref[...], (up_a, up_b), (down_a, down_b), hidden_ref)
+def mix_far_body(
+    devices, halo_ref, own_ref, base_ref, in_ref, taps_ref, up_a, up_b, down_a, down_b, out_ref, hidden_ref
+):
+    place = lax.axis_index("frame")
+    inside = jnp.where(is_even(), place > 0, place < devices - 1)
+    _, _, tap = taps_of(taps_ref)
+    stream = with_halo(halo_ref, own_ref, base_ref, in_ref, tap, inside)
+    out_ref[...] = mix(stream, (up_a, up_b), (down_a, down_b), hidden_ref)
 
 
 def mix_near_body(
@@ -274,13 +276,11 @@
     hidden_ref,
     line_ref,
 ):
-    channels = halo_ref.shape[1]
     place = lax.axis_index("frame")
     even = is_even()
     inside = jnp.logical_not(even) | (place < devices - 1)
     tap, _, _ = taps_of(taps_ref)
-    halo = level_of(dot(halo_ref[...], in_ref[:channels, :]) + base_ref[...])
-    stream = own_ref[...] + jnp.where(inside, tap, 0.0) * halo
+    stream = with_halo(halo_ref, own_ref, base_ref, in_ref, tap, inside)
     near = mix(stream, (up_a, up_b), (down_a, down_b), hidden_ref)
     far = far_ref[...]
     rows, width = far.shape
@@ -383,11 +383,12 @@
     near_halo = lax.ppermute(near, "frame", flips(1))
     near_halo = held(near_halo)
     far = call(functools.partial(far_body, scale), small, 2, attention(1))(features, frames)
-    base, own_near, own_far = call(
-        functools.partial(own_body, devices, scale), (wide,) * 3, 9, attention(1)
-    )(features, near, far, *outers, in_weight, taps)
+    base, own_near, own_far = call(own_body, (wide,) * 3, 5)(features, near, far, in_weight, taps)
+    far_halo = call(functools.partial(halo_body, scale), small, 5, attention(1))(features, *outers)
     hidden = pltpu.VMEM((rows, parts * units), BF16)
-    far = call(mix_far_body, wide, 5, (hidden,))(own_far, *weights)
+    far = call(functools.partial(mix_far_body, devices), wide, 9, (hidden,))(
+        far_halo, own_far, base, in_weight, taps, *weights
+    )
     blocks = width // LANES
     lines = rows * blocks * frame_count
     own = call(

time: 29.9 us -> 29.7 us (level)
  Pallas kernels: 10.7 us -> 10.4 us
    pallas_call x2 -> x3, Pallas kernels: 3.23 us -> 3.3 us  [the longest x1 1.8 us: on_device(): call(functools.partial(mix_far_body, devices), wide, 9, (hidden,))]
  transfers between devices with their start and end apart: 10 -> 10, of which waited for: 3 -> 3; matrix products, arithmetic and copies ran while one was open for 0% -> 0% of each run, Pallas kernels for 27% -> 26%
where the time goes in v7:
time: 29.7 us; the launch traced here: 29.5 us
  starting transfers between devices  12.6 us (42%)
  Pallas kernels  10.4 us (35%)
  waiting for transfers between devices  6.24 us (21%)
    ppermute x1, starting transfers between devices, on_device(): theirs = lax.ppermute(mine, 'frame', flips(masks[0]))  4.14 us
    ppermute x1, waiting for transfers between devices, on_device(): theirs = lax.ppermute(mine, 'frame', flips(mask))  3.27 us
    ppermute x1, starting transfers between devices, on_device(): theirs = lax.ppermute(mine, 'frame', flips(mask))  3.04 us
    ppermute x1, starting transfers between devices, on_device(): near_halo = lax.ppermute(near, 'frame', flips(1))  2.31 us
    pallas_call x1, Pallas kernels, on_device(): call(functools.partial(mix_near_body, devices), kept((lines, LANES), BF16...  1.95 us
    ppermute x1, waiting for transfers between devices, on_device(): theirs = lax.ppermute(mine, 'frame', flips(masks[0]))  1.89 us
    pallas_call x1, Pallas kernels, on_device(): call(functools.partial(mix_far_body, devices), wide, 9, (hidden,))  1.8 us
    pallas_call x1, Pallas kernels, on_device(): call(functools.partial(pick_body, parts), (kept((rows, channels), BF16),...  1.72 us
  transfers between devices with their start and end apart: 10, of which 3 were waited for; matrix products, arithmetic and copies ran while one was open for 0% of the time, Pallas kernels for 26%

profile of v7, /device:TPU:0, one launch (start us, length us, event | category | flops | bytes accessed | tf_op | source)
XLA Modules:
  0.0 29.5 jit_solution(15956770964333984792)
XLA Ops:
  0.0 0.5 %collective-permute-start.3 = (bf16[1,512,1024]{2,1,0:T(8,128)(2,1)}, bf16[1,512,1024]{2,1,0:T(8,128)(2,1)S(1)}, u32[]{:S(2)}, u32[]{:S(2)}) collective-permute-start(bf16[1,512,1024]{2,1,0:T(8,128)(2,1)} %up_a.3), channel_id=1, source_target_pairs={{0,1},{1,0},{2,3},{3,2},{4,5},{5,4},{6,7},{7,6},{8,9},{9,8},{10,11... | collective-permute-start | bytes 3145736 | tf_op jit(solution)/shard_map/ppermute | solution.py:354
  0.5 0.0 collective-permute-start.4
  0.5 1.7 %shard_map.73 = (bf16[256,256]{1,0:T(8,128)(2,1)S(1)}, bf16[2,1024,256]{2,1,0:T(8,128)(2,1)S(1)}, bf16[256,256]{1,0:T(8,128)(2,1)S(1)}) custom-call(s32[1,512]{1,0:T(1,128)} %bitcast.10, s32[2,512]{1,0:T(2,128)} %pixel_hbm.1, bf16[2,1024,256]{2,1,0:T(8,128)(2,1)} %frames_hbm.1), custom_call_target="tpu_custom_call" | custom-call | tf_op jit(solution)/shard_map/pallas_call | solution.py:333
  2.2 0.6 %collective-permute-start.5 = (bf16[256,256]{1,0:T(8,128)(2,1)S(1)}, bf16[256,256]{1,0:T(8,128)(2,1)S(1)}, u32[]{:S(2)}, u32[]{:S(2)}) collective-permute-start(bf16[256,256]{1,0:T(8,128)(2,1)S(1)} %get-tuple-element.19), channel_id=1, source_target_pairs={{4,8},{5,9},{0,1},{12,13},{8,4},{9,5},{1,0},{13,12},{6,10},{7,11},... | collective-permute-start | bytes 393224 | tf_op jit(solution)/shard_map/ppermute | solution.py:353
  2.8 4.1 %collective-permute-start = (bf16[256,256]{1,0:T(8,128)(2,1)S(1)}, bf16[256,256]{1,0:T(8,128)(2,1)S(1)}, u32[]{:S(2)}, u32[]{:S(2)}) collective-permute-start(bf16[256,256]{1,0:T(8,128)(2,1)S(1)} %get-tuple-element.13.a_ref), channel_id=1, source_target_pairs={{0,4},{4,0},{8,12},{12,8},{1,5},{5,1},{9,13},{13,9},{2,6},{6,2},{1... | collective-permute-start | bytes 393224 | tf_op jit(solution)/shard_map/ppermute | solution.py:352
  6.9 0.0 collective-permute-done.5.a_ref
  6.9 1.5 %collective-permute-start.6 = (bf16[256,256]{1,0:T(8,128)(2,1)S(1)}, bf16[256,256]{1,0:T(8,128)(2,1)S(1)}, u32[]{:S(2)}, u32[]{:S(2)}) collective-permute-start(bf16[256,256]{1,0:T(8,128)(2,1)S(1)} %collective-permute-done.5.a_ref), channel_id=1, source_target_pairs={{0,2},{2,0},{1,3},{3,1},{4,6},{6,4},{5,7},{7,5},{8,10},{10,8},{9,1... | collective-permute-start | bytes 393224 | tf_op jit(solution)/shard_map/ppermute | solution.py:364
  8.4 1.9 %collective-permute-done.b_ref = bf16[256,256]{1,0:T(8,128)(2,1)S(1)} collective-permute-done((bf16[256,256]{1,0:T(8,128)(2,1)S(1)}, bf16[256,256]{1,0:T(8,128)(2,1)S(1)}, u32[]{:S(2)}, u32[]{:S(2)}) %collective-permute-start) | collective-permute-done | bytes 131104 | tf_op jit(solution)/shard_map/ppermute | solution.py:352
  10.3 3.0 %collective-permute-start.1 = (bf16[256,256]{1,0:T(8,128)(2,1)S(1)}, bf16[256,256]{1,0:T(8,128)(2,1)S(1)}, u32[]{:S(2)}, u32[]{:S(2)}) collective-permute-start(bf16[256,256]{1,0:T(8,128)(2,1)S(1)} %shard_map.74.a_ref), channel_id=1, source_target_pairs={{0,12},{4,8},{8,4},{12,0},{1,13},{5,9},{9,5},{13,1},{2,14},{6,10},... | collective-permute-start | bytes 393224 | tf_op jit(solution)/shard_map/ppermute | solution.py:360
  13.4 0.5 %collective-permute-start.8 = (bf16[256,256]{1,0:T(8,128)(2,1)S(1)}, bf16[256,256]{1,0:T(8,128)(2,1)S(1)}, u32[]{:S(2)}, u32[]{:S(2)}) collective-permute-start(bf16[256,256]{1,0:T(8,128)(2,1)S(1)} %collective-permute-done.6.b_ref), channel_id=1, source_target_pairs={{0,1},{1,0},{2,3},{3,2},{4,5},{5,4},{6,7},{7,6},{8,9},{9,8},{10,11... | collective-permute-start | bytes 393224 | tf_op jit(solution)/shard_map/ppermute | solution.py:367
  13.9 3.3 %collective-permute-done.1.b_ref = bf16[256,256]{1,0:T(8,128)(2,1)S(1)} collective-permute-done((bf16[256,256]{1,0:T(8,128)(2,1)S(1)}, bf16[256,256]{1,0:T(8,128)(2,1)S(1)}, u32[]{:S(2)}, u32[]{:S(2)}) %collective-permute-start.1) | collective-permute-done | bytes 131104 | tf_op jit(solution)/shard_map/ppermute | solution.py:360
  17.2 0.9 %shard_map.75 = (bf16[256,256]{1,0:T(8,128)(2,1)S(1)}, bf16[256,256]{1,0:T(8,128)(2,1)S(1)}) custom-call(bf16[256,256]{1,0:T(8,128)(2,1)S(1)} %shard_map.74.a_ref, bf16[256,256]{1,0:T(8,128)(2,1)S(1)} %collective-permute-done.1.b_ref, bf16[2,1024,256]{2,1,0:T(8,128)(2,1)S(1)} %get-tuple-element.14.frames_ref), custom_call_target="tpu_custom_call" | custom-call | tf_op jit(solution)/shard_map/pallas_call | solution.py:380
  18.0 2.3 %collective-permute-start.2 = (bf16[256,256]{1,0:T(8,128)(2,1)S(1)}, bf16[256,256]{1,0:T(8,128)(2,1)S(1)}, u32[]{:S(2)}, u32[]{:S(2)}) collective-permute-start(bf16[256,256]{1,0:T(8,128)(2,1)S(1)} %get-tuple-element.15.near_ref), channel_id=1, source_target_pairs={{0,4},{4,0},{8,12},{12,8},{1,5},{5,1},{9,13},{13,9},{2,6},{6,2},{1... | collective-permute-start | bytes 393224 | tf_op jit(solution)/shard_map/ppermute | solution.py:383
  20.4 0.9 %shard_map.76.far_ref = bf16[256,256]{1,0:T(8,128)(2,1)S(1)} custom-call(bf16[256,256]{1,0:T(8,128)(2,1)S(1)} %get-tuple-element.16.features_ref, bf16[2,1024,256]{2,1,0:T(8,128)(2,1)S(1)} %get-tuple-element.14.frames_ref), custom_call_target="tpu_custom_call" | custom-call | tf_op jit(solution)/shard_map/pallas_call | solution.py:385
  21.2 0.0 copy-start.1
  21.3 0.1 copy-done
  21.4 0.6 %shard_map.77 = (f32[256,512]{1,0:T(8,128)S(1)}, f32[256,512]{1,0:T(8,128)S(1)}, f32[256,512]{1,0:T(8,128)S(1)}) custom-call(bf16[256,256]{1,0:T(8,128)(2,1)S(1)} %get-tuple-element.16.features_ref, bf16[256,256]{1,0:T(8,128)(2,1)S(1)} %get-tuple-element.15.near_ref, bf16[256,256]{1,0:T(8,128)(2,1)S(1)} %shard_map.76.far_ref, bf16[512,512]{1,0:T(8,128)(2,1)S(1)} %copy-done, ...), custom_call_target="tpu_custom_call" | custom-call | tf_op jit(solution)/shard_map/pallas_call | solution.py:386
  22.1 0.9 %shard_map.78.halo_ref = bf16[256,256]{1,0:T(8,128)(2,1)S(1)} custom-call(bf16[256,256]{1,0:T(8,128)(2,1)S(1)} %get-tuple-element.16.features_ref, bf16[256,256]{1,0:T(8,128)(2,1)S(1)} %collective-permute-done.5.a_ref, bf16[256,256]{1,0:T(8,128)(2,1)S(1)} %collective-permute-done.6.b_ref, bf16[256,256]{1,0:T(8,128)(2,1)S(1)} %collective-permute-done.7.c_ref, ...), custom_call_target="tpu_custom_call" | custom-call | tf_op jit(solution)/shard_map/pallas_call | solution.py:387
  23.0 1.8 %shard_map.79.far_ref = f32[256,512]{1,0:T(8,128)S(1)} custom-call(bf16[256,256]{1,0:T(8,128)(2,1)S(1)} %shard_map.78.halo_ref, f32[256,512]{1,0:T(8,128)S(1)} %get-tuple-element.20.own_ref, f32[256,512]{1,0:T(8,128)S(1)} %get-tuple-element.18.base_ref, bf16[512,512]{1,0:T(8,128)(2,1)S(1)} %copy-done, f32[1,1536]{1,0:T(1,128)S(1)} %bitcast.8, ...), custom_call_target="tpu_custom_call" | custom-call | tf_op jit(solution)/shard_map/pallas_call | solution.py:389
  24.8 1.9 %shard_map.80.own_ref = bf16[2048,128]{1,0:T(8,128)(2,1)S(1)} custom-call(bf16[256,256]{1,0:T(8,128)(2,1)S(1)} %collective-permute-done.2.halo_ref, f32[256,512]{1,0:T(8,128)S(1)} %get-tuple-element.17.own_ref, f32[256,512]{1,0:T(8,128)S(1)} %get-tuple-element.18.base_ref, bf16[512,512]{1,0:T(8,128)(2,1)S(1)} %copy-done, f32[1,1536]{1,0:T(1,128)S(1)} %bitcast.9, ...), custom_call_target="tpu_custom_call" | custom-call | tf_op jit(solution)/shard_map/pallas_call | solution.py:394
  26.8 0.1 collective-permute-start.9
  26.8 0.8 %shard_map.81._ = bf16[4096,128]{1,0:T(8,128)(2,1)} custom-call(bf16[2048,128]{1,0:T(8,128)(2,1)S(1)} %shard_map.80.own_ref), custom_call_target="tpu_custom_call" | custom-call | tf_op jit(solution)/shard_map/pallas_call | solution.py:403
  27.7 1.1 %collective-permute-done.9.other_ref = bf16[2048,128]{1,0:T(8,128)(2,1)S(1)} collective-permute-done((bf16[2048,128]{1,0:T(8,128)(2,1)S(1)}, bf16[2048,128]{1,0:T(8,128)(2,1)S(1)}, u32[]{:S(2)}, u32[]{:S(2)}) %collective-permute-start.9) | collective-permute-done | bytes 524320 | tf_op jit(solution)/shard_map/ppermute | solution.py:400
  28.7 0.8 %shard_map.82 = bf16[4096,128]{1,0:T(8,128)(2,1)} custom-call(bf16[2048,128]{1,0:T(8,128)(2,1)S(1)} %collective-permute-done.9.other_ref, bf16[4096,128]{1,0:T(8,128)(2,1)} %shard_map.81._), custom_call_target="tpu_custom_call", output_to_operand_aliasing={{}: (1, {})} | custom-call | tf_op jit(solution)/shard_map/pallas_call | solution.py:404
  (14 shorter events, 0.0 us)
Async XLA Ops:
  0.0 22.9 %collective-permute-start.3 = (bf16[1,512,1024]{2,1,0:T(8,128)(2,1)}, bf16[1,512,1024]{2,1,0:T(8,128)(2,1)S(1)}, u32[]{:S(2)}, u32[]{:S(2)}) collective-permute-start(bf16[1,512,1024]{2,1,0:T(8,128)(2,1)} %up_a.3), channel_id=1, source_target_pairs={{0,1},{1,0},{2,3},{3,2},{4,5},{5,4},{6,7},{7,6},{8,9},{9,8},{10,11... | collective-permute-start | bytes 3145736 | tf_op jit(solution)/shard_map/ppermute | solution.py:354
  0.5 22.5 %collective-permute-start.4 = (bf16[1,1024,512]{2,1,0:T(8,128)(2,1)}, bf16[1,1024,512]{2,1,0:T(8,128)(2,1)S(1)}, u32[]{:S(2)}, u32[]{:S(2)}) collective-permute-start(bf16[1,1024,512]{2,1,0:T(8,128)(2,1)} %down_a.3), channel_id=1, source_target_pairs={{0,1},{1,0},{2,3},{3,2},{4,5},{5,4},{6,7},{7,6},{8,9},{9,8},{10,11... | collective-permute-start | bytes 3145736 | tf_op jit(solution)/shard_map/ppermute | solution.py:355
  2.2 4.7 %collective-permute-start.5 = (bf16[256,256]{1,0:T(8,128)(2,1)S(1)}, bf16[256,256]{1,0:T(8,128)(2,1)S(1)}, u32[]{:S(2)}, u32[]{:S(2)}) collective-permute-start(bf16[256,256]{1,0:T(8,128)(2,1)S(1)} %get-tuple-element.19), channel_id=1, source_target_pairs={{4,8},{5,9},{0,1},{12,13},{8,4},{9,5},{1,0},{13,12},{6,10},{7,11},... | collective-permute-start | bytes 393224 | tf_op jit(solution)/shard_map/ppermute | solution.py:353
  2.8 7.5 %collective-permute-start = (bf16[256,256]{1,0:T(8,128)(2,1)S(1)}, bf16[256,256]{1,0:T(8,128)(2,1)S(1)}, u32[]{:S(2)}, u32[]{:S(2)}) collective-permute-start(bf16[256,256]{1,0:T(8,128)(2,1)S(1)} %get-tuple-element.13.a_ref), channel_id=1, source_target_pairs={{0,4},{4,0},{8,12},{12,8},{1,5},{5,1},{9,13},{13,9},{2,6},{6,2},{1... | collective-permute-start | bytes 393224 | tf_op jit(solution)/shard_map/ppermute | solution.py:352
  6.9 6.4 %collective-permute-start.6 = (bf16[256,256]{1,0:T(8,128)(2,1)S(1)}, bf16[256,256]{1,0:T(8,128)(2,1)S(1)}, u32[]{:S(2)}, u32[]{:S(2)}) collective-permute-start(bf16[256,256]{1,0:T(8,128)(2,1)S(1)} %collective-permute-done.5.a_ref), channel_id=1, source_target_pairs={{0,2},{2,0},{1,3},{3,1},{4,6},{6,4},{5,7},{7,5},{8,10},{10,8},{9,1... | collective-permute-start | bytes 393224 | tf_op jit(solution)/shard_map/ppermute | solution.py:364
  10.3 6.8 %collective-permute-start.1 = (bf16[256,256]{1,0:T(8,128)(2,1)S(1)}, bf16[256,256]{1,0:T(8,128)(2,1)S(1)}, u32[]{:S(2)}, u32[]{:S(2)}) collective-permute-start(bf16[256,256]{1,0:T(8,128)(2,1)S(1)} %shard_map.74.a_ref), channel_id=1, source_target_pairs={{0,12},{4,8},{8,4},{12,0},{1,13},{5,9},{9,5},{13,1},{2,14},{6,10},... | collective-permute-start | bytes 393224 | tf_op jit(solution)/shard_map/ppermute | solution.py:360
  13.4 8.7 %collective-permute-start.7 = (bf16[256,256]{1,0:T(8,128)(2,1)S(1)}, bf16[256,256]{1,0:T(8,128)(2,1)S(1)}, u32[]{:S(2)}, u32[]{:S(2)}) collective-permute-start(bf16[256,256]{1,0:T(8,128)(2,1)S(1)} %collective-permute-done.5.a_ref), channel_id=1, source_target_pairs={{0,1},{1,0},{2,3},{3,2},{4,5},{5,4},{6,7},{7,6},{8,9},{9,8},{10,11... | collective-permute-start | bytes 393224 | tf_op jit(solution)/shard_map/ppermute | solution.py:366
  13.4 8.7 %collective-permute-start.8 = (bf16[256,256]{1,0:T(8,128)(2,1)S(1)}, bf16[256,256]{1,0:T(8,128)(2,1)S(1)}, u32[]{:S(2)}, u32[]{:S(2)}) collective-permute-start(bf16[256,256]{1,0:T(8,128)(2,1)S(1)} %collective-permute-done.6.b_ref), channel_id=1, source_target_pairs={{0,1},{1,0},{2,3},{3,2},{4,5},{5,4},{6,7},{7,6},{8,9},{9,8},{10,11... | collective-permute-start | bytes 393224 | tf_op jit(solution)/shard_map/ppermute | solution.py:367
  17.2 4.1 %copy-start.3 = (f32[1,3,512]{2,0,1:T(1,128)S(1)}, f32[1,3,512]{2,0,1:T(1,128)}, u32[]{:S(2)}) copy-start(f32[1,3,512]{2,0,1:T(1,128)} %param.11) | copy-start | bytes 18436
  18.0 6.7 %collective-permute-start.2 = (bf16[256,256]{1,0:T(8,128)(2,1)S(1)}, bf16[256,256]{1,0:T(8,128)(2,1)S(1)}, u32[]{:S(2)}, u32[]{:S(2)}) collective-permute-start(bf16[256,256]{1,0:T(8,128)(2,1)S(1)} %get-tuple-element.15.near_ref), channel_id=1, source_target_pairs={{0,4},{4,0},{8,12},{12,8},{1,5},{5,1},{9,13},{13,9},{2,6},{6,2},{1... | collective-permute-start | bytes 393224 | tf_op jit(solution)/shard_map/ppermute | solution.py:383
  20.4 1.0 %copy-start = (bf16[512,512]{1,0:T(8,128)(2,1)S(1)}, bf16[512,512]{1,0:T(8,128)(2,1)}, u32[]{:S(2)}) copy-start(bf16[512,512]{1,0:T(8,128)(2,1)} %in_ref.5) | copy-start | bytes 1572868
  20.4 2.6 %copy-start.2 = (bf16[1,1024,512]{2,1,0:T(8,128)(2,1)S(1)}, bf16[1,1024,512]{2,1,0:T(8,128)(2,1)}, u32[]{:S(2)}) copy-start(bf16[1,1024,512]{2,1,0:T(8,128)(2,1)} %down_a.3) | copy-start | bytes 3145732
  21.2 1.7 %copy-start.1 = (bf16[1,512,1024]{2,1,0:T(8,128)(2,1)S(1)}, bf16[1,512,1024]{2,1,0:T(8,128)(2,1)}, u32[]{:S(2)}) copy-start(bf16[1,512,1024]{2,1,0:T(8,128)(2,1)} %up_a.3) | copy-start | bytes 3145732
  26.8 2.0 %collective-permute-start.9 = (bf16[2048,128]{1,0:T(8,128)(2,1)S(1)}, bf16[2048,128]{1,0:T(8,128)(2,1)S(1)}, u32[]{:S(2)}, u32[]{:S(2)}) collective-permute-start(bf16[2048,128]{1,0:T(8,128)(2,1)S(1)} %shard_map.80.own_ref), channel_id=1, source_target_pairs={{0,1},{1,0},{2,3},{3,2},{4,5},{5,4},{6,7},{7,6},{8,9},{9,8},{10,11... | collective-permute-start | bytes 1572872 | tf_op jit(solution)/shard_map/ppermute | solution.py:400

commit v8 on v7

--- a/solution.py
+++ b/solution.py
@@ -199,9 +199,22 @@
     normed_ref[...] = attend_split(features_ref[...], blocks, scale, scratch)
 
 
-def halo_body(scale, features_ref, a_ref, b_ref, c_ref, d_ref, normed_ref, *scratch):
-    blocks = [a_ref, b_ref, c_ref, d_ref]
-    normed_ref[...] = attend_split(features_ref[...], blocks, scale, scratch)
+def has_outer(devices):
+    place = lax.axis_index("frame")
+    return jnp.where(is_even(), place > 0, place < devices - 1)
+
+
+def halo_body(devices, scale, features_ref, a_ref, b_ref, c_ref, d_ref, normed_ref, *scratch):
+    inside = has_outer(devices)
+
+    @pl.when(inside)
+    def _():
+        blocks = [a_ref, b_ref, c_ref, d_ref]
+        normed_ref[...] = attend_split(features_ref[...], blocks, scale, scratch)
+
+    @pl.when(jnp.logical_not(inside))
+    def _():
+        normed_ref[...] = jnp.zeros_like(normed_ref)
 
 
 def taps_of(taps_ref):
@@ -253,11 +266,15 @@
 def mix_far_body(
     devices, halo_ref, own_ref, base_ref, in_ref, taps_ref, up_a, up_b, down_a, down_b, out_ref, hidden_ref
 ):
-    place = lax.axis_index("frame")
-    inside = jnp.where(is_even(), place > 0, place < devices - 1)
-    _, _, tap = taps_of(taps_ref)
-    stream = with_halo(halo_ref, own_ref, base_ref, in_ref, tap, inside)
-    out_ref[...] = mix(stream, (up_a, up_b), (down_a, down_b), hidden_ref)
+    inside = has_outer(devices)
+    out_ref[...] = own_ref[...]
+
+    @pl.when(inside)
+    def _():
+        _, _, tap = taps_of(taps_ref)
+        out_ref[...] = with_halo(halo_ref, own_ref, base_ref, in_ref, tap, inside)
+
+    out_ref[...] = mix(out_ref[...], (up_a, up_b), (down_a, down_b), hidden_ref)
 
 
 def mix_near_body(
@@ -384,7 +401,9 @@
     near_halo = held(near_halo)
     far = call(functools.partial(far_body, scale), small, 2, attention(1))(features, frames)
     base, own_near, own_far = call(own_body, (wide,) * 3, 5)(features, near, far, in_weight, taps)
-    far_halo = call(functools.partial(halo_body, scale), small, 5, attention(1))(features, *outers)
+    far_halo = call(functools.partial(halo_body, devices, scale), small, 5, attention(1))(
+        features, *outers
+    )
     hidden = pltpu.VMEM((rows, parts * units), BF16)
     far = call(functools.partial(mix_far_body, devices), wide, 9, (hidden,))(
         far_halo, own_far, base, in_weight, taps, *weights

time: 29.7 us -> 29 us (0.976)
  Pallas kernels: 10.4 us -> 9.24 us
  local copies, waits for them, and re-layouts: 0.16 us -> 0.59 us
    pallas_call x1, Pallas kernels: 0.86 us -> 0.03 us  [on_device(): call(functools.partial(halo_body, devices, scale), small, 5, attention(1))]
    unnamed x8, local copies, waits for them, and re-layouts: 0.16 us -> 0.59 us
    pallas_call x1, Pallas kernels: 1.8 us -> 1.49 us  [on_device(): call(functools.partial(mix_far_body, devices), wide, 9, (hidden,))]
  transfers between devices with their start and end apart: 10 -> 10, of which waited for: 3 -> 3; matrix products, arithmetic and copies ran while one was open for 0% -> 0% of each run, Pallas kernels for 26% -> 22%
where the time goes in v8:
time: 29 us; the launch traced here: 28.9 us
  starting transfers between devices  12.6 us (43%)
  Pallas kernels  9.24 us (32%)
  waiting for transfers between devices  6.24 us (22%)
  local copies, waits for them, and re-layouts  0.59 us (2%)
    ppermute x1, starting transfers between devices, on_device(): theirs = lax.ppermute(mine, 'frame', flips(masks[0]))  4.14 us
    ppermute x1, waiting for transfers between devices, on_device(): theirs = lax.ppermute(mine, 'frame', flips(mask))  3.27 us
    ppermute x1, starting transfers between devices, on_device(): theirs = lax.ppermute(mine, 'frame', flips(mask))  3.04 us
    ppermute x1, starting transfers between devices, on_device(): near_halo = lax.ppermute(near, 'frame', flips(1))  2.31 us
    pallas_call x1, Pallas kernels, on_device(): call(functools.partial(mix_near_body, devices), kept((lines, LANES), BF16...  1.96 us
    ppermute x1, waiting for transfers between devices, on_device(): theirs = lax.ppermute(mine, 'frame', flips(masks[0]))  1.89 us
    pallas_call x1, Pallas kernels, on_device(): call(functools.partial(pick_body, parts), (kept((rows, channels), BF16),...  1.72 us
    pallas_call x1, Pallas kernels, on_device(): call(functools.partial(mix_far_body, devices), wide, 9, (hidden,))  1.49 us
  transfers between devices with their start and end apart: 10, of which 3 were waited for; matrix products, arithmetic and copies ran while one was open for 0% of the time, Pallas kernels for 22%

profile of v8, /device:TPU:0, one launch (start us, length us, event | category | flops | bytes accessed | tf_op | source)
XLA Modules:
  0.0 28.9 jit_solution(4831971684687818585)
XLA Ops:
  0.0 0.5 %collective-permute-start.3 = (bf16[1,512,1024]{2,1,0:T(8,128)(2,1)}, bf16[1,512,1024]{2,1,0:T(8,128)(2,1)S(1)}, u32[]{:S(2)}, u32[]{:S(2)}) collective-permute-start(bf16[1,512,1024]{2,1,0:T(8,128)(2,1)} %up_a.3), channel_id=1, source_target_pairs={{0,1},{1,0},{2,3},{3,2},{4,5},{5,4},{6,7},{7,6},{8,9},{9,8},{10,11... | collective-permute-start | bytes 3145736 | tf_op jit(solution)/shard_map/ppermute | solution.py:371
  0.5 0.0 collective-permute-start.4
  0.5 1.7 %shard_map.73 = (bf16[256,256]{1,0:T(8,128)(2,1)S(1)}, bf16[2,1024,256]{2,1,0:T(8,128)(2,1)S(1)}, bf16[256,256]{1,0:T(8,128)(2,1)S(1)}) custom-call(s32[1,512]{1,0:T(1,128)} %bitcast.10, s32[2,512]{1,0:T(2,128)} %pixel_hbm.1, bf16[2,1024,256]{2,1,0:T(8,128)(2,1)} %frames_hbm.1), custom_call_target="tpu_custom_call" | custom-call | tf_op jit(solution)/shard_map/pallas_call | solution.py:350
  2.2 0.6 %collective-permute-start.5 = (bf16[256,256]{1,0:T(8,128)(2,1)S(1)}, bf16[256,256]{1,0:T(8,128)(2,1)S(1)}, u32[]{:S(2)}, u32[]{:S(2)}) collective-permute-start(bf16[256,256]{1,0:T(8,128)(2,1)S(1)} %get-tuple-element.19), channel_id=1, source_target_pairs={{4,8},{5,9},{0,1},{12,13},{8,4},{9,5},{1,0},{13,12},{6,10},{7,11},... | collective-permute-start | bytes 393224 | tf_op jit(solution)/shard_map/ppermute | solution.py:370
  2.8 4.1 %collective-permute-start = (bf16[256,256]{1,0:T(8,128)(2,1)S(1)}, bf16[256,256]{1,0:T(8,128)(2,1)S(1)}, u32[]{:S(2)}, u32[]{:S(2)}) collective-permute-start(bf16[256,256]{1,0:T(8,128)(2,1)S(1)} %get-tuple-element.13.a_ref), channel_id=1, source_target_pairs={{0,4},{4,0},{8,12},{12,8},{1,5},{5,1},{9,13},{13,9},{2,6},{6,2},{1... | collective-permute-start | bytes 393224 | tf_op jit(solution)/shard_map/ppermute | solution.py:369
  6.9 0.0 collective-permute-done.5.a_ref
  6.9 1.5 %collective-permute-start.6 = (bf16[256,256]{1,0:T(8,128)(2,1)S(1)}, bf16[256,256]{1,0:T(8,128)(2,1)S(1)}, u32[]{:S(2)}, u32[]{:S(2)}) collective-permute-start(bf16[256,256]{1,0:T(8,128)(2,1)S(1)} %collective-permute-done.5.a_ref), channel_id=1, source_target_pairs={{0,2},{2,0},{1,3},{3,1},{4,6},{6,4},{5,7},{7,5},{8,10},{10,8},{9,1... | collective-permute-start | bytes 393224 | tf_op jit(solution)/shard_map/ppermute | solution.py:381
  8.4 1.9 %collective-permute-done.b_ref = bf16[256,256]{1,0:T(8,128)(2,1)S(1)} collective-permute-done((bf16[256,256]{1,0:T(8,128)(2,1)S(1)}, bf16[256,256]{1,0:T(8,128)(2,1)S(1)}, u32[]{:S(2)}, u32[]{:S(2)}) %collective-permute-start) | collective-permute-done | bytes 131104 | tf_op jit(solution)/shard_map/ppermute | solution.py:369
  10.3 3.0 %collective-permute-start.1 = (bf16[256,256]{1,0:T(8,128)(2,1)S(1)}, bf16[256,256]{1,0:T(8,128)(2,1)S(1)}, u32[]{:S(2)}, u32[]{:S(2)}) collective-permute-start(bf16[256,256]{1,0:T(8,128)(2,1)S(1)} %shard_map.74.a_ref), channel_id=1, source_target_pairs={{0,12},{4,8},{8,4},{12,0},{1,13},{5,9},{9,5},{13,1},{2,14},{6,10},... | collective-permute-start | bytes 393224 | tf_op jit(solution)/shard_map/ppermute | solution.py:377
  13.4 0.5 %collective-permute-start.8 = (bf16[256,256]{1,0:T(8,128)(2,1)S(1)}, bf16[256,256]{1,0:T(8,128)(2,1)S(1)}, u32[]{:S(2)}, u32[]{:S(2)}) collective-permute-start(bf16[256,256]{1,0:T(8,128)(2,1)S(1)} %collective-permute-done.6.b_ref), channel_id=1, source_target_pairs={{0,1},{1,0},{2,3},{3,2},{4,5},{5,4},{6,7},{7,6},{8,9},{9,8},{10,11... | collective-permute-start | bytes 393224 | tf_op jit(solution)/shard_map/ppermute | solution.py:384
  13.9 3.3 %collective-permute-done.1.b_ref = bf16[256,256]{1,0:T(8,128)(2,1)S(1)} collective-permute-done((bf16[256,256]{1,0:T(8,128)(2,1)S(1)}, bf16[256,256]{1,0:T(8,128)(2,1)S(1)}, u32[]{:S(2)}, u32[]{:S(2)}) %collective-permute-start.1) | collective-permute-done | bytes 131104 | tf_op jit(solution)/shard_map/ppermute | solution.py:377
  17.2 0.9 %shard_map.75 = (bf16[256,256]{1,0:T(8,128)(2,1)S(1)}, bf16[256,256]{1,0:T(8,128)(2,1)S(1)}) custom-call(bf16[256,256]{1,0:T(8,128)(2,1)S(1)} %shard_map.74.a_ref, bf16[256,256]{1,0:T(8,128)(2,1)S(1)} %collective-permute-done.1.b_ref, bf16[2,1024,256]{2,1,0:T(8,128)(2,1)S(1)} %get-tuple-element.14.frames_ref), custom_call_target="tpu_custom_call" | custom-call | tf_op jit(solution)/shard_map/pallas_call | solution.py:397
  18.0 2.3 %collective-permute-start.2 = (bf16[256,256]{1,0:T(8,128)(2,1)S(1)}, bf16[256,256]{1,0:T(8,128)(2,1)S(1)}, u32[]{:S(2)}, u32[]{:S(2)}) collective-permute-start(bf16[256,256]{1,0:T(8,128)(2,1)S(1)} %get-tuple-element.15.near_ref), channel_id=1, source_target_pairs={{0,4},{4,0},{8,12},{12,8},{1,5},{5,1},{9,13},{13,9},{2,6},{6,2},{1... | collective-permute-start | bytes 393224 | tf_op jit(solution)/shard_map/ppermute | solution.py:400
  20.4 0.9 %shard_map.76.far_ref = bf16[256,256]{1,0:T(8,128)(2,1)S(1)} custom-call(bf16[256,256]{1,0:T(8,128)(2,1)S(1)} %get-tuple-element.16.features_ref, bf16[2,1024,256]{2,1,0:T(8,128)(2,1)S(1)} %get-tuple-element.14.frames_ref), custom_call_target="tpu_custom_call" | custom-call | tf_op jit(solution)/shard_map/pallas_call | solution.py:402
  21.2 0.0 copy-start.1
  21.3 0.1 copy-done
  21.4 0.6 %shard_map.77 = (f32[256,512]{1,0:T(8,128)S(1)}, f32[256,512]{1,0:T(8,128)S(1)}, f32[256,512]{1,0:T(8,128)S(1)}) custom-call(bf16[256,256]{1,0:T(8,128)(2,1)S(1)} %get-tuple-element.16.features_ref, bf16[256,256]{1,0:T(8,128)(2,1)S(1)} %get-tuple-element.15.near_ref, bf16[256,256]{1,0:T(8,128)(2,1)S(1)} %shard_map.76.far_ref, bf16[512,512]{1,0:T(8,128)(2,1)S(1)} %copy-done, ...), custom_call_target="tpu_custom_call" | custom-call | tf_op jit(solution)/shard_map/pallas_call | solution.py:403
  22.1 0.4 %copy-done.1 = bf16[1,512,1024]{2,1,0:T(8,128)(2,1)S(1)} copy-done((bf16[1,512,1024]{2,1,0:T(8,128)(2,1)S(1)}, bf16[1,512,1024]{2,1,0:T(8,128)(2,1)}, u32[]{:S(2)}) %copy-start.1) | copy-done | bytes 1048600
  22.6 1.5 %shard_map.79.far_ref = f32[256,512]{1,0:T(8,128)S(1)} custom-call(bf16[256,256]{1,0:T(8,128)(2,1)S(1)} %shard_map.78.halo_ref, f32[256,512]{1,0:T(8,128)S(1)} %get-tuple-element.20.own_ref, f32[256,512]{1,0:T(8,128)S(1)} %get-tuple-element.18.base_ref, bf16[512,512]{1,0:T(8,128)(2,1)S(1)} %copy-done, f32[1,1536]{1,0:T(1,128)S(1)} %bitcast.8, ...), custom_call_target="tpu_custom_call" | custom-call | tf_op jit(solution)/shard_map/pallas_call | solution.py:408
  24.1 2.0 %shard_map.80.own_ref = bf16[2048,128]{1,0:T(8,128)(2,1)S(1)} custom-call(bf16[256,256]{1,0:T(8,128)(2,1)S(1)} %collective-permute-done.2.halo_ref, f32[256,512]{1,0:T(8,128)S(1)} %get-tuple-element.17.own_ref, f32[256,512]{1,0:T(8,128)S(1)} %get-tuple-element.18.base_ref, bf16[512,512]{1,0:T(8,128)(2,1)S(1)} %copy-done, f32[1,1536]{1,0:T(1,128)S(1)} %bitcast.9, ...), custom_call_target="tpu_custom_call" | custom-call | tf_op jit(solution)/shard_map/pallas_call | solution.py:413
  26.1 0.1 collective-permute-start.9
  26.1 0.8 %shard_map.81._ = bf16[4096,128]{1,0:T(8,128)(2,1)} custom-call(bf16[2048,128]{1,0:T(8,128)(2,1)S(1)} %shard_map.80.own_ref), custom_call_target="tpu_custom_call" | custom-call | tf_op jit(solution)/shard_map/pallas_call | solution.py:422
  27.0 1.1 %collective-permute-done.9.other_ref = bf16[2048,128]{1,0:T(8,128)(2,1)S(1)} collective-permute-done((bf16[2048,128]{1,0:T(8,128)(2,1)S(1)}, bf16[2048,128]{1,0:T(8,128)(2,1)S(1)}, u32[]{:S(2)}, u32[]{:S(2)}) %collective-permute-start.9) | collective-permute-done | bytes 524320 | tf_op jit(solution)/shard_map/ppermute | solution.py:419
  28.0 0.8 %shard_map.82 = bf16[4096,128]{1,0:T(8,128)(2,1)} custom-call(bf16[2048,128]{1,0:T(8,128)(2,1)S(1)} %collective-permute-done.9.other_ref, bf16[4096,128]{1,0:T(8,128)(2,1)} %shard_map.81._), custom_call_target="tpu_custom_call", output_to_operand_aliasing={{}: (1, {})} | custom-call | tf_op jit(solution)/shard_map/pallas_call | solution.py:423
  (14 shorter events, 0.1 us)
Async XLA Ops:
  0.0 22.1 %collective-permute-start.3 = (bf16[1,512,1024]{2,1,0:T(8,128)(2,1)}, bf16[1,512,1024]{2,1,0:T(8,128)(2,1)S(1)}, u32[]{:S(2)}, u32[]{:S(2)}) collective-permute-start(bf16[1,512,1024]{2,1,0:T(8,128)(2,1)} %up_a.3), channel_id=1, source_target_pairs={{0,1},{1,0},{2,3},{3,2},{4,5},{5,4},{6,7},{7,6},{8,9},{9,8},{10,11... | collective-permute-start | bytes 3145736 | tf_op jit(solution)/shard_map/ppermute | solution.py:371
  0.5 21.6 %collective-permute-start.4 = (bf16[1,1024,512]{2,1,0:T(8,128)(2,1)}, bf16[1,1024,512]{2,1,0:T(8,128)(2,1)S(1)}, u32[]{:S(2)}, u32[]{:S(2)}) collective-permute-start(bf16[1,1024,512]{2,1,0:T(8,128)(2,1)} %down_a.3), channel_id=1, source_target_pairs={{0,1},{1,0},{2,3},{3,2},{4,5},{5,4},{6,7},{7,6},{8,9},{9,8},{10,11... | collective-permute-start | bytes 3145736 | tf_op jit(solution)/shard_map/ppermute | solution.py:372
  2.2 4.7 %collective-permute-start.5 = (bf16[256,256]{1,0:T(8,128)(2,1)S(1)}, bf16[256,256]{1,0:T(8,128)(2,1)S(1)}, u32[]{:S(2)}, u32[]{:S(2)}) collective-permute-start(bf16[256,256]{1,0:T(8,128)(2,1)S(1)} %get-tuple-element.19), channel_id=1, source_target_pairs={{4,8},{5,9},{0,1},{12,13},{8,4},{9,5},{1,0},{13,12},{6,10},{7,11},... | collective-permute-start | bytes 393224 | tf_op jit(solution)/shard_map/ppermute | solution.py:370
  2.8 7.5 %collective-permute-start = (bf16[256,256]{1,0:T(8,128)(2,1)S(1)}, bf16[256,256]{1,0:T(8,128)(2,1)S(1)}, u32[]{:S(2)}, u32[]{:S(2)}) collective-permute-start(bf16[256,256]{1,0:T(8,128)(2,1)S(1)} %get-tuple-element.13.a_ref), channel_id=1, source_target_pairs={{0,4},{4,0},{8,12},{12,8},{1,5},{5,1},{9,13},{13,9},{2,6},{6,2},{1... | collective-permute-start | bytes 393224 | tf_op jit(solution)/shard_map/ppermute | solution.py:369
  6.9 6.4 %collective-permute-start.6 = (bf16[256,256]{1,0:T(8,128)(2,1)S(1)}, bf16[256,256]{1,0:T(8,128)(2,1)S(1)}, u32[]{:S(2)}, u32[]{:S(2)}) collective-permute-start(bf16[256,256]{1,0:T(8,128)(2,1)S(1)} %collective-permute-done.5.a_ref), channel_id=1, source_target_pairs={{0,2},{2,0},{1,3},{3,1},{4,6},{6,4},{5,7},{7,5},{8,10},{10,8},{9,1... | collective-permute-start | bytes 393224 | tf_op jit(solution)/shard_map/ppermute | solution.py:381
  10.3 6.8 %collective-permute-start.1 = (bf16[256,256]{1,0:T(8,128)(2,1)S(1)}, bf16[256,256]{1,0:T(8,128)(2,1)S(1)}, u32[]{:S(2)}, u32[]{:S(2)}) collective-permute-start(bf16[256,256]{1,0:T(8,128)(2,1)S(1)} %shard_map.74.a_ref), channel_id=1, source_target_pairs={{0,12},{4,8},{8,4},{12,0},{1,13},{5,9},{9,5},{13,1},{2,14},{6,10},... | collective-permute-start | bytes 393224 | tf_op jit(solution)/shard_map/ppermute | solution.py:377
  13.4 8.7 %collective-permute-start.7 = (bf16[256,256]{1,0:T(8,128)(2,1)S(1)}, bf16[256,256]{1,0:T(8,128)(2,1)S(1)}, u32[]{:S(2)}, u32[]{:S(2)}) collective-permute-start(bf16[256,256]{1,0:T(8,128)(2,1)S(1)} %collective-permute-done.5.a_ref), channel_id=1, source_target_pairs={{0,1},{1,0},{2,3},{3,2},{4,5},{5,4},{6,7},{7,6},{8,9},{9,8},{10,11... | collective-permute-start | bytes 393224 | tf_op jit(solution)/shard_map/ppermute | solution.py:383
  13.4 8.7 %collective-permute-start.8 = (bf16[256,256]{1,0:T(8,128)(2,1)S(1)}, bf16[256,256]{1,0:T(8,128)(2,1)S(1)}, u32[]{:S(2)}, u32[]{:S(2)}) collective-permute-start(bf16[256,256]{1,0:T(8,128)(2,1)S(1)} %collective-permute-done.6.b_ref), channel_id=1, source_target_pairs={{0,1},{1,0},{2,3},{3,2},{4,5},{5,4},{6,7},{7,6},{8,9},{9,8},{10,11... | collective-permute-start | bytes 393224 | tf_op jit(solution)/shard_map/ppermute | solution.py:384
  17.2 4.1 %copy-start.3 = (f32[1,3,512]{2,0,1:T(1,128)S(1)}, f32[1,3,512]{2,0,1:T(1,128)}, u32[]{:S(2)}) copy-start(f32[1,3,512]{2,0,1:T(1,128)} %param.11) | copy-start | bytes 18436
  18.0 6.0 %collective-permute-start.2 = (bf16[256,256]{1,0:T(8,128)(2,1)S(1)}, bf16[256,256]{1,0:T(8,128)(2,1)S(1)}, u32[]{:S(2)}, u32[]{:S(2)}) collective-permute-start(bf16[256,256]{1,0:T(8,128)(2,1)S(1)} %get-tuple-element.15.near_ref), channel_id=1, source_target_pairs={{0,4},{4,0},{8,12},{12,8},{1,5},{5,1},{9,13},{13,9},{2,6},{6,2},{1... | collective-permute-start | bytes 393224 | tf_op jit(solution)/shard_map/ppermute | solution.py:400
  20.4 1.0 %copy-start = (bf16[512,512]{1,0:T(8,128)(2,1)S(1)}, bf16[512,512]{1,0:T(8,128)(2,1)}, u32[]{:S(2)}) copy-start(bf16[512,512]{1,0:T(8,128)(2,1)} %in_ref.5) | copy-start | bytes 1572868
  20.4 1.8 %copy-start.2 = (bf16[1,1024,512]{2,1,0:T(8,128)(2,1)S(1)}, bf16[1,1024,512]{2,1,0:T(8,128)(2,1)}, u32[]{:S(2)}) copy-start(bf16[1,1024,512]{2,1,0:T(8,128)(2,1)} %down_a.3) | copy-start | bytes 3145732
  21.2 1.3 %copy-start.1 = (bf16[1,512,1024]{2,1,0:T(8,128)(2,1)S(1)}, bf16[1,512,1024]{2,1,0:T(8,128)(2,1)}, u32[]{:S(2)}) copy-start(bf16[1,512,1024]{2,1,0:T(8,128)(2,1)} %up_a.3) | copy-start | bytes 3145732
  26.1 2.0 %collective-permute-start.9 = (bf16[2048,128]{1,0:T(8,128)(2,1)S(1)}, bf16[2048,128]{1,0:T(8,128)(2,1)S(1)}, u32[]{:S(2)}, u32[]{:S(2)}) collective-permute-start(bf16[2048,128]{1,0:T(8,128)(2,1)S(1)} %shard_map.80.own_ref), channel_id=1, source_target_pairs={{0,1},{1,0},{2,3},{3,2},{4,5},{5,4},{6,7},{7,6},{8,9},{9,8},{10,11... | collective-permute-start | bytes 1572872 | tf_op jit(solution)/shard_map/ppermute | solution.py:419

commit v9 on v8

--- a/solution.py
+++ b/solution.py
@@ -250,9 +250,9 @@
         units = up_ref.shape[2]
         step = min(256, units)
         for at in range(0, units, step):
-            x = dot(gated, up_ref[0, :, at : at + step])
-            inner = x * (x * x * (0.044715 * math.sqrt(2 / math.pi)) + math.sqrt(2 / math.pi))
-            hidden_ref[:, base + at : base + at + step] = (x + x * jnp.tanh(inner)).astype(BF16)
+            x = dot(gated, up_ref[0, :, at : at + step]).astype(BF16)
+            inner = x * (x * x * BF16(0.044715 * math.sqrt(2 / math.pi)) + BF16(math.sqrt(2 / math.pi)))
+            hidden_ref[:, base + at : base + at + step] = x + x * jnp.tanh(inner)
         base += units
     base = 0
     for up_ref, down_ref in zip(ups, downs):

time: 29 us -> 28.7 us (0.990)
  Pallas kernels: 9.24 us -> 8.94 us
where the time goes in v9:
time: 28.7 us; the launch traced here: 28.6 us
  starting transfers between devices  12.6 us (44%)
  Pallas kernels  8.94 us (31%)
  waiting for transfers between devices  6.24 us (22%)
  local copies, waits for them, and re-layouts  0.59 us (2%)
    ppermute x1, starting transfers between devices, on_device(): theirs = lax.ppermute(mine, 'frame', flips(masks[0]))  4.14 us
    ppermute x1, waiting for transfers between devices, on_device(): theirs = lax.ppermute(mine, 'frame', flips(mask))  3.27 us
    ppermute x1, starting transfers between devices, on_device(): theirs = lax.ppermute(mine, 'frame', flips(mask))  3.04 us
    ppermute x1, starting transfers between devices, on_device(): near_halo = lax.ppermute(near, 'frame', flips(1))  2.31 us
    ppermute x1, waiting for transfers between devices, on_device(): theirs = lax.ppermute(mine, 'frame', flips(masks[0]))  1.89 us
    pallas_call x1, Pallas kernels, on_device(): call(functools.partial(mix_near_body, devices), kept((lines, LANES), BF16...  1.81 us
    pallas_call x1, Pallas kernels, on_device(): call(functools.partial(pick_body, parts), (kept((rows, channels), BF16),...  1.72 us
    ppermute x1, starting transfers between devices, on_device(): outer_b = lax.ppermute(outer, 'query', [(g, g ^ 1) for g in range(groups)])  1.49 us
  transfers between devices with their start and end apart: 10, of which 3 were waited for; matrix products, arithmetic and copies ran while one was open for 0% of the time, Pallas kernels for 22%

profile of v9, /device:TPU:0, one launch (start us, length us, event | category | flops | bytes accessed | tf_op | source)
XLA Modules:
  0.0 28.6 jit_solution(4535044834449748430)
XLA Ops:
  0.0 0.5 %collective-permute-start.3 = (bf16[1,512,1024]{2,1,0:T(8,128)(2,1)}, bf16[1,512,1024]{2,1,0:T(8,128)(2,1)S(1)}, u32[]{:S(2)}, u32[]{:S(2)}) collective-permute-start(bf16[1,512,1024]{2,1,0:T(8,128)(2,1)} %up_a.3), channel_id=1, source_target_pairs={{0,1},{1,0},{2,3},{3,2},{4,5},{5,4},{6,7},{7,6},{8,9},{9,8},{10,11... | collective-permute-start | bytes 3145736 | tf_op jit(solution)/shard_map/ppermute | solution.py:371
  0.5 0.0 collective-permute-start.4
  0.5 1.7 %shard_map.73 = (bf16[256,256]{1,0:T(8,128)(2,1)S(1)}, bf16[2,1024,256]{2,1,0:T(8,128)(2,1)S(1)}, bf16[256,256]{1,0:T(8,128)(2,1)S(1)}) custom-call(s32[1,512]{1,0:T(1,128)} %bitcast.10, s32[2,512]{1,0:T(2,128)} %pixel_hbm.1, bf16[2,1024,256]{2,1,0:T(8,128)(2,1)} %frames_hbm.1), custom_call_target="tpu_custom_call" | custom-call | tf_op jit(solution)/shard_map/pallas_call | solution.py:350
  2.2 0.6 %collective-permute-start.5 = (bf16[256,256]{1,0:T(8,128)(2,1)S(1)}, bf16[256,256]{1,0:T(8,128)(2,1)S(1)}, u32[]{:S(2)}, u32[]{:S(2)}) collective-permute-start(bf16[256,256]{1,0:T(8,128)(2,1)S(1)} %get-tuple-element.19), channel_id=1, source_target_pairs={{4,8},{5,9},{0,1},{12,13},{8,4},{9,5},{1,0},{13,12},{6,10},{7,11},... | collective-permute-start | bytes 393224 | tf_op jit(solution)/shard_map/ppermute | solution.py:370
  2.8 4.1 %collective-permute-start = (bf16[256,256]{1,0:T(8,128)(2,1)S(1)}, bf16[256,256]{1,0:T(8,128)(2,1)S(1)}, u32[]{:S(2)}, u32[]{:S(2)}) collective-permute-start(bf16[256,256]{1,0:T(8,128)(2,1)S(1)} %get-tuple-element.13.a_ref), channel_id=1, source_target_pairs={{0,4},{4,0},{8,12},{12,8},{1,5},{5,1},{9,13},{13,9},{2,6},{6,2},{1... | collective-permute-start | bytes 393224 | tf_op jit(solution)/shard_map/ppermute | solution.py:369
  6.9 0.0 collective-permute-done.5.a_ref
  6.9 1.5 %collective-permute-start.6 = (bf16[256,256]{1,0:T(8,128)(2,1)S(1)}, bf16[256,256]{1,0:T(8,128)(2,1)S(1)}, u32[]{:S(2)}, u32[]{:S(2)}) collective-permute-start(bf16[256,256]{1,0:T(8,128)(2,1)S(1)} %collective-permute-done.5.a_ref), channel_id=1, source_target_pairs={{0,2},{2,0},{1,3},{3,1},{4,6},{6,4},{5,7},{7,5},{8,10},{10,8},{9,1... | collective-permute-start | bytes 393224 | tf_op jit(solution)/shard_map/ppermute | solution.py:381
  8.4 1.9 %collective-permute-done.b_ref = bf16[256,256]{1,0:T(8,128)(2,1)S(1)} collective-permute-done((bf16[256,256]{1,0:T(8,128)(2,1)S(1)}, bf16[256,256]{1,0:T(8,128)(2,1)S(1)}, u32[]{:S(2)}, u32[]{:S(2)}) %collective-permute-start) | collective-permute-done | bytes 131104 | tf_op jit(solution)/shard_map/ppermute | solution.py:369
  10.3 3.0 %collective-permute-start.1 = (bf16[256,256]{1,0:T(8,128)(2,1)S(1)}, bf16[256,256]{1,0:T(8,128)(2,1)S(1)}, u32[]{:S(2)}, u32[]{:S(2)}) collective-permute-start(bf16[256,256]{1,0:T(8,128)(2,1)S(1)} %shard_map.74.a_ref), channel_id=1, source_target_pairs={{0,12},{4,8},{8,4},{12,0},{1,13},{5,9},{9,5},{13,1},{2,14},{6,10},... | collective-permute-start | bytes 393224 | tf_op jit(solution)/shard_map/ppermute | solution.py:377
  13.4 0.5 %collective-permute-start.8 = (bf16[256,256]{1,0:T(8,128)(2,1)S(1)}, bf16[256,256]{1,0:T(8,128)(2,1)S(1)}, u32[]{:S(2)}, u32[]{:S(2)}) collective-permute-start(bf16[256,256]{1,0:T(8,128)(2,1)S(1)} %collective-permute-done.6.b_ref), channel_id=1, source_target_pairs={{0,1},{1,0},{2,3},{3,2},{4,5},{5,4},{6,7},{7,6},{8,9},{9,8},{10,11... | collective-permute-start | bytes 393224 | tf_op jit(solution)/shard_map/ppermute | solution.py:384
  13.9 3.3 %collective-permute-done.1.b_ref = bf16[256,256]{1,0:T(8,128)(2,1)S(1)} collective-permute-done((bf16[256,256]{1,0:T(8,128)(2,1)S(1)}, bf16[256,256]{1,0:T(8,128)(2,1)S(1)}, u32[]{:S(2)}, u32[]{:S(2)}) %collective-permute-start.1) | collective-permute-done | bytes 131104 | tf_op jit(solution)/shard_map/ppermute | solution.py:377
  17.2 0.9 %shard_map.75 = (bf16[256,256]{1,0:T(8,128)(2,1)S(1)}, bf16[256,256]{1,0:T(8,128)(2,1)S(1)}) custom-call(bf16[256,256]{1,0:T(8,128)(2,1)S(1)} %shard_map.74.a_ref, bf16[256,256]{1,0:T(8,128)(2,1)S(1)} %collective-permute-done.1.b_ref, bf16[2,1024,256]{2,1,0:T(8,128)(2,1)S(1)} %get-tuple-element.14.frames_ref), custom_call_target="tpu_custom_call" | custom-call | tf_op jit(solution)/shard_map/pallas_call | solution.py:397
  18.0 2.3 %collective-permute-start.2 = (bf16[256,256]{1,0:T(8,128)(2,1)S(1)}, bf16[256,256]{1,0:T(8,128)(2,1)S(1)}, u32[]{:S(2)}, u32[]{:S(2)}) collective-permute-start(bf16[256,256]{1,0:T(8,128)(2,1)S(1)} %get-tuple-element.15.near_ref), channel_id=1, source_target_pairs={{0,4},{4,0},{8,12},{12,8},{1,5},{5,1},{9,13},{13,9},{2,6},{6,2},{1... | collective-permute-start | bytes 393224 | tf_op jit(solution)/shard_map/ppermute | solution.py:400
  20.4 0.9 %shard_map.76.far_ref = bf16[256,256]{1,0:T(8,128)(2,1)S(1)} custom-call(bf16[256,256]{1,0:T(8,128)(2,1)S(1)} %get-tuple-element.16.features_ref, bf16[2,1024,256]{2,1,0:T(8,128)(2,1)S(1)} %get-tuple-element.14.frames_ref), custom_call_target="tpu_custom_call" | custom-call | tf_op jit(solution)/shard_map/pallas_call | solution.py:402
  21.2 0.0 copy-start.1
  21.3 0.1 copy-done
  21.4 0.6 %shard_map.77 = (f32[256,512]{1,0:T(8,128)S(1)}, f32[256,512]{1,0:T(8,128)S(1)}, f32[256,512]{1,0:T(8,128)S(1)}) custom-call(bf16[256,256]{1,0:T(8,128)(2,1)S(1)} %get-tuple-element.16.features_ref, bf16[256,256]{1,0:T(8,128)(2,1)S(1)} %get-tuple-element.15.near_ref, bf16[256,256]{1,0:T(8,128)(2,1)S(1)} %shard_map.76.far_ref, bf16[512,512]{1,0:T(8,128)(2,1)S(1)} %copy-done, ...), custom_call_target="tpu_custom_call" | custom-call | tf_op jit(solution)/shard_map/pallas_call | solution.py:403
  22.1 0.4 %copy-done.1 = bf16[1,512,1024]{2,1,0:T(8,128)(2,1)S(1)} copy-done((bf16[1,512,1024]{2,1,0:T(8,128)(2,1)S(1)}, bf16[1,512,1024]{2,1,0:T(8,128)(2,1)}, u32[]{:S(2)}) %copy-start.1) | copy-done | bytes 1048600
  22.6 1.4 %shard_map.79.far_ref = f32[256,512]{1,0:T(8,128)S(1)} custom-call(bf16[256,256]{1,0:T(8,128)(2,1)S(1)} %shard_map.78.halo_ref, f32[256,512]{1,0:T(8,128)S(1)} %get-tuple-element.20.own_ref, f32[256,512]{1,0:T(8,128)S(1)} %get-tuple-element.18.base_ref, bf16[512,512]{1,0:T(8,128)(2,1)S(1)} %copy-done, f32[1,1536]{1,0:T(1,128)S(1)} %bitcast.8, ...), custom_call_target="tpu_custom_call" | custom-call | tf_op jit(solution)/shard_map/pallas_call | solution.py:408
  23.9 1.8 %shard_map.80.own_ref = bf16[2048,128]{1,0:T(8,128)(2,1)S(1)} custom-call(bf16[256,256]{1,0:T(8,128)(2,1)S(1)} %collective-permute-done.2.halo_ref, f32[256,512]{1,0:T(8,128)S(1)} %get-tuple-element.17.own_ref, f32[256,512]{1,0:T(8,128)S(1)} %get-tuple-element.18.base_ref, bf16[512,512]{1,0:T(8,128)(2,1)S(1)} %copy-done, f32[1,1536]{1,0:T(1,128)S(1)} %bitcast.9, ...), custom_call_target="tpu_custom_call" | custom-call | tf_op jit(solution)/shard_map/pallas_call | solution.py:413
  25.8 0.1 collective-permute-start.9
  25.8 0.8 %shard_map.81._ = bf16[4096,128]{1,0:T(8,128)(2,1)} custom-call(bf16[2048,128]{1,0:T(8,128)(2,1)S(1)} %shard_map.80.own_ref), custom_call_target="tpu_custom_call" | custom-call | tf_op jit(solution)/shard_map/pallas_call | solution.py:422
  26.7 1.1 %collective-permute-done.9.other_ref = bf16[2048,128]{1,0:T(8,128)(2,1)S(1)} collective-permute-done((bf16[2048,128]{1,0:T(8,128)(2,1)S(1)}, bf16[2048,128]{1,0:T(8,128)(2,1)S(1)}, u32[]{:S(2)}, u32[]{:S(2)}) %collective-permute-start.9) | collective-permute-done | bytes 524320 | tf_op jit(solution)/shard_map/ppermute | solution.py:419
  27.7 0.8 %shard_map.82 = bf16[4096,128]{1,0:T(8,128)(2,1)} custom-call(bf16[2048,128]{1,0:T(8,128)(2,1)S(1)} %collective-permute-done.9.other_ref, bf16[4096,128]{1,0:T(8,128)(2,1)} %shard_map.81._), custom_call_target="tpu_custom_call", output_to_operand_aliasing={{}: (1, {})} | custom-call | tf_op jit(solution)/shard_map/pallas_call | solution.py:423
  (14 shorter events, 0.1 us)
Async XLA Ops:
  0.0 22.1 %collective-permute-start.3 = (bf16[1,512,1024]{2,1,0:T(8,128)(2,1)}, bf16[1,512,1024]{2,1,0:T(8,128)(2,1)S(1)}, u32[]{:S(2)}, u32[]{:S(2)}) collective-permute-start(bf16[1,512,1024]{2,1,0:T(8,128)(2,1)} %up_a.3), channel_id=1, source_target_pairs={{0,1},{1,0},{2,3},{3,2},{4,5},{5,4},{6,7},{7,6},{8,9},{9,8},{10,11... | collective-permute-start | bytes 3145736 | tf_op jit(solution)/shard_map/ppermute | solution.py:371
  0.5 21.6 %collective-permute-start.4 = (bf16[1,1024,512]{2,1,0:T(8,128)(2,1)}, bf16[1,1024,512]{2,1,0:T(8,128)(2,1)S(1)}, u32[]{:S(2)}, u32[]{:S(2)}) collective-permute-start(bf16[1,1024,512]{2,1,0:T(8,128)(2,1)} %down_a.3), channel_id=1, source_target_pairs={{0,1},{1,0},{2,3},{3,2},{4,5},{5,4},{6,7},{7,6},{8,9},{9,8},{10,11... | collective-permute-start | bytes 3145736 | tf_op jit(solution)/shard_map/ppermute | solution.py:372
  2.2 4.7 %collective-permute-start.5 = (bf16[256,256]{1,0:T(8,128)(2,1)S(1)}, bf16[256,256]{1,0:T(8,128)(2,1)S(1)}, u32[]{:S(2)}, u32[]{:S(2)}) collective-permute-start(bf16[256,256]{1,0:T(8,128)(2,1)S(1)} %get-tuple-element.19), channel_id=1, source_target_pairs={{4,8},{5,9},{0,1},{12,13},{8,4},{9,5},{1,0},{13,12},{6,10},{7,11},... | collective-permute-start | bytes 393224 | tf_op jit(solution)/shard_map/ppermute | solution.py:370
  2.8 7.5 %collective-permute-start = (bf16[256,256]{1,0:T(8,128)(2,1)S(1)}, bf16[256,256]{1,0:T(8,128)(2,1)S(1)}, u32[]{:S(2)}, u32[]{:S(2)}) collective-permute-start(bf16[256,256]{1,0:T(8,128)(2,1)S(1)} %get-tuple-element.13.a_ref), channel_id=1, source_target_pairs={{0,4},{4,0},{8,12},{12,8},{1,5},{5,1},{9,13},{13,9},{2,6},{6,2},{1... | collective-permute-start | bytes 393224 | tf_op jit(solution)/shard_map/ppermute | solution.py:369
  6.9 6.4 %collective-permute-start.6 = (bf16[256,256]{1,0:T(8,128)(2,1)S(1)}, bf16[256,256]{1,0:T(8,128)(2,1)S(1)}, u32[]{:S(2)}, u32[]{:S(2)}) collective-permute-start(bf16[256,256]{1,0:T(8,128)(2,1)S(1)} %collective-permute-done.5.a_ref), channel_id=1, source_target_pairs={{0,2},{2,0},{1,3},{3,1},{4,6},{6,4},{5,7},{7,5},{8,10},{10,8},{9,1... | collective-permute-start | bytes 393224 | tf_op jit(solution)/shard_map/ppermute | solution.py:381
  10.3 6.8 %collective-permute-start.1 = (bf16[256,256]{1,0:T(8,128)(2,1)S(1)}, bf16[256,256]{1,0:T(8,128)(2,1)S(1)}, u32[]{:S(2)}, u32[]{:S(2)}) collective-permute-start(bf16[256,256]{1,0:T(8,128)(2,1)S(1)} %shard_map.74.a_ref), channel_id=1, source_target_pairs={{0,12},{4,8},{8,4},{12,0},{1,13},{5,9},{9,5},{13,1},{2,14},{6,10},... | collective-permute-start | bytes 393224 | tf_op jit(solution)/shard_map/ppermute | solution.py:377
  13.4 8.7 %collective-permute-start.7 = (bf16[256,256]{1,0:T(8,128)(2,1)S(1)}, bf16[256,256]{1,0:T(8,128)(2,1)S(1)}, u32[]{:S(2)}, u32[]{:S(2)}) collective-permute-start(bf16[256,256]{1,0:T(8,128)(2,1)S(1)} %collective-permute-done.5.a_ref), channel_id=1, source_target_pairs={{0,1},{1,0},{2,3},{3,2},{4,5},{5,4},{6,7},{7,6},{8,9},{9,8},{10,11... | collective-permute-start | bytes 393224 | tf_op jit(solution)/shard_map/ppermute | solution.py:383
  13.4 8.7 %collective-permute-start.8 = (bf16[256,256]{1,0:T(8,128)(2,1)S(1)}, bf16[256,256]{1,0:T(8,128)(2,1)S(1)}, u32[]{:S(2)}, u32[]{:S(2)}) collective-permute-start(bf16[256,256]{1,0:T(8,128)(2,1)S(1)} %collective-permute-done.6.b_ref), channel_id=1, source_target_pairs={{0,1},{1,0},{2,3},{3,2},{4,5},{5,4},{6,7},{7,6},{8,9},{9,8},{10,11... | collective-permute-start | bytes 393224 | tf_op jit(solution)/shard_map/ppermute | solution.py:384
  17.2 4.1 %copy-start.3 = (f32[1,3,512]{2,0,1:T(1,128)S(1)}, f32[1,3,512]{2,0,1:T(1,128)}, u32[]{:S(2)}) copy-start(f32[1,3,512]{2,0,1:T(1,128)} %param.11) | copy-start | bytes 18436
  18.0 5.9 %collective-permute-start.2 = (bf16[256,256]{1,0:T(8,128)(2,1)S(1)}, bf16[256,256]{1,0:T(8,128)(2,1)S(1)}, u32[]{:S(2)}, u32[]{:S(2)}) collective-permute-start(bf16[256,256]{1,0:T(8,128)(2,1)S(1)} %get-tuple-element.15.near_ref), channel_id=1, source_target_pairs={{0,4},{4,0},{8,12},{12,8},{1,5},{5,1},{9,13},{13,9},{2,6},{6,2},{1... | collective-permute-start | bytes 393224 | tf_op jit(solution)/shard_map/ppermute | solution.py:400
  20.4 1.0 %copy-start = (bf16[512,512]{1,0:T(8,128)(2,1)S(1)}, bf16[512,512]{1,0:T(8,128)(2,1)}, u32[]{:S(2)}) copy-start(bf16[512,512]{1,0:T(8,128)(2,1)} %in_ref.5) | copy-start | bytes 1572868
  20.4 1.8 %copy-start.2 = (bf16[1,1024,512]{2,1,0:T(8,128)(2,1)S(1)}, bf16[1,1024,512]{2,1,0:T(8,128)(2,1)}, u32[]{:S(2)}) copy-start(bf16[1,1024,512]{2,1,0:T(8,128)(2,1)} %down_a.3) | copy-start | bytes 3145732
  21.2 1.3 %copy-start.1 = (bf16[1,512,1024]{2,1,0:T(8,128)(2,1)S(1)}, bf16[1,512,1024]{2,1,0:T(8,128)(2,1)}, u32[]{:S(2)}) copy-start(bf16[1,512,1024]{2,1,0:T(8,128)(2,1)} %up_a.3) | copy-start | bytes 3145732
  25.8 2.0 %collective-permute-start.9 = (bf16[2048,128]{1,0:T(8,128)(2,1)S(1)}, bf16[2048,128]{1,0:T(8,128)(2,1)S(1)}, u32[]{:S(2)}, u32[]{:S(2)}) collective-permute-start(bf16[2048,128]{1,0:T(8,128)(2,1)S(1)} %shard_map.80.own_ref), channel_id=1, source_target_pairs={{0,1},{1,0},{2,3},{3,2},{4,5},{5,4},{6,7},{7,6},{8,9},{9,8},{10,11... | collective-permute-start | bytes 1572872 | tf_op jit(solution)/shard_map/ppermute | solution.py:419

commit v10 on v9

--- a/solution.py
+++ b/solution.py
@@ -248,15 +248,11 @@
     total = None
     for up_ref, down_ref in zip(ups, downs):
         units = up_ref.shape[2]
-        step = min(256, units)
+        step = min(512, units)
         for at in range(0, units, step):
             x = dot(gated, up_ref[0, :, at : at + step]).astype(BF16)
             inner = x * (x * x * BF16(0.044715 * math.sqrt(2 / math.pi)) + BF16(math.sqrt(2 / math.pi)))
             hidden_ref[:, base + at : base + at + step] = x + x * jnp.tanh(inner)
-        base += units
-    base = 0
-    for up_ref, down_ref in zip(ups, downs):
-        units = up_ref.shape[2]
         part = dot(hidden_ref[:, base : base + units], down_ref[0])
         total = part if total is None else total + part
         base += units

time: 28.7 us -> 28.7 us (level)
  no operation moved by 1% of the time
where the time goes in v10:
time: 28.7 us; the launch traced here: 28.6 us
  starting transfers between devices  12.6 us (44%)
  Pallas kernels  8.94 us (31%)
  waiting for transfers between devices  6.24 us (22%)
  local copies, waits for them, and re-layouts  0.59 us (2%)
    ppermute x1, starting transfers between devices, on_device(): theirs = lax.ppermute(mine, 'frame', flips(masks[0]))  4.14 us
    ppermute x1, waiting for transfers between devices, on_device(): theirs = lax.ppermute(mine, 'frame', flips(mask))  3.27 us
    ppermute x1, starting transfers between devices, on_device(): theirs = lax.ppermute(mine, 'frame', flips(mask))  3.04 us
    ppermute x1, starting transfers between devices, on_device(): near_halo = lax.ppermute(near, 'frame', flips(1))  2.31 us
    ppermute x1, waiting for transfers between devices, on_device(): theirs = lax.ppermute(mine, 'frame', flips(masks[0]))  1.89 us
    pallas_call x1, Pallas kernels, on_device(): call(functools.partial(mix_near_body, devices), kept((lines, LANES), BF16...  1.81 us
    pallas_call x1, Pallas kernels, on_device(): call(functools.partial(pick_body, parts), (kept((rows, channels), BF16),...  1.72 us
    ppermute x1, starting transfers between devices, on_device(): outer_b = lax.ppermute(outer, 'query', [(g, g ^ 1) for g in range(groups)])  1.49 us
  transfers between devices with their start and end apart: 10, of which 3 were waited for; matrix products, arithmetic and copies ran while one was open for 0% of the time, Pallas kernels for 22%

profile of v10, /device:TPU:0, one launch (start us, length us, event | category | flops | bytes accessed | tf_op | source)
XLA Modules:
  0.0 28.6 jit_solution(4535044834449748430)
XLA Ops:
  0.0 0.5 %collective-permute-start.3 = (bf16[1,512,1024]{2,1,0:T(8,128)(2,1)}, bf16[1,512,1024]{2,1,0:T(8,128)(2,1)S(1)}, u32[]{:S(2)}, u32[]{:S(2)}) collective-permute-start(bf16[1,512,1024]{2,1,0:T(8,128)(2,1)} %up_a.3), channel_id=1, source_target_pairs={{0,1},{1,0},{2,3},{3,2},{4,5},{5,4},{6,7},{7,6},{8,9},{9,8},{10,11... | collective-permute-start | bytes 3145736 | tf_op jit(solution)/shard_map/ppermute | solution.py:367
  0.5 0.0 collective-permute-start.4
  0.5 1.7 %shard_map.73 = (bf16[256,256]{1,0:T(8,128)(2,1)S(1)}, bf16[2,1024,256]{2,1,0:T(8,128)(2,1)S(1)}, bf16[256,256]{1,0:T(8,128)(2,1)S(1)}) custom-call(s32[1,512]{1,0:T(1,128)} %bitcast.10, s32[2,512]{1,0:T(2,128)} %pixel_hbm.1, bf16[2,1024,256]{2,1,0:T(8,128)(2,1)} %frames_hbm.1), custom_call_target="tpu_custom_call" | custom-call | tf_op jit(solution)/shard_map/pallas_call | solution.py:346
  2.2 0.6 %collective-permute-start.5 = (bf16[256,256]{1,0:T(8,128)(2,1)S(1)}, bf16[256,256]{1,0:T(8,128)(2,1)S(1)}, u32[]{:S(2)}, u32[]{:S(2)}) collective-permute-start(bf16[256,256]{1,0:T(8,128)(2,1)S(1)} %get-tuple-element.19), channel_id=1, source_target_pairs={{4,8},{5,9},{0,1},{12,13},{8,4},{9,5},{1,0},{13,12},{6,10},{7,11},... | collective-permute-start | bytes 393224 | tf_op jit(solution)/shard_map/ppermute | solution.py:366
  2.8 4.1 %collective-permute-start = (bf16[256,256]{1,0:T(8,128)(2,1)S(1)}, bf16[256,256]{1,0:T(8,128)(2,1)S(1)}, u32[]{:S(2)}, u32[]{:S(2)}) collective-permute-start(bf16[256,256]{1,0:T(8,128)(2,1)S(1)} %get-tuple-element.13.a_ref), channel_id=1, source_target_pairs={{0,4},{4,0},{8,12},{12,8},{1,5},{5,1},{9,13},{13,9},{2,6},{6,2},{1... | collective-permute-start | bytes 393224 | tf_op jit(solution)/shard_map/ppermute | solution.py:365
  6.9 0.0 collective-permute-done.5.a_ref
  6.9 1.5 %collective-permute-start.6 = (bf16[256,256]{1,0:T(8,128)(2,1)S(1)}, bf16[256,256]{1,0:T(8,128)(2,1)S(1)}, u32[]{:S(2)}, u32[]{:S(2)}) collective-permute-start(bf16[256,256]{1,0:T(8,128)(2,1)S(1)} %collective-permute-done.5.a_ref), channel_id=1, source_target_pairs={{0,2},{2,0},{1,3},{3,1},{4,6},{6,4},{5,7},{7,5},{8,10},{10,8},{9,1... | collective-permute-start | bytes 393224 | tf_op jit(solution)/shard_map/ppermute | solution.py:377
  8.4 1.9 %collective-permute-done.b_ref = bf16[256,256]{1,0:T(8,128)(2,1)S(1)} collective-permute-done((bf16[256,256]{1,0:T(8,128)(2,1)S(1)}, bf16[256,256]{1,0:T(8,128)(2,1)S(1)}, u32[]{:S(2)}, u32[]{:S(2)}) %collective-permute-start) | collective-permute-done | bytes 131104 | tf_op jit(solution)/shard_map/ppermute | solution.py:365
  10.3 3.0 %collective-permute-start.1 = (bf16[256,256]{1,0:T(8,128)(2,1)S(1)}, bf16[256,256]{1,0:T(8,128)(2,1)S(1)}, u32[]{:S(2)}, u32[]{:S(2)}) collective-permute-start(bf16[256,256]{1,0:T(8,128)(2,1)S(1)} %shard_map.74.a_ref), channel_id=1, source_target_pairs={{0,12},{4,8},{8,4},{12,0},{1,13},{5,9},{9,5},{13,1},{2,14},{6,10},... | collective-permute-start | bytes 393224 | tf_op jit(solution)/shard_map/ppermute | solution.py:373
  13.4 0.5 %collective-permute-start.8 = (bf16[256,256]{1,0:T(8,128)(2,1)S(1)}, bf16[256,256]{1,0:T(8,128)(2,1)S(1)}, u32[]{:S(2)}, u32[]{:S(2)}) collective-permute-start(bf16[256,256]{1,0:T(8,128)(2,1)S(1)} %collective-permute-done.6.b_ref), channel_id=1, source_target_pairs={{0,1},{1,0},{2,3},{3,2},{4,5},{5,4},{6,7},{7,6},{8,9},{9,8},{10,11... | collective-permute-start | bytes 393224 | tf_op jit(solution)/shard_map/ppermute | solution.py:380
  13.9 3.3 %collective-permute-done.1.b_ref = bf16[256,256]{1,0:T(8,128)(2,1)S(1)} collective-permute-done((bf16[256,256]{1,0:T(8,128)(2,1)S(1)}, bf16[256,256]{1,0:T(8,128)(2,1)S(1)}, u32[]{:S(2)}, u32[]{:S(2)}) %collective-permute-start.1) | collective-permute-done | bytes 131104 | tf_op jit(solution)/shard_map/ppermute | solution.py:373
  17.2 0.9 %shard_map.75 = (bf16[256,256]{1,0:T(8,128)(2,1)S(1)}, bf16[256,256]{1,0:T(8,128)(2,1)S(1)}) custom-call(bf16[256,256]{1,0:T(8,128)(2,1)S(1)} %shard_map.74.a_ref, bf16[256,256]{1,0:T(8,128)(2,1)S(1)} %collective-permute-done.1.b_ref, bf16[2,1024,256]{2,1,0:T(8,128)(2,1)S(1)} %get-tuple-element.14.frames_ref), custom_call_target="tpu_custom_call" | custom-call | tf_op jit(solution)/shard_map/pallas_call | solution.py:393
  18.0 2.3 %collective-permute-start.2 = (bf16[256,256]{1,0:T(8,128)(2,1)S(1)}, bf16[256,256]{1,0:T(8,128)(2,1)S(1)}, u32[]{:S(2)}, u32[]{:S(2)}) collective-permute-start(bf16[256,256]{1,0:T(8,128)(2,1)S(1)} %get-tuple-element.15.near_ref), channel_id=1, source_target_pairs={{0,4},{4,0},{8,12},{12,8},{1,5},{5,1},{9,13},{13,9},{2,6},{6,2},{1... | collective-permute-start | bytes 393224 | tf_op jit(solution)/shard_map/ppermute | solution.py:396
  20.4 0.9 %shard_map.76.far_ref = bf16[256,256]{1,0:T(8,128)(2,1)S(1)} custom-call(bf16[256,256]{1,0:T(8,128)(2,1)S(1)} %get-tuple-element.16.features_ref, bf16[2,1024,256]{2,1,0:T(8,128)(2,1)S(1)} %get-tuple-element.14.frames_ref), custom_call_target="tpu_custom_call" | custom-call | tf_op jit(solution)/shard_map/pallas_call | solution.py:398
  21.2 0.0 copy-start.1
  21.3 0.1 copy-done
  21.4 0.6 %shard_map.77 = (f32[256,512]{1,0:T(8,128)S(1)}, f32[256,512]{1,0:T(8,128)S(1)}, f32[256,512]{1,0:T(8,128)S(1)}) custom-call(bf16[256,256]{1,0:T(8,128)(2,1)S(1)} %get-tuple-element.16.features_ref, bf16[256,256]{1,0:T(8,128)(2,1)S(1)} %get-tuple-element.15.near_ref, bf16[256,256]{1,0:T(8,128)(2,1)S(1)} %shard_map.76.far_ref, bf16[512,512]{1,0:T(8,128)(2,1)S(1)} %copy-done, ...), custom_call_target="tpu_custom_call" | custom-call | tf_op jit(solution)/shard_map/pallas_call | solution.py:399
  22.1 0.4 %copy-done.1 = bf16[1,512,1024]{2,1,0:T(8,128)(2,1)S(1)} copy-done((bf16[1,512,1024]{2,1,0:T(8,128)(2,1)S(1)}, bf16[1,512,1024]{2,1,0:T(8,128)(2,1)}, u32[]{:S(2)}) %copy-start.1) | copy-done | bytes 1048600
  22.6 1.4 %shard_map.79.far_ref = f32[256,512]{1,0:T(8,128)S(1)} custom-call(bf16[256,256]{1,0:T(8,128)(2,1)S(1)} %shard_map.78.halo_ref, f32[256,512]{1,0:T(8,128)S(1)} %get-tuple-element.20.own_ref, f32[256,512]{1,0:T(8,128)S(1)} %get-tuple-element.18.base_ref, bf16[512,512]{1,0:T(8,128)(2,1)S(1)} %copy-done, f32[1,1536]{1,0:T(1,128)S(1)} %bitcast.8, ...), custom_call_target="tpu_custom_call" | custom-call | tf_op jit(solution)/shard_map/pallas_call | solution.py:404
  23.9 1.8 %shard_map.80.own_ref = bf16[2048,128]{1,0:T(8,128)(2,1)S(1)} custom-call(bf16[256,256]{1,0:T(8,128)(2,1)S(1)} %collective-permute-done.2.halo_ref, f32[256,512]{1,0:T(8,128)S(1)} %get-tuple-element.17.own_ref, f32[256,512]{1,0:T(8,128)S(1)} %get-tuple-element.18.base_ref, bf16[512,512]{1,0:T(8,128)(2,1)S(1)} %copy-done, f32[1,1536]{1,0:T(1,128)S(1)} %bitcast.9, ...), custom_call_target="tpu_custom_call" | custom-call | tf_op jit(solution)/shard_map/pallas_call | solution.py:409
  25.8 0.1 collective-permute-start.9
  25.8 0.8 %shard_map.81._ = bf16[4096,128]{1,0:T(8,128)(2,1)} custom-call(bf16[2048,128]{1,0:T(8,128)(2,1)S(1)} %shard_map.80.own_ref), custom_call_target="tpu_custom_call" | custom-call | tf_op jit(solution)/shard_map/pallas_call | solution.py:418
  26.7 1.1 %collective-permute-done.9.other_ref = bf16[2048,128]{1,0:T(8,128)(2,1)S(1)} collective-permute-done((bf16[2048,128]{1,0:T(8,128)(2,1)S(1)}, bf16[2048,128]{1,0:T(8,128)(2,1)S(1)}, u32[]{:S(2)}, u32[]{:S(2)}) %collective-permute-start.9) | collective-permute-done | bytes 524320 | tf_op jit(solution)/shard_map/ppermute | solution.py:415
  27.7 0.8 %shard_map.82 = bf16[4096,128]{1,0:T(8,128)(2,1)} custom-call(bf16[2048,128]{1,0:T(8,128)(2,1)S(1)} %collective-permute-done.9.other_ref, bf16[4096,128]{1,0:T(8,128)(2,1)} %shard_map.81._), custom_call_target="tpu_custom_call", output_to_operand_aliasing={{}: (1, {})} | custom-call | tf_op jit(solution)/shard_map/pallas_call | solution.py:419
  (14 shorter events, 0.1 us)
Async XLA Ops:
  0.0 22.1 %collective-permute-start.3 = (bf16[1,512,1024]{2,1,0:T(8,128)(2,1)}, bf16[1,512,1024]{2,1,0:T(8,128)(2,1)S(1)}, u32[]{:S(2)}, u32[]{:S(2)}) collective-permute-start(bf16[1,512,1024]{2,1,0:T(8,128)(2,1)} %up_a.3), channel_id=1, source_target_pairs={{0,1},{1,0},{2,3},{3,2},{4,5},{5,4},{6,7},{7,6},{8,9},{9,8},{10,11... | collective-permute-start | bytes 3145736 | tf_op jit(solution)/shard_map/ppermute | solution.py:367
  0.5 21.6 %collective-permute-start.4 = (bf16[1,1024,512]{2,1,0:T(8,128)(2,1)}, bf16[1,1024,512]{2,1,0:T(8,128)(2,1)S(1)}, u32[]{:S(2)}, u32[]{:S(2)}) collective-permute-start(bf16[1,1024,512]{2,1,0:T(8,128)(2,1)} %down_a.3), channel_id=1, source_target_pairs={{0,1},{1,0},{2,3},{3,2},{4,5},{5,4},{6,7},{7,6},{8,9},{9,8},{10,11... | collective-permute-start | bytes 3145736 | tf_op jit(solution)/shard_map/ppermute | solution.py:368
  2.2 4.7 %collective-permute-start.5 = (bf16[256,256]{1,0:T(8,128)(2,1)S(1)}, bf16[256,256]{1,0:T(8,128)(2,1)S(1)}, u32[]{:S(2)}, u32[]{:S(2)}) collective-permute-start(bf16[256,256]{1,0:T(8,128)(2,1)S(1)} %get-tuple-element.19), channel_id=1, source_target_pairs={{4,8},{5,9},{0,1},{12,13},{8,4},{9,5},{1,0},{13,12},{6,10},{7,11},... | collective-permute-start | bytes 393224 | tf_op jit(solution)/shard_map/ppermute | solution.py:366
  2.8 7.5 %collective-permute-start = (bf16[256,256]{1,0:T(8,128)(2,1)S(1)}, bf16[256,256]{1,0:T(8,128)(2,1)S(1)}, u32[]{:S(2)}, u32[]{:S(2)}) collective-permute-start(bf16[256,256]{1,0:T(8,128)(2,1)S(1)} %get-tuple-element.13.a_ref), channel_id=1, source_target_pairs={{0,4},{4,0},{8,12},{12,8},{1,5},{5,1},{9,13},{13,9},{2,6},{6,2},{1... | collective-permute-start | bytes 393224 | tf_op jit(solution)/shard_map/ppermute | solution.py:365
  6.9 6.4 %collective-permute-start.6 = (bf16[256,256]{1,0:T(8,128)(2,1)S(1)}, bf16[256,256]{1,0:T(8,128)(2,1)S(1)}, u32[]{:S(2)}, u32[]{:S(2)}) collective-permute-start(bf16[256,256]{1,0:T(8,128)(2,1)S(1)} %collective-permute-done.5.a_ref), channel_id=1, source_target_pairs={{0,2},{2,0},{1,3},{3,1},{4,6},{6,4},{5,7},{7,5},{8,10},{10,8},{9,1... | collective-permute-start | bytes 393224 | tf_op jit(solution)/shard_map/ppermute | solution.py:377
  10.3 6.8 %collective-permute-start.1 = (bf16[256,256]{1,0:T(8,128)(2,1)S(1)}, bf16[256,256]{1,0:T(8,128)(2,1)S(1)}, u32[]{:S(2)}, u32[]{:S(2)}) collective-permute-start(bf16[256,256]{1,0:T(8,128)(2,1)S(1)} %shard_map.74.a_ref), channel_id=1, source_target_pairs={{0,12},{4,8},{8,4},{12,0},{1,13},{5,9},{9,5},{13,1},{2,14},{6,10},... | collective-permute-start | bytes 393224 | tf_op jit(solution)/shard_map/ppermute | solution.py:373
  13.4 8.7 %collective-permute-start.7 = (bf16[256,256]{1,0:T(8,128)(2,1)S(1)}, bf16[256,256]{1,0:T(8,128)(2,1)S(1)}, u32[]{:S(2)}, u32[]{:S(2)}) collective-permute-start(bf16[256,256]{1,0:T(8,128)(2,1)S(1)} %collective-permute-done.5.a_ref), channel_id=1, source_target_pairs={{0,1},{1,0},{2,3},{3,2},{4,5},{5,4},{6,7},{7,6},{8,9},{9,8},{10,11... | collective-permute-start | bytes 393224 | tf_op jit(solution)/shard_map/ppermute | solution.py:379
  13.4 8.7 %collective-permute-start.8 = (bf16[256,256]{1,0:T(8,128)(2,1)S(1)}, bf16[256,256]{1,0:T(8,128)(2,1)S(1)}, u32[]{:S(2)}, u32[]{:S(2)}) collective-permute-start(bf16[256,256]{1,0:T(8,128)(2,1)S(1)} %collective-permute-done.6.b_ref), channel_id=1, source_target_pairs={{0,1},{1,0},{2,3},{3,2},{4,5},{5,4},{6,7},{7,6},{8,9},{9,8},{10,11... | collective-permute-start | bytes 393224 | tf_op jit(solution)/shard_map/ppermute | solution.py:380
  17.2 4.1 %copy-start.3 = (f32[1,3,512]{2,0,1:T(1,128)S(1)}, f32[1,3,512]{2,0,1:T(1,128)}, u32[]{:S(2)}) copy-start(f32[1,3,512]{2,0,1:T(1,128)} %param.11) | copy-start | bytes 18436
  18.0 5.9 %collective-permute-start.2 = (bf16[256,256]{1,0:T(8,128)(2,1)S(1)}, bf16[256,256]{1,0:T(8,128)(2,1)S(1)}, u32[]{:S(2)}, u32[]{:S(2)}) collective-permute-start(bf16[256,256]{1,0:T(8,128)(2,1)S(1)} %get-tuple-element.15.near_ref), channel_id=1, source_target_pairs={{0,4},{4,0},{8,12},{12,8},{1,5},{5,1},{9,13},{13,9},{2,6},{6,2},{1... | collective-permute-start | bytes 393224 | tf_op jit(solution)/shard_map/ppermute | solution.py:396
  20.4 1.0 %copy-start = (bf16[512,512]{1,0:T(8,128)(2,1)S(1)}, bf16[512,512]{1,0:T(8,128)(2,1)}, u32[]{:S(2)}) copy-start(bf16[512,512]{1,0:T(8,128)(2,1)} %in_ref.5) | copy-start | bytes 1572868
  20.4 1.8 %copy-start.2 = (bf16[1,1024,512]{2,1,0:T(8,128)(2,1)S(1)}, bf16[1,1024,512]{2,1,0:T(8,128)(2,1)}, u32[]{:S(2)}) copy-start(bf16[1,1024,512]{2,1,0:T(8,128)(2,1)} %down_a.3) | copy-start | bytes 3145732
  21.2 1.3 %copy-start.1 = (bf16[1,512,1024]{2,1,0:T(8,128)(2,1)S(1)}, bf16[1,512,1024]{2,1,0:T(8,128)(2,1)}, u32[]{:S(2)}) copy-start(bf16[1,512,1024]{2,1,0:T(8,128)(2,1)} %up_a.3) | copy-start | bytes 3145732
  25.8 2.0 %collective-permute-start.9 = (bf16[2048,128]{1,0:T(8,128)(2,1)S(1)}, bf16[2048,128]{1,0:T(8,128)(2,1)S(1)}, u32[]{:S(2)}, u32[]{:S(2)}) collective-permute-start(bf16[2048,128]{1,0:T(8,128)(2,1)S(1)} %shard_map.80.own_ref), channel_id=1, source_target_pairs={{0,1},{1,0},{2,3},{3,2},{4,5},{5,4},{6,7},{7,6},{8,9},{9,8},{10,11... | collective-permute-start | bytes 1572872 | tf_op jit(solution)/shard_map/ppermute | solution.py:415
